TPU v7x, 32 devices: a whole 2x2x4 slice. The times are simulated.
32 devices in a mesh: gx: 4 (over y, x), gy: 4 (over z), gz: 2 (over core).
Axes of the slice: x: 2, y: 2, z: 4, core: 2. Of those that a mesh axis runs over, the one named last changes fastest.
Arguments:
- density_scatter: float32 [16, 32, 256], P('gx', 'gy', 'gz'), may hold values from 0.8 to 1.25
- initial_velocity: float32 [3, 16, 32, 256], P(None, 'gx', 'gy', 'gz'), may hold values from -0.12 to 0.12
- bubble_mask: int32 [16, 32, 256], P('gx', 'gy', 'gz'), may hold values from 0 to 1, as said below
- wall_flags: int32 [16, 32, 256], P('gx', 'gy', 'gz'), may hold values 0 or 1
Outputs:
- density_field: float32 [16, 32, 256], P('gx', 'gy', 'gz')
- velocity_field: float32 [3, 16, 32, 256], P(None, 'gx', 'gy', 'gz')
Inputs may be any that keep to these rules, and one draw needn't show every extreme that they name: `bubble_mask`: 1 at nodes inside a vapour bubble, 0 in the liquid. `wall_flags`: 1 at solid nodes, 0 at fluid nodes.
All inputs are finite; a program needn't handle non-finite values. No bound on the sum of `wall_flags` on one device may be relied on, other than what follows from the above.
Results may differ from a plain program's by a relative error of at most 0.0003.
Values sent between devices are 32-bit elements; how exact they have to be, the bound alone decides.
No kernel may reach another device: no remote copies, remote signals or barrier semaphores. Data moves between devices by JAX's collectives and lax.ppermute only.
A program may use at most 64 MiB of HBM per device.

v0:
```python
import math

import jax
import jax.numpy as jnp
import numpy as np
from jax import lax
from jax.sharding import PartitionSpec as P

STEPS = 4


lattice_velocities = np.array(
    [
        [0, 0, 0],
        [1, 0, 0],
        [-1, 0, 0],
        [0, 1, 0],
        [0, -1, 0],
        [0, 0, 1],
        [0, 0, -1],
        [1, 1, 0],
        [-1, -1, 0],
        [1, -1, 0],
        [-1, 1, 0],
        [1, 0, 1],
        [-1, 0, -1],
        [1, 0, -1],
        [-1, 0, 1],
        [0, 1, 1],
        [0, -1, -1],
        [0, 1, -1],
        [0, -1, 1],
    ]
)
weights = [1.0 / 3.0] + [1.0 / 18.0] * 6 + [1.0 / 36.0] * 12
opposite = [0, 2, 1, 4, 3, 6, 5, 8, 7, 10, 9, 12, 11, 14, 13, 16, 15, 18, 17]
liquid = 0.28
vapour = 0.06
wall_potential = 0.5
attractive_coupling = 1.0
critical_thermal_ratio = 0.06
viscous_rate = 1.25


def extended(shard, sides, width):
    for axis, dim in sides:
        peers, length = (lax.axis_size(axis), shard.shape[dim])
        up = [(i, (i + 1) % peers) for i in range(peers)]
        down = [(j, i) for i, j in up]
        last = lax.slice_in_dim(shard, length - width, length, axis=dim)
        first = lax.slice_in_dim(shard, 0, width, axis=dim)
        before = lax.ppermute(last, axis, up)
        after = lax.ppermute(first, axis, down)
        shard = jnp.concatenate([before, shard, after], axis=dim)
    return shard


def relaxation_matrix():
    table = lattice_velocities * 1.0
    first, second, third = (table[:, 0], table[:, 1], table[:, 2])
    squared_speed = first * first + second * second + third * third
    rows = [
        np.ones(19),
        19.0 * squared_speed - 30.0,
        (21.0 * squared_speed * squared_speed - 53.0 * squared_speed + 24.0) / 2.0,
        first,
        (5.0 * squared_speed - 9.0) * first,
        second,
        (5.0 * squared_speed - 9.0) * second,
        third,
        (5.0 * squared_speed - 9.0) * third,
        3.0 * first * first - squared_speed,
        (3.0 * squared_speed - 5.0) * (3.0 * first * first - squared_speed),
        second * second - third * third,
        (3.0 * squared_speed - 5.0) * (second * second - third * third),
        first * second,
        second * third,
        first * third,
        first * (second * second - third * third),
        second * (third * third - first * first),
        third * (first * first - second * second),
    ]
    moment_space_vector = np.stack(rows)
    inverse_transform = moment_space_vector.T / np.sum(
        moment_space_vector * moment_space_vector, axis=1
    )
    rates = np.array(
        [
            0.0,
            1.19,
            1.4,
            0.0,
            1.2,
            0.0,
            1.2,
            0.0,
            1.2,
            viscous_rate,
            1.4,
            viscous_rate,
            1.4,
            viscous_rate,
            viscous_rate,
            viscous_rate,
            1.98,
            1.98,
            1.98,
        ]
    )
    return inverse_transform * rates[None, :] @ moment_space_vector


def equilibrium(mass_per_volume, velocity):
    squared_speed = (
        velocity[0] * velocity[0] + velocity[1] * velocity[1] + velocity[2] * velocity[2]
    )
    rows = []
    for i in range(19):
        projection = (
            float(lattice_velocities[i, 0]) * velocity[0]
            + float(lattice_velocities[i, 1]) * velocity[1]
            + float(lattice_velocities[i, 2]) * velocity[2]
        )
        rows.append(
            weights[i]
            * mass_per_volume
            * (1.0 + 3.0 * projection + 4.5 * projection * projection - 1.5 * squared_speed)
        )
    return jnp.stack(rows)


def moments(populations):
    return jnp.stack(
        [
            sum(
                (
                    float(lattice_velocities[i, k]) * populations[i]
                    for i in range(19)
                    if lattice_velocities[i, k] != 0
                )
            )
            for k in range(3)
        ]
    )


def pseudo_potential(mass_per_volume):
    thermodynamic_stress = (
        mass_per_volume
        * critical_thermal_ratio
        * (
            1.0
            + mass_per_volume
            + mass_per_volume * mass_per_volume
            - mass_per_volume * mass_per_volume * mass_per_volume
        )
        / ((1.0 - mass_per_volume) * (1.0 - mass_per_volume) * (1.0 - mass_per_volume))
        - attractive_coupling * mass_per_volume * mass_per_volume
    )
    return jnp.sqrt(6.0 * (mass_per_volume / 3.0 - thermodynamic_stress))


def attraction(potential, nearby):
    parts = []
    for k in range(3):
        total = sum(
            (
                weights[i] * float(lattice_velocities[i, k]) * nearby[i - 1]
                for i in range(1, 19)
                if lattice_velocities[i, k] != 0
            )
        )
        parts.append(potential * total)
    return jnp.stack(parts)


def collide(populations, mass_per_volume, momentum, force, solid, kernel):
    velocity = momentum / mass_per_volume
    settled = equilibrium(mass_per_volume, velocity)
    pushed = equilibrium(mass_per_volume, velocity + force / mass_per_volume)
    relaxed = jnp.einsum(
        "ij,jxyz->ixyz", kernel, populations - settled, precision=lax.Precision.HIGHEST
    )
    relaxed_distribution = populations - relaxed + pushed - settled
    bounced = populations[np.array(opposite)]
    return jnp.where(solid[None], bounced, relaxed_distribution)


def window(padded, offsets, shape):
    starts = [1 + int(offsets[k]) for k in range(3)]
    return lax.slice(padded, starts, [starts[k] + shape[k] for k in range(3)])


def stream_along(rows, dim, send):
    length = rows[0].shape[dim]
    upward = [i for i in range(19) if lattice_velocities[i, dim] == 1]
    downward = [i for i in range(19) if lattice_velocities[i, dim] == -1]
    upper = jnp.stack([lax.slice_in_dim(rows[i], length - 1, length, axis=dim) for i in upward])
    lower = jnp.stack([lax.slice_in_dim(rows[i], 0, 1, axis=dim) for i in downward])
    rims = jnp.concatenate([lower, upper], axis=dim + 1)
    incoming_populations = send(rims)
    from_below = lax.slice_in_dim(incoming_populations, 0, 1, axis=dim + 1)
    upper_neighbour_share = lax.slice_in_dim(incoming_populations, 3, 4, axis=dim + 1)
    result = list(rows)
    for k, i in enumerate(upward):
        result[i] = jnp.concatenate(
            [from_below[k], lax.slice_in_dim(rows[i], 0, length - 1, axis=dim)], axis=dim
        )
    for k, i in enumerate(downward):
        result[i] = jnp.concatenate(
            [lax.slice_in_dim(rows[i], 1, length, axis=dim), upper_neighbour_share[k]], axis=dim
        )
    return result


def on_device(density_scatter, initial_velocity, bubble_mask, wall_flags):
    kernel = jnp.asarray(relaxation_matrix(), jnp.float32)
    solid = wall_flags == 1
    shape = wall_flags.shape
    mass_per_volume = jnp.where(bubble_mask == 1, vapour, liquid) * density_scatter
    populations = equilibrium(mass_per_volume, initial_velocity)
    for step in range(STEPS):
        mass_per_volume = jnp.sum(populations, axis=0)
        momentum = moments(populations)
        potential = jnp.where(solid, wall_potential, pseudo_potential(mass_per_volume))
        padded = extended(potential, (("gx", 0), ("gy", 1), ("gz", 2)), 1)
        nearby = [window(padded, lattice_velocities[i], shape) for i in range(1, 19)]
        force = attraction(potential, nearby)
        post = collide(populations, mass_per_volume, momentum, force, solid, kernel)
        rows = [post[i] for i in range(19)]
        rows = stream_along(rows, 0, lambda r: extended(r, (("gx", 1),), 1))
        rows = stream_along(rows, 1, lambda r: extended(r, (("gy", 2),), 1))
        rows = stream_along(rows, 2, lambda r: extended(r, (("gz", 3),), 1))
        populations = jnp.stack(rows)
    mass_per_volume = jnp.sum(populations, axis=0)
    momentum = moments(populations)
    density_field = jnp.where(solid, 0.0, mass_per_volume / liquid)
    velocity_field = jnp.where(solid[None], 0.0, math.sqrt(3.0) * momentum / mass_per_volume)
    return (density_field, velocity_field)


def solution(mesh):
    in_specs = (
        P("gx", "gy", "gz"),
        P(None, "gx", "gy", "gz"),
        P("gx", "gy", "gz"),
        P("gx", "gy", "gz"),
    )
    out_specs = (P("gx", "gy", "gz"), P(None, "gx", "gy", "gz"))
    return jax.shard_map(
        on_device, mesh=mesh, in_specs=in_specs, out_specs=out_specs, check_vma=False
    )
```

profile of v0, /device:TPU:0, one launch (start us, length us, event | category | flops | bytes accessed | tf_op | source)
XLA Modules:
  0.0 137.7 jit_solution(16092745943061811150)
XLA Ops:
  1.6 3.0 %collective-permute-start.1 = (f32[1,8,128]{2,1,0:T(8,128)S(1)}, f32[1,8,128]{2,1,0:T(8,128)S(1)}, u32[]{:S(2)}, u32[]{:S(2)}) collective-permute-start(f32[1,8,128]{2,1,0:T(8,128)S(1)} %get-tuple-element.476), channel_id=1, source_target_pairs={{0,8},{8,16},{16,24},{24,0},{1,9},{9,17},{17,25},{25,1},{2,10},{10... | collective-permute-start | bytes 12296 | tf_op jit(solution)/shard_map/ppermute | solution.py:52
  8.2 1.6 %collective-permute-start.3 = (f32[6,1,128]{2,1,0:T(1,128)S(1)}, f32[6,1,128]{2,1,0:T(1,128)S(1)}, u32[]{:S(2)}, u32[]{:S(2)}) collective-permute-start(f32[6,1,128]{2,1,0:T(1,128)S(1)} %get-tuple-element.288), channel_id=1, source_target_pairs={{0,2},{2,4},{4,6},{6,0},{1,3},{3,5},{5,7},{7,1},{8,10},{10,12},{12... | collective-permute-start | bytes 9224 | tf_op jit(solution)/shard_map/ppermute | solution.py:52
  9.9 2.2 %collective-permute-start.2 = (f32[6,1,128]{2,1,0:T(1,128)S(1)}, f32[6,1,128]{2,1,0:T(1,128)S(1)}, u32[]{:S(2)}, u32[]{:S(2)}) collective-permute-start(f32[6,1,128]{2,1,0:T(1,128)S(1)} %get-tuple-element.289), channel_id=1, source_target_pairs={{2,0},{4,2},{6,4},{0,6},{3,1},{5,3},{7,5},{1,7},{10,8},{12,10},{14... | collective-permute-start | bytes 9224 | tf_op jit(solution)/shard_map/ppermute | solution.py:53
  18.2 2.2 %collective-permute-start.7 = (f32[5,1,8,128]{3,2,1,0:T(8,128)S(1)}, f32[5,1,8,128]{3,2,1,0:T(8,128)S(1)}, u32[]{:S(2)}, u32[]{:S(2)}) collective-permute-start(f32[5,1,8,128]{3,2,1,0:T(8,128)S(1)} %get-tuple-element.177), channel_id=1, source_target_pairs={{8,0},{16,8},{24,16},{0,24},{9,1},{17,9},{25,17},{1,25},{10,2},{18... | collective-permute-start | bytes 61448 | tf_op jit(solution)/shard_map/ppermute | solution.py:53
  20.8 1.5 %collective-permute-done.7 = f32[5,1,8,128]{3,2,1,0:T(8,128)S(1)} collective-permute-done((f32[5,1,8,128]{3,2,1,0:T(8,128)S(1)}, f32[5,1,8,128]{3,2,1,0:T(8,128)S(1)}, u32[]{:S(2)}, u32[]{:S(2)}) %collective-permute-start.7) | collective-permute-done | bytes 20512 | tf_op jit(solution)/shard_map/ppermute | solution.py:53
  22.4 2.6 %collective-permute-done.6 = f32[5,1,8,128]{3,2,1,0:T(8,128)S(1)} collective-permute-done((f32[5,1,8,128]{3,2,1,0:T(8,128)S(1)}, f32[5,1,8,128]{3,2,1,0:T(8,128)S(1)}, u32[]{:S(2)}, u32[]{:S(2)}) %collective-permute-start.6) | collective-permute-done | bytes 20512 | tf_op jit(solution)/shard_map/ppermute | solution.py:52
  25.8 1.6 %collective-permute-start.8 = (f32[5,4,1,128]{3,1,2,0:T(4,128)S(1)}, f32[5,4,1,128]{3,1,2,0:T(4,128)S(1)}, u32[]{:S(2)}, u32[]{:S(2)}) collective-permute-start(f32[5,4,1,128]{3,1,2,0:T(4,128)S(1)} %constant_dynamic-update-slice_fusion.67), channel_id=1, source_target_pairs={{0,2},{2,4},{4,6},{6,0},{1,3},{3,5},{5,7},{7,1},{8,10},{10,12},{12... | collective-permute-start | bytes 30728 | tf_op jit(solution)/shard_map/ppermute | solution.py:52
  27.5 2.4 %collective-permute-start.9 = (f32[5,4,1,128]{3,1,2,0:T(4,128)S(1)}, f32[5,4,1,128]{3,1,2,0:T(4,128)S(1)}, u32[]{:S(2)}, u32[]{:S(2)}) collective-permute-start(f32[5,4,1,128]{3,1,2,0:T(4,128)S(1)} %constant_dynamic-update-slice_fusion.72), channel_id=1, source_target_pairs={{2,0},{4,2},{6,4},{0,6},{3,1},{5,3},{7,5},{1,7},{10,8},{12,10},{14... | collective-permute-start | bytes 30728 | tf_op jit(solution)/shard_map/ppermute | solution.py:53
  35.6 2.6 %collective-permute-start.12 = (f32[1,8,128]{2,1,0:T(8,128)S(1)}, f32[1,8,128]{2,1,0:T(8,128)S(1)}, u32[]{:S(2)}, u32[]{:S(2)}) collective-permute-start(f32[1,8,128]{2,1,0:T(8,128)S(1)} %get-tuple-element.418), channel_id=1, source_target_pairs={{8,0},{16,8},{24,16},{0,24},{9,1},{17,9},{25,17},{1,25},{10,2},{18... | collective-permute-start | bytes 12296 | tf_op jit(solution)/shard_map/ppermute | solution.py:53
  41.1 2.8 %collective-permute-start.14 = (f32[6,1,128]{2,1,0:T(1,128)S(1)}, f32[6,1,128]{2,1,0:T(1,128)S(1)}, u32[]{:S(2)}, u32[]{:S(2)}) collective-permute-start(f32[6,1,128]{2,1,0:T(1,128)S(1)} %get-tuple-element.285), channel_id=1, source_target_pairs={{2,0},{4,2},{6,4},{0,6},{3,1},{5,3},{7,5},{1,7},{10,8},{12,10},{14... | collective-permute-start | bytes 9224 | tf_op jit(solution)/shard_map/ppermute | solution.py:53
  49.3 2.7 %collective-permute-start.19 = (f32[5,1,8,128]{3,2,1,0:T(8,128)S(1)}, f32[5,1,8,128]{3,2,1,0:T(8,128)S(1)}, u32[]{:S(2)}, u32[]{:S(2)}) collective-permute-start(f32[5,1,8,128]{3,2,1,0:T(8,128)S(1)} %get-tuple-element.146), channel_id=1, source_target_pairs={{8,0},{16,8},{24,16},{0,24},{9,1},{17,9},{25,17},{1,25},{10,2},{18... | collective-permute-start | bytes 61448 | tf_op jit(solution)/shard_map/ppermute | solution.py:53
  54.2 2.6 %collective-permute-done.18 = f32[5,1,8,128]{3,2,1,0:T(8,128)S(1)} collective-permute-done((f32[5,1,8,128]{3,2,1,0:T(8,128)S(1)}, f32[5,1,8,128]{3,2,1,0:T(8,128)S(1)}, u32[]{:S(2)}, u32[]{:S(2)}) %collective-permute-start.18) | collective-permute-done | bytes 20512 | tf_op jit(solution)/shard_map/ppermute | solution.py:52
  59.1 2.7 %collective-permute-start.21 = (f32[5,4,1,128]{3,1,2,0:T(4,128)S(1)}, f32[5,4,1,128]{3,1,2,0:T(4,128)S(1)}, u32[]{:S(2)}, u32[]{:S(2)}) collective-permute-start(f32[5,4,1,128]{3,1,2,0:T(4,128)S(1)} %constant_dynamic-update-slice_fusion.159), channel_id=1, source_target_pairs={{2,0},{4,2},{6,4},{0,6},{3,1},{5,3},{7,5},{1,7},{10,8},{12,10},{14... | collective-permute-start | bytes 30728 | tf_op jit(solution)/shard_map/ppermute | solution.py:53
  68.9 2.5 %collective-permute-start.24 = (f32[1,8,128]{2,1,0:T(8,128)S(1)}, f32[1,8,128]{2,1,0:T(8,128)S(1)}, u32[]{:S(2)}, u32[]{:S(2)}) collective-permute-start(f32[1,8,128]{2,1,0:T(8,128)S(1)} %get-tuple-element.393), channel_id=1, source_target_pairs={{8,0},{16,8},{24,16},{0,24},{9,1},{17,9},{25,17},{1,25},{10,2},{18... | collective-permute-start | bytes 12296 | tf_op jit(solution)/shard_map/ppermute | solution.py:53
  74.4 2.8 %collective-permute-start.26 = (f32[6,1,128]{2,1,0:T(1,128)S(1)}, f32[6,1,128]{2,1,0:T(1,128)S(1)}, u32[]{:S(2)}, u32[]{:S(2)}) collective-permute-start(f32[6,1,128]{2,1,0:T(1,128)S(1)} %get-tuple-element.281), channel_id=1, source_target_pairs={{2,0},{4,2},{6,4},{0,6},{3,1},{5,3},{7,5},{1,7},{10,8},{12,10},{14... | collective-permute-start | bytes 9224 | tf_op jit(solution)/shard_map/ppermute | solution.py:53
  82.7 2.7 %collective-permute-start.31 = (f32[5,1,8,128]{3,2,1,0:T(8,128)S(1)}, f32[5,1,8,128]{3,2,1,0:T(8,128)S(1)}, u32[]{:S(2)}, u32[]{:S(2)}) collective-permute-start(f32[5,1,8,128]{3,2,1,0:T(8,128)S(1)} %get-tuple-element.116), channel_id=1, source_target_pairs={{8,0},{16,8},{24,16},{0,24},{9,1},{17,9},{25,17},{1,25},{10,2},{18... | collective-permute-start | bytes 61448 | tf_op jit(solution)/shard_map/ppermute | solution.py:53
  85.9 4.2 %collective-permute-done.30 = f32[5,1,8,128]{3,2,1,0:T(8,128)S(1)} collective-permute-done((f32[5,1,8,128]{3,2,1,0:T(8,128)S(1)}, f32[5,1,8,128]{3,2,1,0:T(8,128)S(1)}, u32[]{:S(2)}, u32[]{:S(2)}) %collective-permute-start.30) | collective-permute-done | bytes 20512 | tf_op jit(solution)/shard_map/ppermute | solution.py:52
  91.0 4.1 %collective-permute-start.33 = (f32[5,4,1,128]{3,1,2,0:T(4,128)S(1)}, f32[5,4,1,128]{3,1,2,0:T(4,128)S(1)}, u32[]{:S(2)}, u32[]{:S(2)}) collective-permute-start(f32[5,4,1,128]{3,1,2,0:T(4,128)S(1)} %constant_dynamic-update-slice_fusion.246), channel_id=1, source_target_pairs={{2,0},{4,2},{6,4},{0,6},{3,1},{5,3},{7,5},{1,7},{10,8},{12,10},{14... | collective-permute-start | bytes 30728 | tf_op jit(solution)/shard_map/ppermute | solution.py:53
  96.8 3.8 %collective-permute-done.32 = f32[5,4,1,128]{3,1,2,0:T(4,128)S(1)} collective-permute-done((f32[5,4,1,128]{3,1,2,0:T(4,128)S(1)}, f32[5,4,1,128]{3,1,2,0:T(4,128)S(1)}, u32[]{:S(2)}, u32[]{:S(2)}) %collective-permute-start.32) | collective-permute-done | bytes 10272 | tf_op jit(solution)/shard_map/ppermute | solution.py:52
  104.3 2.8 %collective-permute-start.36 = (f32[1,8,128]{2,1,0:T(8,128)S(1)}, f32[1,8,128]{2,1,0:T(8,128)S(1)}, u32[]{:S(2)}, u32[]{:S(2)}) collective-permute-start(f32[1,8,128]{2,1,0:T(8,128)S(1)} %get-tuple-element.358), channel_id=1, source_target_pairs={{8,0},{16,8},{24,16},{0,24},{9,1},{17,9},{25,17},{1,25},{10,2},{18... | collective-permute-start | bytes 12296 | tf_op jit(solution)/shard_map/ppermute | solution.py:53
  108.9 3.8 %collective-permute-start.38 = (f32[6,1,128]{2,1,0:T(1,128)S(1)}, f32[6,1,128]{2,1,0:T(1,128)S(1)}, u32[]{:S(2)}, u32[]{:S(2)}) collective-permute-start(f32[6,1,128]{2,1,0:T(1,128)S(1)} %get-tuple-element.277), channel_id=1, source_target_pairs={{2,0},{4,2},{6,4},{0,6},{3,1},{5,3},{7,5},{1,7},{10,8},{12,10},{14... | collective-permute-start | bytes 9224 | tf_op jit(solution)/shard_map/ppermute | solution.py:53
  118.1 2.9 %collective-permute-start.42 = (f32[5,1,8,128]{3,2,1,0:T(8,128)S(1)}, f32[5,1,8,128]{3,2,1,0:T(8,128)S(1)}, u32[]{:S(2)}, u32[]{:S(2)}) collective-permute-start(f32[5,1,8,128]{3,2,1,0:T(8,128)S(1)} %get-tuple-element.85), channel_id=1, source_target_pairs={{0,8},{8,16},{16,24},{24,0},{1,9},{9,17},{17,25},{25,1},{2,10},{10... | collective-permute-start | bytes 61448 | tf_op jit(solution)/shard_map/ppermute | solution.py:52
  121.6 3.2 %collective-permute-done.43 = f32[5,1,8,128]{3,2,1,0:T(8,128)S(1)} collective-permute-done((f32[5,1,8,128]{3,2,1,0:T(8,128)S(1)}, f32[5,1,8,128]{3,2,1,0:T(8,128)S(1)}, u32[]{:S(2)}, u32[]{:S(2)}) %collective-permute-start.43) | collective-permute-done | bytes 20512 | tf_op jit(solution)/shard_map/ppermute | solution.py:53
  126.1 3.9 %collective-permute-start.45 = (f32[5,4,1,128]{3,1,2,0:T(4,128)S(1)}, f32[5,4,1,128]{3,1,2,0:T(4,128)S(1)}, u32[]{:S(2)}, u32[]{:S(2)}) collective-permute-start(f32[5,4,1,128]{3,1,2,0:T(4,128)S(1)} %constant_dynamic-update-slice_fusion.333), channel_id=1, source_target_pairs={{2,0},{4,2},{6,4},{0,6},{3,1},{5,3},{7,5},{1,7},{10,8},{12,10},{14... | collective-permute-start | bytes 30728 | tf_op jit(solution)/shard_map/ppermute | solution.py:53
  (794 shorter events, 66.0 us)
Async XLA Ops:
  1.6 5.6 %collective-permute-start.1 = (f32[1,8,128]{2,1,0:T(8,128)S(1)}, f32[1,8,128]{2,1,0:T(8,128)S(1)}, u32[]{:S(2)}, u32[]{:S(2)}) collective-permute-start(f32[1,8,128]{2,1,0:T(8,128)S(1)} %get-tuple-element.476), channel_id=1, source_target_pairs={{0,8},{8,16},{16,24},{24,0},{1,9},{9,17},{17,25},{25,1},{2,10},{10... | collective-permute-start | bytes 12296 | tf_op jit(solution)/shard_map/ppermute | solution.py:52
  8.2 5.4 %collective-permute-start.3 = (f32[6,1,128]{2,1,0:T(1,128)S(1)}, f32[6,1,128]{2,1,0:T(1,128)S(1)}, u32[]{:S(2)}, u32[]{:S(2)}) collective-permute-start(f32[6,1,128]{2,1,0:T(1,128)S(1)} %get-tuple-element.288), channel_id=1, source_target_pairs={{0,2},{2,4},{4,6},{6,0},{1,3},{3,5},{5,7},{7,1},{8,10},{10,12},{12... | collective-permute-start | bytes 9224 | tf_op jit(solution)/shard_map/ppermute | solution.py:52
  20.4 4.7 %collective-permute-start.6 = (f32[5,1,8,128]{3,2,1,0:T(8,128)S(1)}, f32[5,1,8,128]{3,2,1,0:T(8,128)S(1)}, u32[]{:S(2)}, u32[]{:S(2)}) collective-permute-start(f32[5,1,8,128]{3,2,1,0:T(8,128)S(1)} %get-tuple-element.178), channel_id=1, source_target_pairs={{0,8},{8,16},{16,24},{24,0},{1,9},{9,17},{17,25},{25,1},{2,10},{10... | collective-permute-start | bytes 61448 | tf_op jit(solution)/shard_map/ppermute | solution.py:52
  25.8 5.6 %collective-permute-start.8 = (f32[5,4,1,128]{3,1,2,0:T(4,128)S(1)}, f32[5,4,1,128]{3,1,2,0:T(4,128)S(1)}, u32[]{:S(2)}, u32[]{:S(2)}) collective-permute-start(f32[5,4,1,128]{3,1,2,0:T(4,128)S(1)} %constant_dynamic-update-slice_fusion.67), channel_id=1, source_target_pairs={{0,2},{2,4},{4,6},{6,0},{1,3},{3,5},{5,7},{7,1},{8,10},{10,12},{12... | collective-permute-start | bytes 30728 | tf_op jit(solution)/shard_map/ppermute | solution.py:52
  35.3 4.5 %collective-permute-start.13 = (f32[1,8,128]{2,1,0:T(8,128)S(1)}, f32[1,8,128]{2,1,0:T(8,128)S(1)}, u32[]{:S(2)}, u32[]{:S(2)}) collective-permute-start(f32[1,8,128]{2,1,0:T(8,128)S(1)} %get-tuple-element.417), channel_id=1, source_target_pairs={{0,8},{8,16},{16,24},{24,0},{1,9},{9,17},{17,25},{25,1},{2,10},{10... | collective-permute-start | bytes 12296 | tf_op jit(solution)/shard_map/ppermute | solution.py:52
  35.6 4.5 %collective-permute-start.12 = (f32[1,8,128]{2,1,0:T(8,128)S(1)}, f32[1,8,128]{2,1,0:T(8,128)S(1)}, u32[]{:S(2)}, u32[]{:S(2)}) collective-permute-start(f32[1,8,128]{2,1,0:T(8,128)S(1)} %get-tuple-element.418), channel_id=1, source_target_pairs={{8,0},{16,8},{24,16},{0,24},{9,1},{17,9},{25,17},{1,25},{10,2},{18... | collective-permute-start | bytes 12296 | tf_op jit(solution)/shard_map/ppermute | solution.py:53
  40.1 5.4 %collective-permute-start.15 = (f32[6,1,128]{2,1,0:T(1,128)S(1)}, f32[6,1,128]{2,1,0:T(1,128)S(1)}, u32[]{:S(2)}, u32[]{:S(2)}) collective-permute-start(f32[6,1,128]{2,1,0:T(1,128)S(1)} %get-tuple-element.284), channel_id=1, source_target_pairs={{0,2},{2,4},{4,6},{6,0},{1,3},{3,5},{5,7},{7,1},{8,10},{10,12},{12... | collective-permute-start | bytes 9224 | tf_op jit(solution)/shard_map/ppermute | solution.py:52
  41.1 4.4 %collective-permute-start.14 = (f32[6,1,128]{2,1,0:T(1,128)S(1)}, f32[6,1,128]{2,1,0:T(1,128)S(1)}, u32[]{:S(2)}, u32[]{:S(2)}) collective-permute-start(f32[6,1,128]{2,1,0:T(1,128)S(1)} %get-tuple-element.285), channel_id=1, source_target_pairs={{2,0},{4,2},{6,4},{0,6},{3,1},{5,3},{7,5},{1,7},{10,8},{12,10},{14... | collective-permute-start | bytes 9224 | tf_op jit(solution)/shard_map/ppermute | solution.py:53
  49.3 4.7 %collective-permute-start.19 = (f32[5,1,8,128]{3,2,1,0:T(8,128)S(1)}, f32[5,1,8,128]{3,2,1,0:T(8,128)S(1)}, u32[]{:S(2)}, u32[]{:S(2)}) collective-permute-start(f32[5,1,8,128]{3,2,1,0:T(8,128)S(1)} %get-tuple-element.146), channel_id=1, source_target_pairs={{8,0},{16,8},{24,16},{0,24},{9,1},{17,9},{25,17},{1,25},{10,2},{18... | collective-permute-start | bytes 61448 | tf_op jit(solution)/shard_map/ppermute | solution.py:53
  52.0 4.7 %collective-permute-start.18 = (f32[5,1,8,128]{3,2,1,0:T(8,128)S(1)}, f32[5,1,8,128]{3,2,1,0:T(8,128)S(1)}, u32[]{:S(2)}, u32[]{:S(2)}) collective-permute-start(f32[5,1,8,128]{3,2,1,0:T(8,128)S(1)} %get-tuple-element.147), channel_id=1, source_target_pairs={{0,8},{8,16},{16,24},{24,0},{1,9},{9,17},{17,25},{25,1},{2,10},{10... | collective-permute-start | bytes 61448 | tf_op jit(solution)/shard_map/ppermute | solution.py:52
  57.8 5.5 %collective-permute-start.20 = (f32[5,4,1,128]{3,1,2,0:T(4,128)S(1)}, f32[5,4,1,128]{3,1,2,0:T(4,128)S(1)}, u32[]{:S(2)}, u32[]{:S(2)}) collective-permute-start(f32[5,4,1,128]{3,1,2,0:T(4,128)S(1)} %constant_dynamic-update-slice_fusion.154), channel_id=1, source_target_pairs={{0,2},{2,4},{4,6},{6,0},{1,3},{3,5},{5,7},{7,1},{8,10},{10,12},{12... | collective-permute-start | bytes 30728 | tf_op jit(solution)/shard_map/ppermute | solution.py:52
  68.4 4.6 %collective-permute-start.25 = (f32[1,8,128]{2,1,0:T(8,128)S(1)}, f32[1,8,128]{2,1,0:T(8,128)S(1)}, u32[]{:S(2)}, u32[]{:S(2)}) collective-permute-start(f32[1,8,128]{2,1,0:T(8,128)S(1)} %get-tuple-element.392), channel_id=1, source_target_pairs={{0,8},{8,16},{16,24},{24,0},{1,9},{9,17},{17,25},{25,1},{2,10},{10... | collective-permute-start | bytes 12296 | tf_op jit(solution)/shard_map/ppermute | solution.py:52
  73.3 5.4 %collective-permute-start.27 = (f32[6,1,128]{2,1,0:T(1,128)S(1)}, f32[6,1,128]{2,1,0:T(1,128)S(1)}, u32[]{:S(2)}, u32[]{:S(2)}) collective-permute-start(f32[6,1,128]{2,1,0:T(1,128)S(1)} %get-tuple-element.280), channel_id=1, source_target_pairs={{0,2},{2,4},{4,6},{6,0},{1,3},{3,5},{5,7},{7,1},{8,10},{10,12},{12... | collective-permute-start | bytes 9224 | tf_op jit(solution)/shard_map/ppermute | solution.py:52
  82.7 7.4 %collective-permute-start.31 = (f32[5,1,8,128]{3,2,1,0:T(8,128)S(1)}, f32[5,1,8,128]{3,2,1,0:T(8,128)S(1)}, u32[]{:S(2)}, u32[]{:S(2)}) collective-permute-start(f32[5,1,8,128]{3,2,1,0:T(8,128)S(1)} %get-tuple-element.116), channel_id=1, source_target_pairs={{8,0},{16,8},{24,16},{0,24},{9,1},{17,9},{25,17},{1,25},{10,2},{18... | collective-permute-start | bytes 61448 | tf_op jit(solution)/shard_map/ppermute | solution.py:53
  85.4 4.7 %collective-permute-start.30 = (f32[5,1,8,128]{3,2,1,0:T(8,128)S(1)}, f32[5,1,8,128]{3,2,1,0:T(8,128)S(1)}, u32[]{:S(2)}, u32[]{:S(2)}) collective-permute-start(f32[5,1,8,128]{3,2,1,0:T(8,128)S(1)} %get-tuple-element.117), channel_id=1, source_target_pairs={{0,8},{8,16},{16,24},{24,0},{1,9},{9,17},{17,25},{25,1},{2,10},{10... | collective-permute-start | bytes 61448 | tf_op jit(solution)/shard_map/ppermute | solution.py:52
  91.0 5.4 %collective-permute-start.33 = (f32[5,4,1,128]{3,1,2,0:T(4,128)S(1)}, f32[5,4,1,128]{3,1,2,0:T(4,128)S(1)}, u32[]{:S(2)}, u32[]{:S(2)}) collective-permute-start(f32[5,4,1,128]{3,1,2,0:T(4,128)S(1)} %constant_dynamic-update-slice_fusion.246), channel_id=1, source_target_pairs={{2,0},{4,2},{6,4},{0,6},{3,1},{5,3},{7,5},{1,7},{10,8},{12,10},{14... | collective-permute-start | bytes 30728 | tf_op jit(solution)/shard_map/ppermute | solution.py:53
  95.1 5.5 %collective-permute-start.32 = (f32[5,4,1,128]{3,1,2,0:T(4,128)S(1)}, f32[5,4,1,128]{3,1,2,0:T(4,128)S(1)}, u32[]{:S(2)}, u32[]{:S(2)}) collective-permute-start(f32[5,4,1,128]{3,1,2,0:T(4,128)S(1)} %constant_dynamic-update-slice_fusion.241), channel_id=1, source_target_pairs={{0,2},{2,4},{4,6},{6,0},{1,3},{3,5},{5,7},{7,1},{8,10},{10,12},{12... | collective-permute-start | bytes 30728 | tf_op jit(solution)/shard_map/ppermute | solution.py:52
  104.1 4.5 %collective-permute-start.37 = (f32[1,8,128]{2,1,0:T(8,128)S(1)}, f32[1,8,128]{2,1,0:T(8,128)S(1)}, u32[]{:S(2)}, u32[]{:S(2)}) collective-permute-start(f32[1,8,128]{2,1,0:T(8,128)S(1)} %get-tuple-element.357), channel_id=1, source_target_pairs={{0,8},{8,16},{16,24},{24,0},{1,9},{9,17},{17,25},{25,1},{2,10},{10... | collective-permute-start | bytes 12296 | tf_op jit(solution)/shard_map/ppermute | solution.py:52
  104.3 4.6 %collective-permute-start.36 = (f32[1,8,128]{2,1,0:T(8,128)S(1)}, f32[1,8,128]{2,1,0:T(8,128)S(1)}, u32[]{:S(2)}, u32[]{:S(2)}) collective-permute-start(f32[1,8,128]{2,1,0:T(8,128)S(1)} %get-tuple-element.358), channel_id=1, source_target_pairs={{8,0},{16,8},{24,16},{0,24},{9,1},{17,9},{25,17},{1,25},{10,2},{18... | collective-permute-start | bytes 12296 | tf_op jit(solution)/shard_map/ppermute | solution.py:53
  108.9 5.4 %collective-permute-start.39 = (f32[6,1,128]{2,1,0:T(1,128)S(1)}, f32[6,1,128]{2,1,0:T(1,128)S(1)}, u32[]{:S(2)}, u32[]{:S(2)}) collective-permute-start(f32[6,1,128]{2,1,0:T(1,128)S(1)} %get-tuple-element.276), channel_id=1, source_target_pairs={{0,2},{2,4},{4,6},{6,0},{1,3},{3,5},{5,7},{7,1},{8,10},{10,12},{12... | collective-permute-start | bytes 9224 | tf_op jit(solution)/shard_map/ppermute | solution.py:52
  108.9 5.4 %collective-permute-start.38 = (f32[6,1,128]{2,1,0:T(1,128)S(1)}, f32[6,1,128]{2,1,0:T(1,128)S(1)}, u32[]{:S(2)}, u32[]{:S(2)}) collective-permute-start(f32[6,1,128]{2,1,0:T(1,128)S(1)} %get-tuple-element.277), channel_id=1, source_target_pairs={{2,0},{4,2},{6,4},{0,6},{3,1},{5,3},{7,5},{1,7},{10,8},{12,10},{14... | collective-permute-start | bytes 9224 | tf_op jit(solution)/shard_map/ppermute | solution.py:53
  118.1 6.8 %collective-permute-start.42 = (f32[5,1,8,128]{3,2,1,0:T(8,128)S(1)}, f32[5,1,8,128]{3,2,1,0:T(8,128)S(1)}, u32[]{:S(2)}, u32[]{:S(2)}) collective-permute-start(f32[5,1,8,128]{3,2,1,0:T(8,128)S(1)} %get-tuple-element.85), channel_id=1, source_target_pairs={{0,8},{8,16},{16,24},{24,0},{1,9},{9,17},{17,25},{25,1},{2,10},{10... | collective-permute-start | bytes 61448 | tf_op jit(solution)/shard_map/ppermute | solution.py:52
  126.0 5.5 %collective-permute-start.44 = (f32[5,4,1,128]{3,1,2,0:T(4,128)S(1)}, f32[5,4,1,128]{3,1,2,0:T(4,128)S(1)}, u32[]{:S(2)}, u32[]{:S(2)}) collective-permute-start(f32[5,4,1,128]{3,1,2,0:T(4,128)S(1)} %constant_dynamic-update-slice_fusion.328), channel_id=1, source_target_pairs={{0,2},{2,4},{4,6},{6,0},{1,3},{3,5},{5,7},{7,1},{8,10},{10,12},{12... | collective-permute-start | bytes 30728 | tf_op jit(solution)/shard_map/ppermute | solution.py:52
  126.1 5.8 %collective-permute-start.45 = (f32[5,4,1,128]{3,1,2,0:T(4,128)S(1)}, f32[5,4,1,128]{3,1,2,0:T(4,128)S(1)}, u32[]{:S(2)}, u32[]{:S(2)}) collective-permute-start(f32[5,4,1,128]{3,1,2,0:T(4,128)S(1)} %constant_dynamic-update-slice_fusion.333), channel_id=1, source_target_pairs={{2,0},{4,2},{6,4},{0,6},{3,1},{5,3},{7,5},{1,7},{10,8},{12,10},{14... | collective-permute-start | bytes 30728 | tf_op jit(solution)/shard_map/ppermute | solution.py:53
  (26 other events, 58.6 us)
where the time goes:
time: 138 us
  starting transfers between devices  60.1 us (44%)
  waiting for transfers between devices  41 us (30%)
  other arithmetic  17.1 us (12%)
  local copies, waits for them, and re-layouts  13 us (9%)
  between operations  4.19 us (3%)
  matrix products  2.4 us (2%)
    ppermute x24, starting transfers between devices, extended(): after = lax.ppermute(first, axis, down)  42.6 us
    ppermute x24, waiting for transfers between devices, extended(): before = lax.ppermute(last, axis, up)  27.9 us
    ppermute x24, starting transfers between devices, extended(): before = lax.ppermute(last, axis, up)  17.5 us
    ppermute x24, waiting for transfers between devices, extended(): after = lax.ppermute(first, axis, down)  13.1 us
    unnamed x166, other arithmetic  3.66 us
  transfers between devices with their start and end apart: 48, of which 37 were waited for; matrix products, arithmetic and copies ran while one was open for 6% of the time, Pallas kernels for 0%

commit v1 on v0

v1 whole, which is shorter than its diff:
```python
import math

import jax
import jax.numpy as jnp
import numpy as np
from jax import lax
from jax.experimental import pallas as pl
from jax.experimental.pallas import tpu as pltpu
from jax.sharding import PartitionSpec as P

STEPS = 4
HALO = 2 * STEPS
LANES = 128

C = np.array(
    [
        [0, 0, 0],
        [1, 0, 0],
        [-1, 0, 0],
        [0, 1, 0],
        [0, -1, 0],
        [0, 0, 1],
        [0, 0, -1],
        [1, 1, 0],
        [-1, -1, 0],
        [1, -1, 0],
        [-1, 1, 0],
        [1, 0, 1],
        [-1, 0, -1],
        [1, 0, -1],
        [-1, 0, 1],
        [0, 1, 1],
        [0, -1, -1],
        [0, 1, -1],
        [0, -1, 1],
    ]
)
WEIGHTS = [1.0 / 3.0] + [1.0 / 18.0] * 6 + [1.0 / 36.0] * 12
OPPOSITE = [0, 2, 1, 4, 3, 6, 5, 8, 7, 10, 9, 12, 11, 14, 13, 16, 15, 18, 17]
LIQUID = 0.28
VAPOUR = 0.06
WALL_POTENTIAL = 0.5
ATTRACTION = 1.0
TEMPERATURE = 0.06

KEEP_E = 1.0 - 1.19
KEEP_P = 1.0 - 1.4
KEEP_Q = 1.0 - 1.2
KEEP_N = 1.0 - 1.25
KEEP_M = 1.0 - 1.98


def equilibrium(rho, u):
    rest = 1.0 - 1.5 * (u[0] * u[0] + u[1] * u[1] + u[2] * u[2])
    scaled = [None] * 3
    scaled[0] = rho * WEIGHTS[0]
    scaled[1] = rho * WEIGHTS[1]
    scaled[2] = rho * WEIGHTS[7]
    rows = [scaled[0] * rest]
    for i in range(1, 19, 2):
        terms = [u[k] if C[i, k] > 0 else -u[k] for k in range(3) if C[i, k] != 0]
        along = terms[0] if len(terms) == 1 else terms[0] + terms[1]
        even = rest + 4.5 * (along * along)
        odd = 3.0 * along
        w = scaled[len(terms)]
        rows += [w * (even + odd), w * (even - odd)]
    return rows


def potential(rho, solid):
    square = rho * rho
    gap = 1.0 - rho
    pressure = (
        rho * TEMPERATURE * (1.0 + rho + square - square * rho) / (gap * gap * gap)
        - ATTRACTION * square
    )
    return jnp.where(solid, WALL_POTENTIAL, jnp.sqrt(6.0 * (rho * (1.0 / 3.0) - pressure)))


def moments(f):
    d = [None] + [f[i] - f[i + 1] for i in range(1, 19, 2)]
    jx = d[1] + ((d[4] + d[5]) + (d[6] + d[7]))
    jy = d[2] + ((d[4] - d[5]) + (d[8] + d[9]))
    jz = d[3] + ((d[6] - d[7]) + (d[8] - d[9]))
    return jx, jy, jz


def collide(f, force, solid):
    s = [None] + [f[i] + f[i + 1] for i in range(1, 19, 2)]
    d = [None] + [f[i] - f[i + 1] for i in range(1, 19, 2)]
    xy, xz, yz = s[4] + s[5], s[6] + s[7], s[8] + s[9]
    axes = s[1] + s[2] + s[3]
    diagonals = xy + xz + yz
    rho = f[0] + axes + diagonals
    p_xy, q_xy = d[4] + d[5], d[4] - d[5]
    p_xz, q_xz = d[6] + d[7], d[6] - d[7]
    p_yz, q_yz = d[8] + d[9], d[8] - d[9]
    j = [d[1] + (p_xy + p_xz), d[2] + (q_xy + p_yz), d[3] + (q_xz + q_yz)]
    inverse = 1.0 / rho
    u = [j[k] * inverse for k in range(3)]
    moved = [j[k] + force[k] for k in range(3)]
    v = [moved[k] * inverse for k in range(3)]
    uu = [j[k] * u[k] for k in range(3)]
    vv = [moved[k] * v[k] for k in range(3)]
    u2 = uu[0] + uu[1] + uu[2]
    v2 = vv[0] + vv[1] + vv[2]

    energy = (
        KEEP_E * (8.0 * diagonals - 11.0 * axes - 30.0 * f[0])
        - (11.0 * (1.0 - KEEP_E)) * rho
        + 19.0 * (v2 - KEEP_E * u2)
    )
    epsilon = (
        KEEP_P * (12.0 * f[0] - 4.0 * axes + diagonals)
        + (3.0 * (1.0 - KEEP_P)) * rho
        - 5.5 * (v2 - KEEP_P * u2)
    )
    mass = rho * (1.0 / 19.0)
    even_rest = mass - (30.0 / 2394.0) * energy + (12.0 / 252.0) * epsilon
    even_axis = mass - (11.0 / 2394.0) * energy - (4.0 / 252.0) * epsilon
    even_diag = mass + (8.0 / 2394.0) * energy + (1.0 / 252.0) * epsilon

    def stress(a, b, at_v, at_u, scale):
        on_axis = (
            ((KEEP_N + 2.0 * KEEP_P) * scale) * a
            + ((KEEP_N - KEEP_P) * scale) * b
            + (1.5 * scale) * at_v
            - ((KEEP_N + 0.5 * KEEP_P) * scale) * at_u
        )
        half = 0.5 * scale
        on_diagonal = (
            ((2.0 * KEEP_N - 2.0 * KEEP_P) * half) * a
            + ((2.0 * KEEP_N + KEEP_P) * half) * b
            + (1.5 * half) * at_v
            - ((2.0 * KEEP_N - 0.5 * KEEP_P) * half) * at_u
        )
        return on_axis, on_diagonal

    h, g = stress(
        3.0 * s[1] - axes,
        diagonals - 3.0 * yz,
        3.0 * vv[0] - v2,
        3.0 * uu[0] - u2,
        1.0 / 36.0,
    )
    k, l = stress(s[2] - s[3], xy - xz, vv[1] - vv[2], uu[1] - uu[2], 1.0 / 12.0)

    def shear(a, b, pair):
        return (0.25 * KEEP_N) * (pair - j[a] * u[b]) + 0.25 * (moved[a] * v[b])

    t_xy = shear(0, 1, s[4] - s[5])
    t_xz = shear(0, 2, s[6] - s[7])
    t_yz = shear(1, 2, s[8] - s[9])

    flux_j = KEEP_Q * 5.0 / 3.0 - 2.0 / 3.0
    axis_odd = [
        ((1.0 - flux_j) / 10.0) * j[n] + (0.5 * KEEP_Q) * d[n + 1] + (1.0 / 6.0) * force[n]
        for n in range(3)
    ]
    diag_odd = [
        (0.1 + flux_j / 40.0) * j[n] - (KEEP_Q / 8.0) * d[n + 1] + (1.0 / 12.0) * force[n]
        for n in range(3)
    ]
    third = KEEP_M / 8.0
    mx, my, mz = third * (p_xy - p_xz), third * (p_yz - q_xy), third * (q_xz - q_yz)

    twist = even_axis - h
    evens = [even_axis + 2.0 * h, twist + k, twist - k]
    ring = even_diag + g
    e_xy, e_xz, e_yz = ring + l, ring - l, even_diag - 2.0 * g
    a, b = diag_odd[0] + mx, diag_odd[1] - my
    odd_xy = (a + b, a - b)
    a, b = diag_odd[0] - mx, diag_odd[2] + mz
    odd_xz = (a + b, a - b)
    a, b = diag_odd[1] + my, diag_odd[2] - mz
    odd_yz = (a + b, a - b)

    post = [even_rest]
    for n in range(3):
        post += [evens[n] + axis_odd[n], evens[n] - axis_odd[n]]
    for even, t, odd in ((e_xy, t_xy, odd_xy), (e_xz, t_xz, odd_xz), (e_yz, t_yz, odd_yz)):
        same, cross = even + t, even - t
        post += [same + odd[0], same - odd[0], cross + odd[1], cross - odd[1]]
    return [jnp.where(solid, f[OPPOSITE[i]], post[i]) for i in range(19)]


class Shape:
    def __init__(self, mesh, block):
        self.nx, self.ny, self.nz = (mesh.shape[a] for a in ("gx", "gy", "gz"))
        self.x, self.y, self.z = block
        self.slab = self.z // self.nx
        width = 1
        while width < self.slab + 2 * HALO:
            width *= 2
        self.width = width
        self.groups = LANES // width
        self.own = self.x // self.groups
        self.subs = self.x * self.nx // self.groups
        self.rows = self.y + 2 * HALO
        assert self.z == LANES and self.slab * self.nx == self.z and width <= LANES
        assert self.y == HALO and self.own * self.groups == self.x
        assert self.subs % 8 == 0 and self.slab * self.x <= LANES
        if self.nx & (self.nx - 1) == 0:
            self.peer = lambda k, slot: jnp.bitwise_xor(k, slot)
            self.perm = lambda slot: [(i, i ^ slot) for i in range(self.nx)]
            self.sender = self.peer
        else:
            self.peer = lambda k, slot: lax.rem(k + slot, self.nx)
            self.sender = lambda k, slot: lax.rem(k + self.nx - slot, self.nx)
            self.perm = lambda slot: [(i, (i + slot) % self.nx) for i in range(self.nx)]


def vmem(n):
    return [pl.BlockSpec(memory_space=pltpu.VMEM)] * n


def gather_inputs(scatter, velocity, bubbles, walls):
    def body(s_ref, u_ref, b_ref, w_ref, out):
        out[0] = jnp.where(b_ref[...] == 1, VAPOUR, LIQUID) * s_ref[...]
        for k in range(3):
            out[1 + k] = u_ref[k]
        out[4] = jnp.where(w_ref[...] == 1, 1.0, 0.0)

    return pl.pallas_call(
        body,
        name="pack_inputs",
        out_shape=jax.ShapeDtypeStruct((5,) + scatter.shape, jnp.float32),
        in_specs=vmem(4),
        out_specs=vmem(1)[0],
    )(scatter, velocity, bubbles, walls)


def cut_slabs(values, before, after, sh):
    def body(v_ref, b_ref, a_ref, *outs):
        k = lax.axis_index("gx")
        lane = lax.broadcasted_iota(jnp.int32, (sh.y, LANES), 1)
        group = lane // sh.width
        for slot, out in enumerate(outs):
            q = sh.peer(k, slot)
            low = (lane >= LANES - HALO) & (q == 0)
            high = (lane < HALO) & (q == sh.nx - 1)
            start = HALO - q * sh.slab + 2 * LANES
            for n in range(5):
                for m in range(sh.own):
                    merged = None
                    for g in range(sh.groups):
                        x = m * sh.groups + g
                        plane = jnp.where(low, b_ref[n, x], v_ref[n, x])
                        plane = jnp.where(high, a_ref[n, x], plane)
                        plane = pltpu.roll(plane, lax.rem(start + g * sh.width, LANES), 1)
                        merged = plane if g == 0 else jnp.where(group == g, plane, merged)
                    out[n, m] = merged

    return pl.pallas_call(
        body,
        name="cut_slabs",
        out_shape=[jax.ShapeDtypeStruct((5, sh.own, sh.y, LANES), jnp.float32)] * sh.nx,
        in_specs=vmem(3),
        out_specs=vmem(sh.nx),
    )(values, before, after)


def run_steps(below, middle, above, sh):
    rows, subs, width = sh.rows, sh.subs, sh.width

    def body(b_ref, m_ref, a_ref, *rest):
        outs = rest[: sh.nx]
        raw, first, second, psi_ref, solid_ref, done = rest[sh.nx :]
        k = lax.axis_index("gx")
        lane = lax.broadcasted_iota(jnp.int32, (subs, LANES), 1)
        group = lane // width

        for slot in range(sh.nx):
            base = sh.sender(k, slot) * (sh.own * rows)
            for part, ref in enumerate((b_ref, m_ref, a_ref)):
                for n in range(5):
                    for m in range(sh.own):
                        at = pl.multiple_of(base + m * rows + part * sh.y, 8)
                        raw[n, pl.ds(at, sh.y), :] = ref[slot, n, m]

        def shifted(value, cx, cz):
            if cx == 1:
                turned = pltpu.roll(value, 1, 0)
                value = jnp.where(group == sh.groups - 1, turned, value)
            if cx == -1:
                turned = pltpu.roll(value, subs - 1, 0)
                value = jnp.where(group == 0, turned, value)
            turn = (cx * width + cz) % LANES
            return pltpu.roll(value, turn, 1) if turn else value

        def start(y, _):
            read = lambda n: raw[n, pl.ds(y, subs, stride=rows), :]
            rho, u = read(0), [read(1), read(2), read(3)]
            solid_ref[y] = read(4)
            for i, row in enumerate(equilibrium(rho, u)):
                first[i, y] = row
            return 0

        lax.fori_loop(0, rows, start, 0)

        source, target = first, second
        for step in range(STEPS):

            def weigh(y, source=source):
                rho = source[0, y]
                for i in range(1, 19):
                    rho = rho + source[i, y]
                psi_ref[y] = potential(rho, solid_ref[y] > 0.5)

            def advance(y, source=source, target=target):
                here, up, down = psi_ref[y], psi_ref[y + 1], psi_ref[y - 1]
                both, rise = up + down, up - down
                doubled = 2.0 * here + both
                z_sum = doubled + (shifted(here, 0, -1) + shifted(here, 0, 1))
                x_sum = doubled + (shifted(here, -1, 0) + shifted(here, 1, 0))
                scale = here * (1.0 / 36.0)
                force = [
                    scale * (shifted(z_sum, -1, 0) - shifted(z_sum, 1, 0)),
                    scale
                    * (
                        2.0 * rise
                        + (shifted(rise, -1, 0) + shifted(rise, 1, 0))
                        + (shifted(rise, 0, -1) + shifted(rise, 0, 1))
                    ),
                    scale * (shifted(x_sum, 0, -1) - shifted(x_sum, 0, 1)),
                ]
                f = [source[i, y] for i in range(19)]
                post = collide(f, force, solid_ref[y] > 0.5)
                for i in range(19):
                    cx, cy, cz = (int(c) for c in C[i])
                    target[i, y + cy] = shifted(post[i], cx, cz)

            lo = 2 * step

            def weigh_some(n, _):
                for r in range(4):
                    weigh(lo + 4 * n + r)
                return 0

            def advance_some(n, _):
                for r in range(2):
                    advance(lo + 1 + 2 * n + r)
                return 0

            lax.fori_loop(0, (rows - 2 * lo) // 4, weigh_some, 0)
            lax.fori_loop(0, (rows - 2 * lo - 2) // 2, advance_some, 0)
            source, target = target, source

        def finish(y, _):
            f = [source[i, y + HALO] for i in range(19)]
            rho = f[0]
            for i in range(1, 19):
                rho = rho + f[i]
            fluid = solid_ref[y + HALO] < 0.5
            inverse = math.sqrt(3.0) / rho
            results = [rho * (1.0 / LIQUID)] + [c * inverse for c in moments(f)]
            for n, value in enumerate(results):
                done[n, pl.ds(y, subs, stride=sh.y), :] = jnp.where(fluid, value, 0.0)
            return 0

        lax.fori_loop(0, sh.y, finish, 0)

        lane = lax.broadcasted_iota(jnp.int32, (sh.y, LANES), 1)
        place = lane // sh.slab
        for slot, out in enumerate(outs):
            base = sh.peer(k, slot) * (sh.own * sh.y)
            for n in range(4):
                merged = None
                for x in range(sh.x):
                    m, g = divmod(x, sh.groups)
                    at = pl.multiple_of(base + m * sh.y, 8)
                    turn = (x * sh.slab - g * width - HALO) % LANES
                    value = done[n, pl.ds(at, sh.y), :]
                    value = pltpu.roll(value, turn, 1) if turn else value
                    merged = value if x == 0 else jnp.where(place == x, value, merged)
                out[n] = merged

    populations = pltpu.VMEM((19, rows, subs, LANES), jnp.float32)
    return pl.pallas_call(
        body,
        name="run_steps",
        out_shape=[jax.ShapeDtypeStruct((4, sh.y, LANES), jnp.float32)] * sh.nx,
        in_specs=vmem(3),
        out_specs=vmem(sh.nx),
        scratch_shapes=[
            pltpu.VMEM((5, subs * rows, LANES), jnp.float32),
            populations,
            populations,
            pltpu.VMEM((rows, subs, LANES), jnp.float32),
            pltpu.VMEM((rows, subs, LANES), jnp.float32),
            pltpu.VMEM((4, subs * sh.y, LANES), jnp.float32),
        ],
    )(below, middle, above)


def place_outputs(pieces, sh):
    def body(*refs):
        ins, (density, velocity) = refs[: sh.nx], refs[sh.nx :]
        k = lax.axis_index("gx")
        lane = lax.broadcasted_iota(jnp.int32, (sh.y, LANES), 1)
        place = lane // sh.slab
        for n in range(4):
            for x in range(sh.x):
                merged = None
                for slot, ref in enumerate(ins):
                    q = sh.sender(k, slot)
                    turn = lax.rem((q - x) * sh.slab + LANES, LANES)
                    value = pltpu.roll(ref[n], turn, 1)
                    merged = value if slot == 0 else jnp.where(place == q, value, merged)
                if n == 0:
                    density[x] = merged
                else:
                    velocity[n - 1, x] = merged

    block = (sh.x, sh.y, sh.z)
    return pl.pallas_call(
        body,
        name="place_outputs",
        out_shape=[
            jax.ShapeDtypeStruct(block, jnp.float32),
            jax.ShapeDtypeStruct((3,) + block, jnp.float32),
        ],
        in_specs=vmem(sh.nx),
        out_specs=vmem(2),
    )(*pieces)


def ring(size, step):
    return [(i, (i + step) % size) for i in range(size)]


def solution(mesh):
    def on_device(density_scatter, initial_velocity, bubble_mask, wall_flags):
        sh = Shape(mesh, wall_flags.shape)
        values = gather_inputs(density_scatter, initial_velocity, bubble_mask, wall_flags)
        before = lax.ppermute(values, "gz", ring(sh.nz, 1))
        after = before if sh.nz == 2 else lax.ppermute(values, "gz", ring(sh.nz, -1))
        slabs = cut_slabs(values, before, after, sh)
        got = [slabs[0]]
        for slot in range(1, sh.nx):
            got.append(lax.ppermute(slabs[slot], "gx", sh.perm(slot)))
        middle = jnp.stack(got)
        below = lax.ppermute(middle, "gy", ring(sh.ny, 1))
        above = lax.ppermute(middle, "gy", ring(sh.ny, -1))
        pieces = run_steps(below, middle, above, sh)
        back = [pieces[0]]
        for slot in range(1, sh.nx):
            back.append(lax.ppermute(pieces[slot], "gx", sh.perm(slot)))
        return tuple(place_outputs(back, sh))

    in_specs = (
        P("gx", "gy", "gz"),
        P(None, "gx", "gy", "gz"),
        P("gx", "gy", "gz"),
        P("gx", "gy", "gz"),
    )
    out_specs = (P("gx", "gy", "gz"), P(None, "gx", "gy", "gz"))
    return jax.shard_map(
        on_device, mesh=mesh, in_specs=in_specs, out_specs=out_specs, check_vma=False
    )
```

time: 138 us -> 48.5 us (0.35)
  starting transfers between devices: 60.1 us -> 12 us
  waiting for transfers between devices: 41 us -> 15.9 us
  Pallas kernels: 0 us -> 16.9 us
  other arithmetic: 17.1 us -> 0.79 us
  local copies, waits for them, and re-layouts: 13 us -> 1.9 us
  between operations: 4.19 us -> 0.66 us
  matrix products: 2.4 us -> 0 us
    ppermute x48 -> x9, starting transfers between devices: 60.1 us -> 12 us  [the longest x3 4.35 us: on_device(): got.append(lax.ppermute(slabs[slot], 'gx', sh.perm(slot)))]
    ppermute x48 -> x9, waiting for transfers between devices: 41 us -> 15.9 us  [the longest x3 5.11 us: on_device(): got.append(lax.ppermute(slabs[slot], 'gx', sh.perm(slot)))]
    pallas_call x0 -> x4, Pallas kernels: none -> 16.9 us  [the longest x1 12.2 us: run_steps(): pl.pallas_call(body, name='run_steps', out_shape=[jax.ShapeDtypeStruct((4...]
    slice x126 -> x0, local copies, waits for them, and re-layouts: 5.2 us -> none  [the longest x17 1.6 us: stream_along(): lax.slice_in_dim(rows[i], length - 1, length, axis=dim)]
    unnamed x166 -> x0, other arithmetic: 3.66 us -> none
    concatenate x110 -> x0, other arithmetic: 3.48 us -> none  [the longest x48 2 us: stream_along(): jnp.concatenate([lax.slice_in_dim(rows[i], 1, length, axis=dim), upper_ne...]
    select_n x10 -> x0, other arithmetic: 3.37 us -> none  [the longest x4 1.37 us: on_device(): jnp.where(solid, wall_potential, pseudo_potential(mass_per_volume))]
    dot_general x4 -> x0, matrix products: 2.4 us -> none  [collide(): jnp.einsum('ij,jxyz->ixyz', kernel, populations - settled, precision=lax....]
  transfers between devices with their start and end apart: 48 -> 9, of which waited for: 37 -> 9; matrix products, arithmetic and copies ran while one was open for 6% -> 0% of each run, Pallas kernels for 0% -> 0%
where the time goes in v1:
time: 48.5 us; the launch traced here: 48.2 us
  Pallas kernels  16.9 us (35%)
  waiting for transfers between devices  15.9 us (33%)
  starting transfers between devices  12 us (25%)
  local copies, waits for them, and re-layouts  1.9 us (4%)
  other arithmetic  0.79 us (2%)
  between operations  0.66 us (1%)
    pallas_call x1, Pallas kernels, run_steps(): pl.pallas_call(body, name='run_steps', out_shape=[jax.ShapeDtypeStruct((4...  12.2 us
    ppermute x3, waiting for transfers between devices, on_device(): got.append(lax.ppermute(slabs[slot], 'gx', sh.perm(slot)))  5.11 us
    ppermute x3, starting transfers between devices, on_device(): got.append(lax.ppermute(slabs[slot], 'gx', sh.perm(slot)))  4.35 us
    ppermute x1, waiting for transfers between devices, on_device(): above = lax.ppermute(middle, 'gy', ring(sh.ny, -1))  3.82 us
    ppermute x1, starting transfers between devices, on_device(): above = lax.ppermute(middle, 'gy', ring(sh.ny, -1))  3.65 us
    ppermute x3, starting transfers between devices, on_device(): back.append(lax.ppermute(pieces[slot], 'gx', sh.perm(slot)))  3.49 us
    ppermute x1, waiting for transfers between devices, on_device(): below = lax.ppermute(middle, 'gy', ring(sh.ny, 1))  3.43 us
    ppermute x3, waiting for transfers between devices, on_device(): back.append(lax.ppermute(pieces[slot], 'gx', sh.perm(slot)))  2.4 us
  transfers between devices with their start and end apart: 9, of which 9 were waited for; matrix products, arithmetic and copies ran while one was open for 0% of the time, Pallas kernels for 0%

profile of v1, /device:TPU:0, one launch (start us, length us, event | category | flops | bytes accessed | tf_op | source)
XLA Modules:
  0.0 48.2 jit_solution(9220937754449237101)
XLA Ops:
  0.6 1.4 %pack_inputs.1.v_ref = f32[5,4,8,128]{3,2,1,0:T(8,128)} custom-call(f32[4,8,128]{2,1,0:T(8,128)} %s_ref.1, f32[3,4,8,128]{3,2,1,0:T(8,128)} %u_ref.1, s32[4,8,128]{2,1,0:T(8,128)} %b_ref.1, s32[4,8,128]{2,1,0:T(8,128)} %w_ref.1), custom_call_target="tpu_custom_call" | custom-call | tf_op jit(solution)/shard_map/pack_inputs/pallas_call | solution.py:224
  2.1 0.5 %collective-permute-start = (f32[5,4,8,128]{3,2,1,0:T(8,128)}, f32[5,4,8,128]{3,2,1,0:T(8,128)S(1)}, u32[]{:S(2)}, u32[]{:S(2)}) collective-permute-start(f32[5,4,8,128]{3,2,1,0:T(8,128)} %pack_inputs.1.v_ref), channel_id=1, source_target_pairs={{0,1},{1,0},{2,3},{3,2},{4,5},{5,4},{6,7},{7,6},{8,9},{9,8},{10,11... | collective-permute-start | bytes 245768 | tf_op jit(solution)/shard_map/ppermute | solution.py:436
  2.6 1.1 %collective-permute-done.b_ref.a_ref = f32[5,4,8,128]{3,2,1,0:T(8,128)S(1)} collective-permute-done((f32[5,4,8,128]{3,2,1,0:T(8,128)}, f32[5,4,8,128]{3,2,1,0:T(8,128)S(1)}, u32[]{:S(2)}, u32[]{:S(2)}) %collective-permute-start) | collective-permute-done | bytes 81952 | tf_op jit(solution)/shard_map/ppermute | solution.py:436
  3.7 0.6 %copy-done.1 = f32[5,4,8,128]{3,2,1,0:T(8,128)} copy-done((f32[5,4,8,128]{3,2,1,0:T(8,128)}, f32[5,4,8,128]{3,2,1,0:T(8,128)S(1)}, u32[]{:S(2)}) %copy-start.1) | copy-done | bytes 81944
  4.3 1.8 %cut_slabs.1 = (f32[5,2,8,128]{3,2,1,0:T(8,128)}, f32[5,2,8,128]{3,2,1,0:T(8,128)}, f32[5,2,8,128]{3,2,1,0:T(8,128)}, f32[5,2,8,128]{3,2,1,0:T(8,128)}) custom-call(f32[5,4,8,128]{3,2,1,0:T(8,128)} %pack_inputs.1.v_ref, f32[5,4,8,128]{3,2,1,0:T(8,128)} %copy-done.1, f32[5,4,8,128]{3,2,1,0:T(8,128)} %copy-done.1), custom_call_target="tpu_custom_call" | custom-call | tf_op jit(solution)/shard_map/cut_slabs/pallas_call | solution.py:254
  6.1 2.8 %collective-permute-start.1 = (f32[5,2,8,128]{3,2,1,0:T(8,128)}, f32[5,2,8,128]{3,2,1,0:T(8,128)S(1)}, u32[]{:S(2)}, u32[]{:S(2)}) collective-permute-start(f32[5,2,8,128]{3,2,1,0:T(8,128)} %get-tuple-element.11), channel_id=1, source_target_pairs={{0,8},{8,0},{16,24},{24,16},{1,9},{9,1},{17,25},{25,17},{2,10},{10... | collective-permute-start | bytes 122888 | tf_op jit(solution)/shard_map/ppermute | solution.py:441
  8.9 1.5 %collective-permute-start.2 = (f32[5,2,8,128]{3,2,1,0:T(8,128)}, f32[5,2,8,128]{3,2,1,0:T(8,128)S(1)}, u32[]{:S(2)}, u32[]{:S(2)}) collective-permute-start(f32[5,2,8,128]{3,2,1,0:T(8,128)} %get-tuple-element.12), channel_id=1, source_target_pairs={{0,16},{8,24},{16,0},{24,8},{1,17},{9,25},{17,1},{25,9},{2,18},{10... | collective-permute-start | bytes 122888 | tf_op jit(solution)/shard_map/ppermute | solution.py:441
  10.4 0.7 %collective-permute-done.1 = f32[5,2,8,128]{3,2,1,0:T(8,128)S(1)} collective-permute-done((f32[5,2,8,128]{3,2,1,0:T(8,128)}, f32[5,2,8,128]{3,2,1,0:T(8,128)S(1)}, u32[]{:S(2)}, u32[]{:S(2)}) %collective-permute-start.1) | collective-permute-done | bytes 40992 | tf_op jit(solution)/shard_map/ppermute | solution.py:441
  11.1 2.0 %collective-permute-done.2 = f32[5,2,8,128]{3,2,1,0:T(8,128)S(1)} collective-permute-done((f32[5,2,8,128]{3,2,1,0:T(8,128)}, f32[5,2,8,128]{3,2,1,0:T(8,128)S(1)}, u32[]{:S(2)}, u32[]{:S(2)}) %collective-permute-start.2) | collective-permute-done | bytes 40992 | tf_op jit(solution)/shard_map/ppermute | solution.py:441
  13.1 2.4 %collective-permute-done.3 = f32[5,2,8,128]{3,2,1,0:T(8,128)S(1)} collective-permute-done((f32[5,2,8,128]{3,2,1,0:T(8,128)}, f32[5,2,8,128]{3,2,1,0:T(8,128)S(1)}, u32[]{:S(2)}, u32[]{:S(2)}) %collective-permute-start.3) | collective-permute-done | bytes 40992 | tf_op jit(solution)/shard_map/ppermute | solution.py:441
  15.5 0.8 %pad_maximum_fusion.m_ref = f32[4,5,2,8,128]{4,3,2,1,0:T(8,128)S(1)} fusion(f32[1,5,2,8,128]{4,3,2,1,0:T(8,128)S(1)} %bitcast.7, f32[1,5,2,8,128]{4,3,2,1,0:T(8,128)S(1)} %bitcast.6, f32[1,5,2,8,128]{4,3,2,1,0:T(8,128)S(1)} %bitcast.5, f32[1,5,2,8,128]{4,3,2,1,0:T(8,128)} %bitcast.4), kind=kLoop, calls=%fused_computation | loop fusion | flops 122880 | bytes 327680 | tf_op jit(solution)/shard_map/stack | solution.py:442
  16.3 3.7 %collective-permute-start.5 = (f32[4,5,2,8,128]{4,3,2,1,0:T(8,128)S(1)}, f32[4,5,2,8,128]{4,3,2,1,0:T(8,128)S(1)}, u32[]{:S(2)}, u32[]{:S(2)}) collective-permute-start(f32[4,5,2,8,128]{4,3,2,1,0:T(8,128)S(1)} %pad_maximum_fusion.m_ref), channel_id=1, source_target_pairs={{0,6},{2,0},{4,2},{6,4},{1,7},{3,1},{5,3},{7,5},{8,14},{10,8},{12,... | collective-permute-start | bytes 491528 | tf_op jit(solution)/shard_map/ppermute | solution.py:444
  20.0 3.8 %collective-permute-done.5.a_ref = f32[4,5,2,8,128]{4,3,2,1,0:T(8,128)S(1)} collective-permute-done((f32[4,5,2,8,128]{4,3,2,1,0:T(8,128)S(1)}, f32[4,5,2,8,128]{4,3,2,1,0:T(8,128)S(1)}, u32[]{:S(2)}, u32[]{:S(2)}) %collective-permute-start.5) | collective-permute-done | bytes 163872 | tf_op jit(solution)/shard_map/ppermute | solution.py:444
  23.8 3.4 %collective-permute-done.4.b_ref = f32[4,5,2,8,128]{4,3,2,1,0:T(8,128)S(1)} collective-permute-done((f32[4,5,2,8,128]{4,3,2,1,0:T(8,128)S(1)}, f32[4,5,2,8,128]{4,3,2,1,0:T(8,128)S(1)}, u32[]{:S(2)}, u32[]{:S(2)}) %collective-permute-start.4) | collective-permute-done | bytes 163872 | tf_op jit(solution)/shard_map/ppermute | solution.py:443
  27.3 0.7 %copy-done.3 = f32[4,5,2,8,128]{4,3,2,1,0:T(8,128)} copy-done((f32[4,5,2,8,128]{4,3,2,1,0:T(8,128)}, f32[4,5,2,8,128]{4,3,2,1,0:T(8,128)S(1)}, u32[]{:S(2)}) %copy-start.3) | copy-done | bytes 163864
  27.9 12.2 %run_steps.1 = (f32[4,8,128]{2,1,0:T(8,128)}, f32[4,8,128]{2,1,0:T(8,128)}, f32[4,8,128]{2,1,0:T(8,128)}, f32[4,8,128]{2,1,0:T(8,128)}) custom-call(f32[4,5,2,8,128]{4,3,2,1,0:T(8,128)} %copy-done.3, f32[4,5,2,8,128]{4,3,2,1,0:T(8,128)} %copy-done, f32[4,5,2,8,128]{4,3,2,1,0:T(8,128)} %copy-done.2), custom_call_target="tpu_custom_call" | custom-call | tf_op jit(solution)/shard_map/run_steps/pallas_call | solution.py:379
  40.1 0.5 %collective-permute-start.6 = (f32[4,8,128]{2,1,0:T(8,128)}, f32[4,8,128]{2,1,0:T(8,128)S(1)}, u32[]{:S(2)}, u32[]{:S(2)}) collective-permute-start(f32[4,8,128]{2,1,0:T(8,128)} %get-tuple-element.15), channel_id=1, source_target_pairs={{0,8},{8,0},{16,24},{24,16},{1,9},{9,1},{17,25},{25,17},{2,10},{10... | collective-permute-start | bytes 49160 | tf_op jit(solution)/shard_map/ppermute | solution.py:448
  40.6 0.5 %collective-permute-start.7 = (f32[4,8,128]{2,1,0:T(8,128)}, f32[4,8,128]{2,1,0:T(8,128)S(1)}, u32[]{:S(2)}, u32[]{:S(2)}) collective-permute-start(f32[4,8,128]{2,1,0:T(8,128)} %get-tuple-element.16), channel_id=1, source_target_pairs={{0,16},{8,24},{16,0},{24,8},{1,17},{9,25},{17,1},{25,9},{2,18},{10... | collective-permute-start | bytes 49160 | tf_op jit(solution)/shard_map/ppermute | solution.py:448
  41.2 2.4 %collective-permute-start.8 = (f32[4,8,128]{2,1,0:T(8,128)}, f32[4,8,128]{2,1,0:T(8,128)S(1)}, u32[]{:S(2)}, u32[]{:S(2)}) collective-permute-start(f32[4,8,128]{2,1,0:T(8,128)} %get-tuple-element.17), channel_id=1, source_target_pairs={{0,24},{8,16},{16,8},{24,0},{1,25},{9,17},{17,9},{25,1},{2,26},{10... | collective-permute-start | bytes 49160 | tf_op jit(solution)/shard_map/ppermute | solution.py:448
  43.6 0.5 collective-permute-done.6.refs_1_
  44.1 0.5 %collective-permute-done.7.refs_2_ = f32[4,8,128]{2,1,0:T(8,128)S(1)} collective-permute-done((f32[4,8,128]{2,1,0:T(8,128)}, f32[4,8,128]{2,1,0:T(8,128)S(1)}, u32[]{:S(2)}, u32[]{:S(2)}) %collective-permute-start.7) | collective-permute-done | bytes 16416 | tf_op jit(solution)/shard_map/ppermute | solution.py:448
  44.6 1.4 %collective-permute-done.8.refs_3_ = f32[4,8,128]{2,1,0:T(8,128)S(1)} collective-permute-done((f32[4,8,128]{2,1,0:T(8,128)}, f32[4,8,128]{2,1,0:T(8,128)S(1)}, u32[]{:S(2)}, u32[]{:S(2)}) %collective-permute-start.8) | collective-permute-done | bytes 16416 | tf_op jit(solution)/shard_map/ppermute | solution.py:448
  46.0 0.6 %copy-done.6 = f32[4,8,128]{2,1,0:T(8,128)} copy-done((f32[4,8,128]{2,1,0:T(8,128)}, f32[4,8,128]{2,1,0:T(8,128)S(1)}, u32[]{:S(2)}) %copy-start.6) | copy-done | bytes 16408
  46.6 1.6 %place_outputs.1 = (f32[4,8,128]{2,1,0:T(8,128)}, f32[3,4,8,128]{3,2,1,0:T(8,128)}) custom-call(f32[4,8,128]{2,1,0:T(8,128)} %get-tuple-element.14.refs_0_, f32[4,8,128]{2,1,0:T(8,128)} %copy-done.4, f32[4,8,128]{2,1,0:T(8,128)} %copy-done.5, f32[4,8,128]{2,1,0:T(8,128)} %copy-done.6), custom_call_target="tpu_custom_call" | custom-call | tf_op jit(solution)/shard_map/place_outputs/pallas_call | solution.py:416
  (13 shorter events, 0.0 us)
Async XLA Ops:
  2.1 1.6 %collective-permute-start = (f32[5,4,8,128]{3,2,1,0:T(8,128)}, f32[5,4,8,128]{3,2,1,0:T(8,128)S(1)}, u32[]{:S(2)}, u32[]{:S(2)}) collective-permute-start(f32[5,4,8,128]{3,2,1,0:T(8,128)} %pack_inputs.1.v_ref), channel_id=1, source_target_pairs={{0,1},{1,0},{2,3},{3,2},{4,5},{5,4},{6,7},{7,6},{8,9},{9,8},{10,11... | collective-permute-start | bytes 245768 | tf_op jit(solution)/shard_map/ppermute | solution.py:436
  3.7 0.6 %copy-start.1 = (f32[5,4,8,128]{3,2,1,0:T(8,128)}, f32[5,4,8,128]{3,2,1,0:T(8,128)S(1)}, u32[]{:S(2)}) copy-start(f32[5,4,8,128]{3,2,1,0:T(8,128)S(1)} %collective-permute-done.b_ref.a_ref) | copy-start | bytes 245764
  6.1 5.0 %collective-permute-start.1 = (f32[5,2,8,128]{3,2,1,0:T(8,128)}, f32[5,2,8,128]{3,2,1,0:T(8,128)S(1)}, u32[]{:S(2)}, u32[]{:S(2)}) collective-permute-start(f32[5,2,8,128]{3,2,1,0:T(8,128)} %get-tuple-element.11), channel_id=1, source_target_pairs={{0,8},{8,0},{16,24},{24,16},{1,9},{9,1},{17,25},{25,17},{2,10},{10... | collective-permute-start | bytes 122888 | tf_op jit(solution)/shard_map/ppermute | solution.py:441
  8.9 4.2 %collective-permute-start.2 = (f32[5,2,8,128]{3,2,1,0:T(8,128)}, f32[5,2,8,128]{3,2,1,0:T(8,128)S(1)}, u32[]{:S(2)}, u32[]{:S(2)}) collective-permute-start(f32[5,2,8,128]{3,2,1,0:T(8,128)} %get-tuple-element.12), channel_id=1, source_target_pairs={{0,16},{8,24},{16,0},{24,8},{1,17},{9,25},{17,1},{25,9},{2,18},{10... | collective-permute-start | bytes 122888 | tf_op jit(solution)/shard_map/ppermute | solution.py:441
  10.4 5.1 %collective-permute-start.3 = (f32[5,2,8,128]{3,2,1,0:T(8,128)}, f32[5,2,8,128]{3,2,1,0:T(8,128)S(1)}, u32[]{:S(2)}, u32[]{:S(2)}) collective-permute-start(f32[5,2,8,128]{3,2,1,0:T(8,128)} %get-tuple-element.13), channel_id=1, source_target_pairs={{0,24},{8,16},{16,8},{24,0},{1,25},{9,17},{17,9},{25,1},{2,26},{10... | collective-permute-start | bytes 122888 | tf_op jit(solution)/shard_map/ppermute | solution.py:441
  16.3 10.9 %copy-start = (f32[4,5,2,8,128]{4,3,2,1,0:T(8,128)}, f32[4,5,2,8,128]{4,3,2,1,0:T(8,128)S(1)}, u32[]{:S(2)}) copy-start(f32[4,5,2,8,128]{4,3,2,1,0:T(8,128)S(1)} %pad_maximum_fusion.m_ref) | copy-start | bytes 491524
  16.3 7.5 %collective-permute-start.5 = (f32[4,5,2,8,128]{4,3,2,1,0:T(8,128)S(1)}, f32[4,5,2,8,128]{4,3,2,1,0:T(8,128)S(1)}, u32[]{:S(2)}, u32[]{:S(2)}) collective-permute-start(f32[4,5,2,8,128]{4,3,2,1,0:T(8,128)S(1)} %pad_maximum_fusion.m_ref), channel_id=1, source_target_pairs={{0,6},{2,0},{4,2},{6,4},{1,7},{3,1},{5,3},{7,5},{8,14},{10,8},{12,... | collective-permute-start | bytes 491528 | tf_op jit(solution)/shard_map/ppermute | solution.py:444
  20.0 7.3 %collective-permute-start.4 = (f32[4,5,2,8,128]{4,3,2,1,0:T(8,128)S(1)}, f32[4,5,2,8,128]{4,3,2,1,0:T(8,128)S(1)}, u32[]{:S(2)}, u32[]{:S(2)}) collective-permute-start(f32[4,5,2,8,128]{4,3,2,1,0:T(8,128)S(1)} %pad_maximum_fusion.m_ref), channel_id=1, source_target_pairs={{0,2},{2,4},{4,6},{6,0},{1,3},{3,5},{5,7},{7,1},{8,10},{10,12},{12... | collective-permute-start | bytes 491528 | tf_op jit(solution)/shard_map/ppermute | solution.py:443
  23.8 3.4 %copy-start.2 = (f32[4,5,2,8,128]{4,3,2,1,0:T(8,128)}, f32[4,5,2,8,128]{4,3,2,1,0:T(8,128)S(1)}, u32[]{:S(2)}) copy-start(f32[4,5,2,8,128]{4,3,2,1,0:T(8,128)S(1)} %collective-permute-done.5.a_ref) | copy-start | bytes 491524
  27.3 0.7 %copy-start.3 = (f32[4,5,2,8,128]{4,3,2,1,0:T(8,128)}, f32[4,5,2,8,128]{4,3,2,1,0:T(8,128)S(1)}, u32[]{:S(2)}) copy-start(f32[4,5,2,8,128]{4,3,2,1,0:T(8,128)S(1)} %collective-permute-done.4.b_ref) | copy-start | bytes 491524
  40.1 3.9 %collective-permute-start.6 = (f32[4,8,128]{2,1,0:T(8,128)}, f32[4,8,128]{2,1,0:T(8,128)S(1)}, u32[]{:S(2)}, u32[]{:S(2)}) collective-permute-start(f32[4,8,128]{2,1,0:T(8,128)} %get-tuple-element.15), channel_id=1, source_target_pairs={{0,8},{8,0},{16,24},{24,16},{1,9},{9,1},{17,25},{25,17},{2,10},{10... | collective-permute-start | bytes 49160 | tf_op jit(solution)/shard_map/ppermute | solution.py:448
  40.6 3.9 %collective-permute-start.7 = (f32[4,8,128]{2,1,0:T(8,128)}, f32[4,8,128]{2,1,0:T(8,128)S(1)}, u32[]{:S(2)}, u32[]{:S(2)}) collective-permute-start(f32[4,8,128]{2,1,0:T(8,128)} %get-tuple-element.16), channel_id=1, source_target_pairs={{0,16},{8,24},{16,0},{24,8},{1,17},{9,25},{17,1},{25,9},{2,18},{10... | collective-permute-start | bytes 49160 | tf_op jit(solution)/shard_map/ppermute | solution.py:448
  41.2 4.8 %collective-permute-start.8 = (f32[4,8,128]{2,1,0:T(8,128)}, f32[4,8,128]{2,1,0:T(8,128)S(1)}, u32[]{:S(2)}, u32[]{:S(2)}) collective-permute-start(f32[4,8,128]{2,1,0:T(8,128)} %get-tuple-element.17), channel_id=1, source_target_pairs={{0,24},{8,16},{16,8},{24,0},{1,25},{9,17},{17,9},{25,1},{2,26},{10... | collective-permute-start | bytes 49160 | tf_op jit(solution)/shard_map/ppermute | solution.py:448
  44.1 1.9 %copy-start.4 = (f32[4,8,128]{2,1,0:T(8,128)}, f32[4,8,128]{2,1,0:T(8,128)S(1)}, u32[]{:S(2)}) copy-start(f32[4,8,128]{2,1,0:T(8,128)S(1)} %collective-permute-done.6.refs_1_) | copy-start | bytes 49156
  44.6 1.4 %copy-start.5 = (f32[4,8,128]{2,1,0:T(8,128)}, f32[4,8,128]{2,1,0:T(8,128)S(1)}, u32[]{:S(2)}) copy-start(f32[4,8,128]{2,1,0:T(8,128)S(1)} %collective-permute-done.7.refs_2_) | copy-start | bytes 49156
  46.0 0.6 %copy-start.6 = (f32[4,8,128]{2,1,0:T(8,128)}, f32[4,8,128]{2,1,0:T(8,128)S(1)}, u32[]{:S(2)}) copy-start(f32[4,8,128]{2,1,0:T(8,128)S(1)} %collective-permute-done.8.refs_3_) | copy-start | bytes 49156

commit v2 on v1

--- a/solution.py
+++ b/solution.py
@@ -214,6 +214,26 @@
     return [pl.BlockSpec(memory_space=pltpu.VMEM)] * n
 
 
+def grant(words):
+    return pltpu.CompilerParams(vmem_limit_bytes=(words * 4 * 5) // 4 + (1 << 20))
+
+
+def join_slots(parts):
+    def body(*refs):
+        for n, ref in enumerate(refs[:-1]):
+            refs[-1][n] = ref[...]
+
+    block = parts[0].shape
+    return pl.pallas_call(
+        body,
+        name="join_slots",
+        out_shape=jax.ShapeDtypeStruct((len(parts),) + block, jnp.float32),
+        in_specs=vmem(len(parts)),
+        out_specs=vmem(1)[0],
+        compiler_params=grant(2 * len(parts) * math.prod(block)),
+    )(*parts)
+
+
 def gather_inputs(scatter, velocity, bubbles, walls):
     def body(s_ref, u_ref, b_ref, w_ref, out):
         out[0] = jnp.where(b_ref[...] == 1, VAPOUR, LIQUID) * s_ref[...]
@@ -227,6 +247,7 @@
         out_shape=jax.ShapeDtypeStruct((5,) + scatter.shape, jnp.float32),
         in_specs=vmem(4),
         out_specs=vmem(1)[0],
+        compiler_params=grant(11 * math.prod(scatter.shape)),
     )(scatter, velocity, bubbles, walls)
 
 
@@ -257,6 +278,7 @@
         out_shape=[jax.ShapeDtypeStruct((5, sh.own, sh.y, LANES), jnp.float32)] * sh.nx,
         in_specs=vmem(3),
         out_specs=vmem(sh.nx),
+        compiler_params=grant((15 + 20) * math.prod(values.shape)),
     )(values, before, after)
 
 
@@ -390,6 +412,12 @@
             pltpu.VMEM((rows, subs, LANES), jnp.float32),
             pltpu.VMEM((4, subs * sh.y, LANES), jnp.float32),
         ],
+        compiler_params=grant(
+            (2 * 19 + 2) * math.prod(populations.shape[1:])
+            + (5 * rows + 4 * sh.y) * subs * LANES
+            + 3 * math.prod(middle.shape)
+            + 4 * sh.nx * sh.y * LANES
+        ),
     )(below, middle, above)
 
 
@@ -422,6 +450,7 @@
         ],
         in_specs=vmem(sh.nx),
         out_specs=vmem(2),
+        compiler_params=grant(8 * sh.nx * sh.y * LANES + 8 * math.prod(block)),
     )(*pieces)
 
 
@@ -439,7 +468,7 @@
         got = [slabs[0]]
         for slot in range(1, sh.nx):
             got.append(lax.ppermute(slabs[slot], "gx", sh.perm(slot)))
-        middle = jnp.stack(got)
+        middle = join_slots(got)
         below = lax.ppermute(middle, "gy", ring(sh.ny, 1))
         above = lax.ppermute(middle, "gy", ring(sh.ny, -1))
         pieces = run_steps(below, middle, above, sh)

time: 48.5 us -> 43 us (0.89)
  Pallas kernels: 16.9 us -> 11.5 us
  local copies, waits for them, and re-layouts: 1.9 us -> 2.94 us
  other arithmetic: 0.79 us -> 0 us
  waiting for transfers between devices: 15.9 us -> 15.2 us
    pallas_call x1, Pallas kernels: 12.2 us -> 10.5 us  [run_steps(): pl.pallas_call(body, name='run_steps', out_shape=[jax.ShapeDtypeStruct((4...]
    pallas_call x1, Pallas kernels: 1.75 us -> 0.16 us  [cut_slabs(): pl.pallas_call(body, name='cut_slabs', out_shape=[jax.ShapeDtypeStruct((5...]
    pallas_call x1, Pallas kernels: 1.45 us -> 0.01 us  [gather_inputs(): pl.pallas_call(body, name='pack_inputs', out_shape=jax.ShapeDtypeStruct((...]
    unnamed x14 -> x8, local copies, waits for them, and re-layouts: 1.9 us -> 2.94 us
    another operation x1 -> x0, other arithmetic: 0.79 us -> none  [on_device(): middle = jnp.stack(got)]
    pallas_call x1, Pallas kernels: 1.55 us -> 0.78 us  [place_outputs(): pl.pallas_call(body, name='place_outputs', out_shape=[jax.ShapeDtypeStruc...]
where the time goes in v2:
time: 43 us; the launch traced here: 42.5 us
  waiting for transfers between devices  15.2 us (35%)
  starting transfers between devices  12.2 us (28%)
  Pallas kernels  11.5 us (27%)
  local copies, waits for them, and re-layouts  2.94 us (7%)
  between operations  0.67 us (2%)
    pallas_call x1, Pallas kernels, run_steps(): pl.pallas_call(body, name='run_steps', out_shape=[jax.ShapeDtypeStruct((4...  10.5 us
    ppermute x3, waiting for transfers between devices, on_device(): got.append(lax.ppermute(slabs[slot], 'gx', sh.perm(slot)))  4.88 us
    ppermute x3, starting transfers between devices, on_device(): got.append(lax.ppermute(slabs[slot], 'gx', sh.perm(slot)))  4.43 us
    ppermute x1, waiting for transfers between devices, on_device(): above = lax.ppermute(middle, 'gy', ring(sh.ny, -1))  3.82 us
    ppermute x1, starting transfers between devices, on_device(): above = lax.ppermute(middle, 'gy', ring(sh.ny, -1))  3.65 us
    ppermute x3, starting transfers between devices, on_device(): back.append(lax.ppermute(pieces[slot], 'gx', sh.perm(slot)))  3.55 us
    ppermute x1, waiting for transfers between devices, on_device(): below = lax.ppermute(middle, 'gy', ring(sh.ny, 1))  3.43 us
    unnamed x8, local copies, waits for them, and re-layouts  2.94 us
  transfers between devices with their start and end apart: 9, of which 9 were waited for; matrix products, arithmetic and copies ran while one was open for 0% of the time, Pallas kernels for 0%

profile of v2, /device:TPU:0, one launch (start us, length us, event | category | flops | bytes accessed | tf_op | source)
XLA Modules:
  0.0 42.5 jit_solution(4830806592987710218)
XLA Ops:
  0.6 0.8 %copy-done = f32[3,4,8,128]{3,2,1,0:T(8,128)S(1)} copy-done((f32[3,4,8,128]{3,2,1,0:T(8,128)S(1)}, f32[3,4,8,128]{3,2,1,0:T(8,128)}, u32[]{:S(2)}) %copy-start) | copy-done | bytes 49176
  1.4 0.7 %copy-done.1 = f32[4,8,128]{2,1,0:T(8,128)S(1)} copy-done((f32[4,8,128]{2,1,0:T(8,128)S(1)}, f32[4,8,128]{2,1,0:T(8,128)}, u32[]{:S(2)}) %copy-start.1) | copy-done | bytes 16408
  2.1 0.7 %copy-done.2 = s32[4,8,128]{2,1,0:T(8,128)S(1)} copy-done((s32[4,8,128]{2,1,0:T(8,128)S(1)}, s32[4,8,128]{2,1,0:T(8,128)}, u32[]{:S(2)}) %copy-start.2) | copy-done | bytes 16408
  2.9 0.7 %copy-done.3 = s32[4,8,128]{2,1,0:T(8,128)S(1)} copy-done((s32[4,8,128]{2,1,0:T(8,128)S(1)}, s32[4,8,128]{2,1,0:T(8,128)}, u32[]{:S(2)}) %copy-start.3) | copy-done | bytes 16408
  3.6 0.6 %collective-permute-start = (f32[5,4,8,128]{3,2,1,0:T(8,128)S(1)}, f32[5,4,8,128]{3,2,1,0:T(8,128)S(1)}, u32[]{:S(2)}, u32[]{:S(2)}) collective-permute-start(f32[5,4,8,128]{3,2,1,0:T(8,128)S(1)} %pack_inputs.1.v_ref), channel_id=1, source_target_pairs={{0,1},{1,0},{2,3},{3,2},{4,5},{5,4},{6,7},{7,6},{8,9},{9,8},{10,11... | collective-permute-start | bytes 245768 | tf_op jit(solution)/shard_map/ppermute | solution.py:465
  4.2 0.9 %collective-permute-done.b_ref.a_ref = f32[5,4,8,128]{3,2,1,0:T(8,128)S(1)} collective-permute-done((f32[5,4,8,128]{3,2,1,0:T(8,128)S(1)}, f32[5,4,8,128]{3,2,1,0:T(8,128)S(1)}, u32[]{:S(2)}, u32[]{:S(2)}) %collective-permute-start) | collective-permute-done | bytes 81952 | tf_op jit(solution)/shard_map/ppermute | solution.py:465
  5.1 0.2 cut_slabs.1
  5.2 2.9 %collective-permute-start.1 = (f32[5,2,8,128]{3,2,1,0:T(8,128)S(1)}, f32[5,2,8,128]{3,2,1,0:T(8,128)S(1)}, u32[]{:S(2)}, u32[]{:S(2)}) collective-permute-start(f32[5,2,8,128]{3,2,1,0:T(8,128)S(1)} %get-tuple-element.11), channel_id=1, source_target_pairs={{0,8},{8,0},{16,24},{24,16},{1,9},{9,1},{17,25},{25,17},{2,10},{10... | collective-permute-start | bytes 122888 | tf_op jit(solution)/shard_map/ppermute | solution.py:470
  8.1 1.5 %collective-permute-start.2 = (f32[5,2,8,128]{3,2,1,0:T(8,128)S(1)}, f32[5,2,8,128]{3,2,1,0:T(8,128)S(1)}, u32[]{:S(2)}, u32[]{:S(2)}) collective-permute-start(f32[5,2,8,128]{3,2,1,0:T(8,128)S(1)} %get-tuple-element.12), channel_id=1, source_target_pairs={{0,16},{8,24},{16,0},{24,8},{1,17},{9,25},{17,1},{25,9},{2,18},{10... | collective-permute-start | bytes 122888 | tf_op jit(solution)/shard_map/ppermute | solution.py:470
  9.7 0.0 collective-permute-start.3
  9.7 0.4 %collective-permute-done.1.refs_1_ = f32[5,2,8,128]{3,2,1,0:T(8,128)S(1)} collective-permute-done((f32[5,2,8,128]{3,2,1,0:T(8,128)S(1)}, f32[5,2,8,128]{3,2,1,0:T(8,128)S(1)}, u32[]{:S(2)}, u32[]{:S(2)}) %collective-permute-start.1) | collective-permute-done | bytes 40992 | tf_op jit(solution)/shard_map/ppermute | solution.py:470
  10.1 2.0 %collective-permute-done.2.refs_2_ = f32[5,2,8,128]{3,2,1,0:T(8,128)S(1)} collective-permute-done((f32[5,2,8,128]{3,2,1,0:T(8,128)S(1)}, f32[5,2,8,128]{3,2,1,0:T(8,128)S(1)}, u32[]{:S(2)}, u32[]{:S(2)}) %collective-permute-start.2) | collective-permute-done | bytes 40992 | tf_op jit(solution)/shard_map/ppermute | solution.py:470
  12.1 2.4 %collective-permute-done.3.refs_3_ = f32[5,2,8,128]{3,2,1,0:T(8,128)S(1)} collective-permute-done((f32[5,2,8,128]{3,2,1,0:T(8,128)S(1)}, f32[5,2,8,128]{3,2,1,0:T(8,128)S(1)}, u32[]{:S(2)}, u32[]{:S(2)}) %collective-permute-start.3) | collective-permute-done | bytes 40992 | tf_op jit(solution)/shard_map/ppermute | solution.py:470
  14.6 3.7 %collective-permute-start.5 = (f32[4,5,2,8,128]{4,3,2,1,0:T(8,128)S(1)}, f32[4,5,2,8,128]{4,3,2,1,0:T(8,128)S(1)}, u32[]{:S(2)}, u32[]{:S(2)}) collective-permute-start(f32[4,5,2,8,128]{4,3,2,1,0:T(8,128)S(1)} %join_slots.1.m_ref), channel_id=1, source_target_pairs={{0,6},{2,0},{4,2},{6,4},{1,7},{3,1},{5,3},{7,5},{8,14},{10,8},{12,... | collective-permute-start | bytes 491528 | tf_op jit(solution)/shard_map/ppermute | solution.py:473
  18.2 3.8 %collective-permute-done.5.a_ref = f32[4,5,2,8,128]{4,3,2,1,0:T(8,128)S(1)} collective-permute-done((f32[4,5,2,8,128]{4,3,2,1,0:T(8,128)S(1)}, f32[4,5,2,8,128]{4,3,2,1,0:T(8,128)S(1)}, u32[]{:S(2)}, u32[]{:S(2)}) %collective-permute-start.5) | collective-permute-done | bytes 163872 | tf_op jit(solution)/shard_map/ppermute | solution.py:473
  22.1 3.4 %collective-permute-done.4.b_ref = f32[4,5,2,8,128]{4,3,2,1,0:T(8,128)S(1)} collective-permute-done((f32[4,5,2,8,128]{4,3,2,1,0:T(8,128)S(1)}, f32[4,5,2,8,128]{4,3,2,1,0:T(8,128)S(1)}, u32[]{:S(2)}, u32[]{:S(2)}) %collective-permute-start.4) | collective-permute-done | bytes 163872 | tf_op jit(solution)/shard_map/ppermute | solution.py:472
  25.5 10.5 %run_steps.1 = (f32[4,8,128]{2,1,0:T(8,128)S(1)}, f32[4,8,128]{2,1,0:T(8,128)S(1)}, f32[4,8,128]{2,1,0:T(8,128)S(1)}, f32[4,8,128]{2,1,0:T(8,128)S(1)}) custom-call(f32[4,5,2,8,128]{4,3,2,1,0:T(8,128)S(1)} %collective-permute-done.4.b_ref, f32[4,5,2,8,128]{4,3,2,1,0:T(8,128)S(1)} %join_slots.1.m_ref, f32[4,5,2,8,128]{4,3,2,1,0:T(8,128)S(1)} %collective-permute-done.5.a_ref), custom_call_target="tpu_custom_call" | custom-call | tf_op jit(solution)/shard_map/run_steps/pallas_call | solution.py:401
  36.0 0.6 %collective-permute-start.6 = (f32[4,8,128]{2,1,0:T(8,128)S(1)}, f32[4,8,128]{2,1,0:T(8,128)S(1)}, u32[]{:S(2)}, u32[]{:S(2)}) collective-permute-start(f32[4,8,128]{2,1,0:T(8,128)S(1)} %get-tuple-element.15), channel_id=1, source_target_pairs={{0,8},{8,0},{16,24},{24,16},{1,9},{9,1},{17,25},{25,17},{2,10},{10... | collective-permute-start | bytes 49160 | tf_op jit(solution)/shard_map/ppermute | solution.py:477
  36.6 0.5 %collective-permute-start.7 = (f32[4,8,128]{2,1,0:T(8,128)S(1)}, f32[4,8,128]{2,1,0:T(8,128)S(1)}, u32[]{:S(2)}, u32[]{:S(2)}) collective-permute-start(f32[4,8,128]{2,1,0:T(8,128)S(1)} %get-tuple-element.16), channel_id=1, source_target_pairs={{0,16},{8,24},{16,0},{24,8},{1,17},{9,25},{17,1},{25,9},{2,18},{10... | collective-permute-start | bytes 49160 | tf_op jit(solution)/shard_map/ppermute | solution.py:477
  37.1 2.4 %collective-permute-start.8 = (f32[4,8,128]{2,1,0:T(8,128)S(1)}, f32[4,8,128]{2,1,0:T(8,128)S(1)}, u32[]{:S(2)}, u32[]{:S(2)}) collective-permute-start(f32[4,8,128]{2,1,0:T(8,128)S(1)} %get-tuple-element.17), channel_id=1, source_target_pairs={{0,24},{8,16},{16,8},{24,0},{1,25},{9,17},{17,9},{25,1},{2,26},{10... | collective-permute-start | bytes 49160 | tf_op jit(solution)/shard_map/ppermute | solution.py:477
  39.5 0.2 collective-permute-done.6.refs_1_
  39.8 0.5 %collective-permute-done.7.refs_2_ = f32[4,8,128]{2,1,0:T(8,128)S(1)} collective-permute-done((f32[4,8,128]{2,1,0:T(8,128)S(1)}, f32[4,8,128]{2,1,0:T(8,128)S(1)}, u32[]{:S(2)}, u32[]{:S(2)}) %collective-permute-start.7) | collective-permute-done | bytes 16416 | tf_op jit(solution)/shard_map/ppermute | solution.py:477
  40.3 1.4 %collective-permute-done.8.refs_3_ = f32[4,8,128]{2,1,0:T(8,128)S(1)} collective-permute-done((f32[4,8,128]{2,1,0:T(8,128)S(1)}, f32[4,8,128]{2,1,0:T(8,128)S(1)}, u32[]{:S(2)}, u32[]{:S(2)}) %collective-permute-start.8) | collective-permute-done | bytes 16416 | tf_op jit(solution)/shard_map/ppermute | solution.py:477
  41.7 0.8 %place_outputs.1 = (f32[4,8,128]{2,1,0:T(8,128)}, f32[3,4,8,128]{3,2,1,0:T(8,128)}) custom-call(f32[4,8,128]{2,1,0:T(8,128)S(1)} %get-tuple-element.14.refs_0_, f32[4,8,128]{2,1,0:T(8,128)S(1)} %collective-permute-done.6.refs_1_, f32[4,8,128]{2,1,0:T(8,128)S(1)} %collective-permute-done.7.refs_2_, f32[4,8,128]{2,1,0:T(8,128)S(1)} %collective-permute-done.8.refs_3_), custom_call_target="tpu_custom_call" | custom-call | tf_op jit(solution)/shard_map/place_outputs/pallas_call | solution.py:444
  (7 shorter events, 0.0 us)
Async XLA Ops:
  0.6 0.8 %copy-start = (f32[3,4,8,128]{3,2,1,0:T(8,128)S(1)}, f32[3,4,8,128]{3,2,1,0:T(8,128)}, u32[]{:S(2)}) copy-start(f32[3,4,8,128]{3,2,1,0:T(8,128)} %u_ref.1) | copy-start | bytes 147460
  1.4 0.7 %copy-start.1 = (f32[4,8,128]{2,1,0:T(8,128)S(1)}, f32[4,8,128]{2,1,0:T(8,128)}, u32[]{:S(2)}) copy-start(f32[4,8,128]{2,1,0:T(8,128)} %s_ref.1) | copy-start | bytes 49156
  2.1 0.7 %copy-start.2 = (s32[4,8,128]{2,1,0:T(8,128)S(1)}, s32[4,8,128]{2,1,0:T(8,128)}, u32[]{:S(2)}) copy-start(s32[4,8,128]{2,1,0:T(8,128)} %b_ref.1) | copy-start | bytes 49156
  2.9 0.7 %copy-start.3 = (s32[4,8,128]{2,1,0:T(8,128)S(1)}, s32[4,8,128]{2,1,0:T(8,128)}, u32[]{:S(2)}) copy-start(s32[4,8,128]{2,1,0:T(8,128)} %w_ref.1) | copy-start | bytes 49156
  3.6 1.5 %collective-permute-start = (f32[5,4,8,128]{3,2,1,0:T(8,128)S(1)}, f32[5,4,8,128]{3,2,1,0:T(8,128)S(1)}, u32[]{:S(2)}, u32[]{:S(2)}) collective-permute-start(f32[5,4,8,128]{3,2,1,0:T(8,128)S(1)} %pack_inputs.1.v_ref), channel_id=1, source_target_pairs={{0,1},{1,0},{2,3},{3,2},{4,5},{5,4},{6,7},{7,6},{8,9},{9,8},{10,11... | collective-permute-start | bytes 245768 | tf_op jit(solution)/shard_map/ppermute | solution.py:465
  5.2 4.9 %collective-permute-start.1 = (f32[5,2,8,128]{3,2,1,0:T(8,128)S(1)}, f32[5,2,8,128]{3,2,1,0:T(8,128)S(1)}, u32[]{:S(2)}, u32[]{:S(2)}) collective-permute-start(f32[5,2,8,128]{3,2,1,0:T(8,128)S(1)} %get-tuple-element.11), channel_id=1, source_target_pairs={{0,8},{8,0},{16,24},{24,16},{1,9},{9,1},{17,25},{25,17},{2,10},{10... | collective-permute-start | bytes 122888 | tf_op jit(solution)/shard_map/ppermute | solution.py:470
  8.1 4.0 %collective-permute-start.2 = (f32[5,2,8,128]{3,2,1,0:T(8,128)S(1)}, f32[5,2,8,128]{3,2,1,0:T(8,128)S(1)}, u32[]{:S(2)}, u32[]{:S(2)}) collective-permute-start(f32[5,2,8,128]{3,2,1,0:T(8,128)S(1)} %get-tuple-element.12), channel_id=1, source_target_pairs={{0,16},{8,24},{16,0},{24,8},{1,17},{9,25},{17,1},{25,9},{2,18},{10... | collective-permute-start | bytes 122888 | tf_op jit(solution)/shard_map/ppermute | solution.py:470
  9.7 4.9 %collective-permute-start.3 = (f32[5,2,8,128]{3,2,1,0:T(8,128)S(1)}, f32[5,2,8,128]{3,2,1,0:T(8,128)S(1)}, u32[]{:S(2)}, u32[]{:S(2)}) collective-permute-start(f32[5,2,8,128]{3,2,1,0:T(8,128)S(1)} %get-tuple-element.13), channel_id=1, source_target_pairs={{0,24},{8,16},{16,8},{24,0},{1,25},{9,17},{17,9},{25,1},{2,26},{10... | collective-permute-start | bytes 122888 | tf_op jit(solution)/shard_map/ppermute | solution.py:470
  14.6 7.5 %collective-permute-start.5 = (f32[4,5,2,8,128]{4,3,2,1,0:T(8,128)S(1)}, f32[4,5,2,8,128]{4,3,2,1,0:T(8,128)S(1)}, u32[]{:S(2)}, u32[]{:S(2)}) collective-permute-start(f32[4,5,2,8,128]{4,3,2,1,0:T(8,128)S(1)} %join_slots.1.m_ref), channel_id=1, source_target_pairs={{0,6},{2,0},{4,2},{6,4},{1,7},{3,1},{5,3},{7,5},{8,14},{10,8},{12,... | collective-permute-start | bytes 491528 | tf_op jit(solution)/shard_map/ppermute | solution.py:473
  18.2 7.3 %collective-permute-start.4 = (f32[4,5,2,8,128]{4,3,2,1,0:T(8,128)S(1)}, f32[4,5,2,8,128]{4,3,2,1,0:T(8,128)S(1)}, u32[]{:S(2)}, u32[]{:S(2)}) collective-permute-start(f32[4,5,2,8,128]{4,3,2,1,0:T(8,128)S(1)} %join_slots.1.m_ref), channel_id=1, source_target_pairs={{0,2},{2,4},{4,6},{6,0},{1,3},{3,5},{5,7},{7,1},{8,10},{10,12},{12... | collective-permute-start | bytes 491528 | tf_op jit(solution)/shard_map/ppermute | solution.py:472
  36.0 3.8 %collective-permute-start.6 = (f32[4,8,128]{2,1,0:T(8,128)S(1)}, f32[4,8,128]{2,1,0:T(8,128)S(1)}, u32[]{:S(2)}, u32[]{:S(2)}) collective-permute-start(f32[4,8,128]{2,1,0:T(8,128)S(1)} %get-tuple-element.15), channel_id=1, source_target_pairs={{0,8},{8,0},{16,24},{24,16},{1,9},{9,1},{17,25},{25,17},{2,10},{10... | collective-permute-start | bytes 49160 | tf_op jit(solution)/shard_map/ppermute | solution.py:477
  36.6 3.7 %collective-permute-start.7 = (f32[4,8,128]{2,1,0:T(8,128)S(1)}, f32[4,8,128]{2,1,0:T(8,128)S(1)}, u32[]{:S(2)}, u32[]{:S(2)}) collective-permute-start(f32[4,8,128]{2,1,0:T(8,128)S(1)} %get-tuple-element.16), channel_id=1, source_target_pairs={{0,16},{8,24},{16,0},{24,8},{1,17},{9,25},{17,1},{25,9},{2,18},{10... | collective-permute-start | bytes 49160 | tf_op jit(solution)/shard_map/ppermute | solution.py:477
  37.1 4.6 %collective-permute-start.8 = (f32[4,8,128]{2,1,0:T(8,128)S(1)}, f32[4,8,128]{2,1,0:T(8,128)S(1)}, u32[]{:S(2)}, u32[]{:S(2)}) collective-permute-start(f32[4,8,128]{2,1,0:T(8,128)S(1)} %get-tuple-element.17), channel_id=1, source_target_pairs={{0,24},{8,16},{16,8},{24,0},{1,25},{9,17},{17,9},{25,1},{2,26},{10... | collective-permute-start | bytes 49160 | tf_op jit(solution)/shard_map/ppermute | solution.py:477

commit v3 on v2

v3 whole, which is shorter than its diff:
```python
import math

import jax
import jax.numpy as jnp
import numpy as np
from jax import lax
from jax.experimental import pallas as pl
from jax.experimental.pallas import tpu as pltpu
from jax.sharding import PartitionSpec as P

STEPS = 4
HALO = 2 * STEPS
LANES = 128

START_ROWS = 12
WEIGH_ROWS = 12
PAD = 2
PIPELINE = False


C = np.array(
    [
        [0, 0, 0],
        [1, 0, 0],
        [-1, 0, 0],
        [0, 1, 0],
        [0, -1, 0],
        [0, 0, 1],
        [0, 0, -1],
        [1, 1, 0],
        [-1, -1, 0],
        [1, -1, 0],
        [-1, 1, 0],
        [1, 0, 1],
        [-1, 0, -1],
        [1, 0, -1],
        [-1, 0, 1],
        [0, 1, 1],
        [0, -1, -1],
        [0, 1, -1],
        [0, -1, 1],
    ]
)
WEIGHTS = [1.0 / 3.0] + [1.0 / 18.0] * 6 + [1.0 / 36.0] * 12
OPPOSITE = [0, 2, 1, 4, 3, 6, 5, 8, 7, 10, 9, 12, 11, 14, 13, 16, 15, 18, 17]
MIRROR = [int(np.flatnonzero((C == c * [1, -1, 1]).all(1))[0]) for c in C]
LIQUID = 0.28
VAPOUR = 0.06
WALL_POTENTIAL = 0.5
ATTRACTION = 1.0
TEMPERATURE = 0.06

KEEP_E = 1.0 - 1.19
KEEP_P = 1.0 - 1.4
KEEP_Q = 1.0 - 1.2
KEEP_N = 1.0 - 1.25
KEEP_M = 1.0 - 1.98


def equilibrium(rho, u):
    rest = 1.0 - 1.5 * (u[0] * u[0] + u[1] * u[1] + u[2] * u[2])
    rows = [(rho * WEIGHTS[0]) * rest]
    scaled = [None, rho * WEIGHTS[1], rho * WEIGHTS[7]]
    still = [None] + [w * rest for w in scaled[1:]]
    triple = [None] + [3.0 * w for w in scaled[1:]]
    for i in range(1, 19, 2):
        terms = [u[k] if C[i, k] > 0 else -u[k] for k in range(3) if C[i, k] != 0]
        n = len(terms)
        along = terms[0] if n == 1 else terms[0] + terms[1]
        odd = triple[n] * along
        even = still[n] + (1.5 * odd) * along
        rows += [even + odd, even - odd]
    return rows


def potential(rho, solid):
    square = rho * rho
    gap = 1.0 - rho
    pressure = (
        rho * TEMPERATURE * (1.0 + rho + square - square * rho) / (gap * gap * gap)
        - ATTRACTION * square
    )
    return jnp.where(solid, WALL_POTENTIAL, jnp.sqrt(6.0 * (rho * (1.0 / 3.0) - pressure)))


def times(c, value):
    c = float(np.float32(c))
    return value if c == 1.0 else -value if c == -1.0 else c * value


def moments(f):
    d = [None] + [f[i] - f[i + 1] for i in range(1, 19, 2)]
    jx = d[1] + ((d[4] + d[5]) + (d[6] + d[7]))
    jy = d[2] + ((d[4] - d[5]) + (d[8] + d[9]))
    jz = d[3] + ((d[6] - d[7]) + (d[8] - d[9]))
    return jx, jy, jz


def collide(f, force, solid):
    s = [None] + [f[i] + f[i + 1] for i in range(1, 19, 2)]
    d = [None] + [f[i] - f[i + 1] for i in range(1, 19, 2)]
    xy, xz, yz = s[4] + s[5], s[6] + s[7], s[8] + s[9]
    axes = s[1] + s[2] + s[3]
    diagonals = xy + xz + yz
    rho = f[0] + axes + diagonals
    p_xy, q_xy = d[4] + d[5], d[4] - d[5]
    p_xz, q_xz = d[6] + d[7], d[6] - d[7]
    p_yz, q_yz = d[8] + d[9], d[8] - d[9]
    j = [d[1] + (p_xy + p_xz), d[2] + (q_xy + p_yz), d[3] + (q_xz + q_yz)]
    inverse = 1.0 / rho
    u = [j[k] * inverse for k in range(3)]
    moved = [j[k] + force[k] for k in range(3)]
    v = [moved[k] * inverse for k in range(3)]
    uu = [j[k] * u[k] for k in range(3)]
    vv = [moved[k] * v[k] for k in range(3)]
    u2 = uu[0] + uu[1] + uu[2]
    v2 = vv[0] + vv[1] + vv[2]

    def isotropic(of_energy, of_epsilon):
        parts = (
            (1.0 / 19.0 - of_energy * (11.0 + 19.0 * KEEP_E) + of_epsilon * (3.0 + 9.0 * KEEP_P), rho),
            (of_energy * 19.0 * KEEP_E - of_epsilon * 16.0 * KEEP_P, axes),
            (of_energy * 38.0 * KEEP_E - of_epsilon * 11.0 * KEEP_P, diagonals),
            (of_energy * 19.0 - of_epsilon * 5.5, v2),
            (-of_energy * 19.0 * KEEP_E + of_epsilon * 5.5 * KEEP_P, u2),
        )
        return sum((c * value for c, value in parts[1:]), parts[0][0] * parts[0][1])

    even_axis = isotropic(-11.0 / 2394.0, -4.0 / 252.0)
    even_diag = isotropic(8.0 / 2394.0, 1.0 / 252.0)
    even_rest = rho - 6.0 * even_axis - 12.0 * even_diag

    def stress(a, b, at_v, at_u, scale):
        on_axis = (
            ((KEEP_N + 2.0 * KEEP_P) * scale) * a
            + ((KEEP_N - KEEP_P) * scale) * b
            + (1.5 * scale) * at_v
            - ((KEEP_N + 0.5 * KEEP_P) * scale) * at_u
        )
        half = 0.5 * scale
        on_diagonal = (
            ((2.0 * KEEP_N - 2.0 * KEEP_P) * half) * a
            + ((2.0 * KEEP_N + KEEP_P) * half) * b
            + (1.5 * half) * at_v
            - ((2.0 * KEEP_N - 0.5 * KEEP_P) * half) * at_u
        )
        return on_axis, on_diagonal

    h, g = stress(
        3.0 * s[1] - axes,
        diagonals - 3.0 * yz,
        3.0 * vv[0] - v2,
        3.0 * uu[0] - u2,
        1.0 / 36.0,
    )
    k, l = stress(s[2] - s[3], xy - xz, vv[1] - vv[2], uu[1] - uu[2], 1.0 / 12.0)

    quarter = [None, 0.25 * v[1], 0.25 * v[2]]

    def shear(a, b, pair):
        return (0.25 * KEEP_N) * (pair - j[a] * u[b]) + moved[a] * quarter[b]

    t_xy = shear(0, 1, s[4] - s[5])
    t_xz = shear(0, 2, s[6] - s[7])
    t_yz = shear(1, 2, s[8] - s[9])

    flux = [
        times(-5.0 * KEEP_Q, d[n + 1])
        + (times(KEEP_Q * 5.0 / 3.0 - 2.0 / 3.0, moved[n]) - (KEEP_Q * 5.0 / 3.0) * force[n])
        for n in range(3)
    ]
    tenth = [0.1 * moved[n] for n in range(3)]
    axis_odd = [tenth[n] - 0.1 * flux[n] for n in range(3)]
    diag_odd = [tenth[n] + 0.025 * flux[n] for n in range(3)]
    third = KEEP_M / 8.0
    mx, my, mz = third * (p_xy - p_xz), third * (p_yz - q_xy), third * (q_xz - q_yz)

    twist = even_axis - h
    evens = [even_axis + 2.0 * h, twist + k, twist - k]
    ring = even_diag + g
    e_xy, e_xz, e_yz = ring + l, ring - l, even_diag - 2.0 * g
    a, b = diag_odd[0] + mx, diag_odd[1] - my
    odd_xy = (a + b, a - b)
    a, b = diag_odd[0] - mx, diag_odd[2] + mz
    odd_xz = (a + b, a - b)
    a, b = diag_odd[1] + my, diag_odd[2] - mz
    odd_yz = (a + b, a - b)

    post = [even_rest]
    for n in range(3):
        post += [evens[n] + axis_odd[n], evens[n] - axis_odd[n]]
    for even, t, odd in ((e_xy, t_xy, odd_xy), (e_xz, t_xz, odd_xz), (e_yz, t_yz, odd_yz)):
        same, cross = even + t, even - t
        post += [same + odd[0], same - odd[0], cross + odd[1], cross - odd[1]]
    return [jnp.where(solid, f[OPPOSITE[i]], post[i]) for i in range(19)]


class Shape:
    def __init__(self, mesh, block):
        self.nx, self.ny, self.nz = (mesh.shape[a] for a in ("gx", "gy", "gz"))
        self.x, self.y, self.z = block
        self.slab = self.z // self.nx
        self.width = LANES // 2
        self.groups = 2
        self.own = self.x // self.groups
        self.subs = self.x * self.nx // self.groups
        self.rows = self.y + 2 * HALO
        assert self.z == LANES and self.slab * self.nx == self.z
        assert self.slab + 2 * HALO <= self.width and 2 * self.slab <= self.width
        assert self.y == HALO and self.own * self.groups == self.x
        assert self.subs % 8 == 0
        if self.nx & (self.nx - 1) == 0:
            self.peer = lambda k, slot: jnp.bitwise_xor(k, slot)
            self.perm = lambda slot: [(i, i ^ slot) for i in range(self.nx)]
            self.sender = self.peer
        else:
            self.peer = lambda k, slot: lax.rem(k + slot, self.nx)
            self.sender = lambda k, slot: lax.rem(k + self.nx - slot, self.nx)
            self.perm = lambda slot: [(i, (i + slot) % self.nx) for i in range(self.nx)]


def vmem(n):
    return [pl.BlockSpec(memory_space=pltpu.VMEM)] * n


def grant(words):
    return pltpu.CompilerParams(vmem_limit_bytes=(words * 4 * 5) // 4 + (1 << 20))


def join_slots(parts):
    def body(*refs):
        for n, ref in enumerate(refs[:-1]):
            refs[-1][n] = ref[...]

    block = parts[0].shape
    return pl.pallas_call(
        body,
        name="join_slots",
        out_shape=jax.ShapeDtypeStruct((len(parts),) + block, jnp.float32),
        in_specs=vmem(len(parts)),
        out_specs=vmem(1)[0],
        compiler_params=grant(2 * len(parts) * math.prod(block)),
    )(*parts)


def gather_inputs(scatter, velocity, bubbles, walls):
    rho = jnp.where(bubbles == 1, VAPOUR, LIQUID) * scatter
    solid = jnp.where(walls == 1, 1.0, 0.0)
    return jnp.concatenate([rho[None], velocity, solid[None]])


def cut_slabs(values, before, after, sh):
    def body(v_ref, b_ref, a_ref, *outs):
        k = lax.axis_index("gx")
        lane = lax.broadcasted_iota(jnp.int32, (sh.y, LANES), 1)
        group = lane // sh.width
        for slot, out in enumerate(outs):
            q = sh.peer(k, slot)
            low = (lane >= LANES - HALO) & (q == 0)
            high = (lane < HALO) & (q == sh.nx - 1)
            start = HALO - q * sh.slab + 2 * LANES
            for n in range(5):
                for m in range(sh.own):
                    merged = None
                    for g in range(sh.groups):
                        x = m * sh.groups + g
                        plane = jnp.where(low, b_ref[n, x], v_ref[n, x])
                        plane = jnp.where(high, a_ref[n, x], plane)
                        plane = pltpu.roll(plane, lax.rem(start + g * sh.width, LANES), 1)
                        merged = plane if g == 0 else jnp.where(group == g, plane, merged)
                    out[n, m] = merged

    return pl.pallas_call(
        body,
        name="cut_slabs",
        out_shape=[jax.ShapeDtypeStruct((5, sh.own, sh.y, LANES), jnp.float32)] * sh.nx,
        in_specs=vmem(3),
        out_specs=vmem(sh.nx),
        compiler_params=grant((15 + 20) * math.prod(values.shape)),
    )(values, before, after)


def run_steps(below, middle, above, sh):
    half, subs = sh.rows // 2, sh.subs
    last = PAD + half - 1

    def body(b_ref, m_ref, a_ref, *rest):
        outs = rest[: sh.nx]
        raw, first, second, psi_ref, solid_ref, force_ref, post_ref, done = rest[sh.nx :]
        k = lax.axis_index("gx")
        lane = lax.broadcasted_iota(jnp.int32, (subs, LANES), 1)
        low = lane < sh.width

        for slot in range(sh.nx):
            base = sh.sender(k, slot) * (sh.own * sh.rows)
            for part, ref in enumerate((b_ref, m_ref, a_ref)):
                for n in range(5):
                    for m in range(sh.own):
                        at = pl.multiple_of(base + m * sh.rows + part * sh.y, 8)
                        raw[n, pl.ds(at, sh.y), :] = ref[slot, n, m]

        def along_x(pair, cx):
            if cx == 1:
                return pltpu.roll(pair[1], 1, 0), pair[0]
            if cx == -1:
                return pair[1], pltpu.roll(pair[0], subs - 1, 0)
            return pair

        def along_z(value, cz):
            return pltpu.roll(value, cz % LANES, 1) if cz % LANES else value

        def over(count, at_once, step):
            at_once = min(at_once, count)
            while count % at_once:
                at_once -= 1

            def trip(n, _):
                for r in range(at_once):
                    step(n * at_once + r)
                return 0

            if count == at_once:
                trip(0, 0)
            else:
                lax.fori_loop(0, count // at_once, trip, 0)

        def weigh(f, y, p):
            psi_ref[p, y] = potential(sum(f[1:], f[0]), solid_ref[p, y] > 0.5)

        def reflect():
            for p in range(2):
                psi_ref[p, last + 1] = pltpu.roll(psi_ref[p, last], sh.width, 1)

        def start(n):
            y = PAD + n
            pairs = []
            for v in range(5):
                near = raw[v, pl.ds(n, subs, stride=sh.rows), :]
                far = raw[v, pl.ds(sh.rows - 1 - n, subs, stride=sh.rows), :]
                far = -far if v == 2 else far
                even = jnp.where(low, near, pltpu.roll(far, sh.width, 1))
                odd = jnp.where(low, pltpu.roll(near, sh.width, 1), far)
                pairs.append((even, odd))
            for p in range(2):
                rho, ux, uy, uz, solid = (pair[p] for pair in pairs)
                f = equilibrium(rho, [ux, uy, uz])
                solid_ref[p, y] = solid
                for i in range(19):
                    first[i, p, y] = f[i]
                weigh(f, y, p)

        over(half, START_ROWS, start)

        source, target = first, second
        for step in range(STEPS):
            lo = PAD + 2 * step
            if step > 0:

                def weigh_again(n, source=source, lo=lo):
                    for p in range(2):
                        weigh([source[i, p, lo + n] for i in range(19)], lo + n, p)

                over(half - 2 * step, WEIGH_ROWS, weigh_again)
            reflect()

            def push(y):
                here, up, down = (
                    [psi_ref[p, at] for p in range(2)] for at in (y, y + 1, y - 1)
                )
                rise = [up[p] - down[p] for p in range(2)]
                doubled = [2.0 * here[p] + (up[p] + down[p]) for p in range(2)]
                before, after = along_x(here, 1), along_x(here, -1)
                rise_x = [a + b for a, b in zip(along_x(rise, 1), along_x(rise, -1))]
                z_sum = [
                    doubled[p] + (along_z(here[p], 1) + along_z(here[p], -1)) for p in range(2)
                ]
                x_sum = [doubled[p] + (before[p] + after[p]) for p in range(2)]
                fx = [a - b for a, b in zip(along_x(z_sum, -1), along_x(z_sum, 1))]
                for p in range(2):
                    fy = (2.0 * rise[p] + rise_x[p]) + (
                        along_z(rise[p], 1) + along_z(rise[p], -1)
                    )
                    fz = along_z(x_sum[p], -1) - along_z(x_sum[p], 1)
                    scale = here[p] * (1.0 / 36.0)
                    for n, value in enumerate((fx[p], fy, fz)):
                        force_ref[n, p, y] = scale * value

            def stream(posts, y, at_end, target=target):
                for i in range(19):
                    cx, cy, cz = (int(c) for c in C[i])
                    to, row = i, y + cy
                    if at_end and cy == 1:
                        to, row, cz = MIRROR[i], y, cz + sh.width
                    for p, value in enumerate(along_x(posts[i], cx)):
                        target[to, p, row] = along_z(value, cz)

            def settle(y, p, forces, source=source):
                f = [source[i, p, y] for i in range(19)]
                return collide(f, forces, solid_ref[p, y] > 0.5)

            def load_forces(y):
                return [[force_ref[n, p, y] for n in range(3)] for p in range(2)]

            def load_posts():
                return [[post_ref[i, p] for p in range(2)] for i in range(19)]

            rows = half - 1 - 2 * step
            if PIPELINE:

                def advance(n, _, lo=lo, push=push, stream=stream, settle=settle):
                    y = lo + 1 + n
                    forces = load_forces(y)
                    stream(load_posts(), y - 1, False)
                    push(y + 1)
                    for p in range(2):
                        post = settle(y, p, forces[p])
                        for i in range(19):
                            post_ref[i, p] = post[i]
                    return 0

                push(lo + 1)
                lax.fori_loop(0, rows, advance, 0)
                stream(load_posts(), last, True)
            else:

                def advance(n, _, lo=lo, push=push, stream=stream, settle=settle):
                    y = lo + 1 + n
                    forces = load_forces(y)
                    push(y + 1)
                    both = [settle(y, p, forces[p]) for p in range(2)]
                    stream(list(zip(*both)), y, False)
                    return 0

                push(lo + 1)
                lax.fori_loop(0, rows - 1, advance, 0)
                forces = load_forces(last)
                both = [settle(last, p, forces[p]) for p in range(2)]
                stream(list(zip(*both)), last, True)
            source, target = target, source

        quarter = sh.y // 2
        for n in range(quarter):
            y = PAD + HALO + n
            for p in range(2):
                f = [source[i, p, y] for i in range(19)]
                rho = sum(f[1:], f[0])
                fluid = solid_ref[p, y] < 0.5
                jx, jy, jz = moments(f)
                inverse = math.sqrt(3.0) / rho
                results = [rho * (1.0 / LIQUID), jx * inverse, jy * inverse, jz * inverse]
                for v, value in enumerate(results):
                    value = jnp.where(fluid, value, 0.0)
                    done[0, v, p, pl.ds(n, subs, stride=quarter), :] = value
                    value = -value if v == 2 else value
                    done[1, v, p, pl.ds(quarter - 1 - n, subs, stride=quarter), :] = value

        size = sh.own * quarter
        lane = lax.broadcasted_iota(jnp.int32, (size, LANES), 1)
        high = lane >= sh.width
        odd = (lane % sh.width) >= sh.slab
        for slot, out in enumerate(outs):
            at = pl.ds(pl.multiple_of(sh.peer(k, slot) * size, size), size)
            for v in range(4):
                even_odd = [
                    jnp.where(high, done[1, v, p, at, :], done[0, v, p, at, :]) for p in range(2)
                ]
                out[v] = jnp.where(
                    odd,
                    along_z(even_odd[1], sh.slab - HALO),
                    along_z(even_odd[0], -HALO),
                )

    padded = half + 2 * PAD
    row = (2, padded, subs, LANES)
    scratch = [
        (5, subs * sh.rows, LANES),
        (19,) + row,
        (19,) + row,
        row,
        row,
        (3,) + row,
        (19, 2, subs, LANES),
        (2, 4, 2, subs * sh.y // 2, LANES),
    ]
    piece = (4, sh.own * sh.y // 2, LANES)
    words = sum(math.prod(shape) for shape in scratch)
    return pl.pallas_call(
        body,
        name="run_steps",
        out_shape=[jax.ShapeDtypeStruct(piece, jnp.float32)] * sh.nx,
        in_specs=vmem(3),
        out_specs=vmem(sh.nx),
        scratch_shapes=[pltpu.VMEM(shape, jnp.float32) for shape in scratch],
        compiler_params=grant(words + 3 * math.prod(middle.shape) + sh.nx * math.prod(piece)),
    )(below, middle, above)


def place_outputs(pieces, sh):
    quarter = sh.y // 2
    size = sh.own * quarter

    def body(*refs):
        ins, (density, velocity) = refs[: sh.nx], refs[sh.nx :]
        k = lax.axis_index("gx")
        place = lax.broadcasted_iota(jnp.int32, (size, LANES), 1) // sh.slab
        upper = lax.broadcasted_iota(jnp.int32, (sh.y, LANES), 0) < quarter
        for v in range(4):
            for p in range(2):
                halves = []
                for g in range(2):
                    merged = None
                    for slot, ref in enumerate(ins):
                        q = sh.sender(k, slot)
                        turn = q * sh.slab - g * sh.width - p * sh.slab + 2 * LANES
                        value = pltpu.roll(ref[v], lax.rem(turn, LANES), 1)
                        merged = value if slot == 0 else jnp.where(place == q, value, merged)
                    halves.append(merged)
                for m in range(sh.own):
                    to = density.at[2 * m + p] if v == 0 else velocity.at[v - 1, 2 * m + p]
                    for g in range(2):
                        to[g * quarter : (g + 1) * quarter, :] = halves[g][
                            m * quarter : (m + 1) * quarter
                        ]

    block = (sh.x, sh.y, sh.z)
    return pl.pallas_call(
        body,
        name="place_outputs",
        out_shape=[
            jax.ShapeDtypeStruct(block, jnp.float32),
            jax.ShapeDtypeStruct((3,) + block, jnp.float32),
        ],
        in_specs=vmem(sh.nx),
        out_specs=vmem(2),
        compiler_params=grant(8 * sh.nx * sh.y * LANES + 8 * math.prod(block)),
    )(*pieces)


def ring(size, step):
    return [(i, (i + step) % size) for i in range(size)]


def solution(mesh):
    def on_device(density_scatter, initial_velocity, bubble_mask, wall_flags):
        sh = Shape(mesh, wall_flags.shape)
        values = gather_inputs(density_scatter, initial_velocity, bubble_mask, wall_flags)
        before = lax.ppermute(values, "gz", ring(sh.nz, 1))
        after = before if sh.nz == 2 else lax.ppermute(values, "gz", ring(sh.nz, -1))
        slabs = cut_slabs(values, before, after, sh)
        got = [slabs[0]]
        for slot in range(1, sh.nx):
            got.append(lax.ppermute(slabs[slot], "gx", sh.perm(slot)))
        middle = join_slots(got)
        below = lax.ppermute(middle, "gy", ring(sh.ny, 1))
        above = lax.ppermute(middle, "gy", ring(sh.ny, -1))
        pieces = run_steps(below, middle, above, sh)
        back = [pieces[0]]
        for slot in range(1, sh.nx):
            back.append(lax.ppermute(pieces[slot], "gx", sh.perm(slot)))
        return tuple(place_outputs(back, sh))

    in_specs = (
        P("gx", "gy", "gz"),
        P(None, "gx", "gy", "gz"),
        P("gx", "gy", "gz"),
        P("gx", "gy", "gz"),
    )
    out_specs = (P("gx", "gy", "gz"), P(None, "gx", "gy", "gz"))
    return jax.shard_map(
        on_device, mesh=mesh, in_specs=in_specs, out_specs=out_specs, check_vma=False
    )
```

time: 43 us -> 35.9 us (0.83)
  Pallas kernels: 11.5 us -> 6.83 us
  local copies, waits for them, and re-layouts: 2.94 us -> 0.02 us
  other arithmetic: 0 us -> 0.78 us
    pallas_call x2 -> x1, Pallas kernels: 10.5 us -> 5.88 us  [run_steps(): pl.pallas_call(body, name='run_steps', out_shape=[jax.ShapeDtypeStruct(pi...]
    unnamed x8 -> x2, local copies, waits for them, and re-layouts: 2.94 us -> 0.02 us
    broadcast_in_dim x0 -> x1, other arithmetic: none -> 0.77 us  [gather_inputs(): return jnp.concatenate([rho[None], velocity, solid[None]])]
where the time goes in v3:
time: 35.9 us; the launch traced here: 35.7 us
  waiting for transfers between devices  15.2 us (42%)
  starting transfers between devices  12.2 us (34%)
  Pallas kernels  6.83 us (19%)
  other arithmetic  0.78 us (2%)
  between operations  0.67 us (2%)
    pallas_call x1, Pallas kernels, run_steps(): pl.pallas_call(body, name='run_steps', out_shape=[jax.ShapeDtypeStruct(pi...  5.88 us
    ppermute x3, waiting for transfers between devices, on_device(): got.append(lax.ppermute(slabs[slot], 'gx', sh.perm(slot)))  4.88 us
    ppermute x3, starting transfers between devices, on_device(): got.append(lax.ppermute(slabs[slot], 'gx', sh.perm(slot)))  4.43 us
    ppermute x1, waiting for transfers between devices, on_device(): above = lax.ppermute(middle, 'gy', ring(sh.ny, -1))  3.82 us
    ppermute x1, starting transfers between devices, on_device(): above = lax.ppermute(middle, 'gy', ring(sh.ny, -1))  3.65 us
    ppermute x3, starting transfers between devices, on_device(): back.append(lax.ppermute(pieces[slot], 'gx', sh.perm(slot)))  3.55 us
    ppermute x1, waiting for transfers between devices, on_device(): below = lax.ppermute(middle, 'gy', ring(sh.ny, 1))  3.43 us
    ppermute x3, waiting for transfers between devices, on_device(): back.append(lax.ppermute(pieces[slot], 'gx', sh.perm(slot)))  2.19 us
  transfers between devices with their start and end apart: 9, of which 9 were waited for; matrix products, arithmetic and copies ran while one was open for 0% of the time, Pallas kernels for 0%

profile of v3, /device:TPU:0, one launch (start us, length us, event | category | flops | bytes accessed | tf_op | source)
XLA Modules:
  0.0 35.7 jit_solution(1739314955185577047)
XLA Ops:
  0.6 0.0 copy-start
  0.6 0.8 %select_bitcast_fusion = (f32[1,4,8,128]{3,2,1,0:T(8,128)S(1)}, f32[1,4,8,128]{3,2,1,0:T(8,128)S(1)}) fusion(s32[4,8,128]{2,1,0:T(8,128)} %param.7, f32[4,8,128]{2,1,0:T(8,128)} %param.4, s32[4,8,128]{2,1,0:T(8,128)} %param.6), kind=kLoop, calls=%fused_computation.1 | loop fusion | flops 20480 | bytes 81920 | tf_op jit(solution)/shard_map/broadcast_in_dim | solution.py:249
  1.4 0.0 copy-done
  1.4 0.5 %collective-permute-start = (f32[5,4,8,128]{3,2,1,0:T(8,128)S(1)}, f32[5,4,8,128]{3,2,1,0:T(8,128)S(1)}, u32[]{:S(2)}, u32[]{:S(2)}) collective-permute-start(f32[5,4,8,128]{3,2,1,0:T(8,128)S(1)} %pad_maximum_fusion.v_ref), channel_id=1, source_target_pairs={{0,1},{1,0},{2,3},{3,2},{4,5},{5,4},{6,7},{7,6},{8,9},{9,8},{10,11... | collective-permute-start | bytes 245768 | tf_op jit(solution)/shard_map/ppermute | solution.py:547
  2.0 0.9 %collective-permute-done.b_ref.a_ref = f32[5,4,8,128]{3,2,1,0:T(8,128)S(1)} collective-permute-done((f32[5,4,8,128]{3,2,1,0:T(8,128)S(1)}, f32[5,4,8,128]{3,2,1,0:T(8,128)S(1)}, u32[]{:S(2)}, u32[]{:S(2)}) %collective-permute-start) | collective-permute-done | bytes 81952 | tf_op jit(solution)/shard_map/ppermute | solution.py:547
  2.9 0.2 cut_slabs.1
  3.1 2.9 %collective-permute-start.1 = (f32[5,2,8,128]{3,2,1,0:T(8,128)S(1)}, f32[5,2,8,128]{3,2,1,0:T(8,128)S(1)}, u32[]{:S(2)}, u32[]{:S(2)}) collective-permute-start(f32[5,2,8,128]{3,2,1,0:T(8,128)S(1)} %get-tuple-element.11), channel_id=1, source_target_pairs={{0,8},{8,0},{16,24},{24,16},{1,9},{9,1},{17,25},{25,17},{2,10},{10... | collective-permute-start | bytes 122888 | tf_op jit(solution)/shard_map/ppermute | solution.py:552
  6.0 1.5 %collective-permute-start.2 = (f32[5,2,8,128]{3,2,1,0:T(8,128)S(1)}, f32[5,2,8,128]{3,2,1,0:T(8,128)S(1)}, u32[]{:S(2)}, u32[]{:S(2)}) collective-permute-start(f32[5,2,8,128]{3,2,1,0:T(8,128)S(1)} %get-tuple-element.12), channel_id=1, source_target_pairs={{0,16},{8,24},{16,0},{24,8},{1,17},{9,25},{17,1},{25,9},{2,18},{10... | collective-permute-start | bytes 122888 | tf_op jit(solution)/shard_map/ppermute | solution.py:552
  7.5 0.0 collective-permute-start.3
  7.5 0.4 %collective-permute-done.1.refs_1_ = f32[5,2,8,128]{3,2,1,0:T(8,128)S(1)} collective-permute-done((f32[5,2,8,128]{3,2,1,0:T(8,128)S(1)}, f32[5,2,8,128]{3,2,1,0:T(8,128)S(1)}, u32[]{:S(2)}, u32[]{:S(2)}) %collective-permute-start.1) | collective-permute-done | bytes 40992 | tf_op jit(solution)/shard_map/ppermute | solution.py:552
  8.0 2.0 %collective-permute-done.2.refs_2_ = f32[5,2,8,128]{3,2,1,0:T(8,128)S(1)} collective-permute-done((f32[5,2,8,128]{3,2,1,0:T(8,128)S(1)}, f32[5,2,8,128]{3,2,1,0:T(8,128)S(1)}, u32[]{:S(2)}, u32[]{:S(2)}) %collective-permute-start.2) | collective-permute-done | bytes 40992 | tf_op jit(solution)/shard_map/ppermute | solution.py:552
  10.0 2.4 %collective-permute-done.3.refs_3_ = f32[5,2,8,128]{3,2,1,0:T(8,128)S(1)} collective-permute-done((f32[5,2,8,128]{3,2,1,0:T(8,128)S(1)}, f32[5,2,8,128]{3,2,1,0:T(8,128)S(1)}, u32[]{:S(2)}, u32[]{:S(2)}) %collective-permute-start.3) | collective-permute-done | bytes 40992 | tf_op jit(solution)/shard_map/ppermute | solution.py:552
  12.4 3.7 %collective-permute-start.5 = (f32[4,5,2,8,128]{4,3,2,1,0:T(8,128)S(1)}, f32[4,5,2,8,128]{4,3,2,1,0:T(8,128)S(1)}, u32[]{:S(2)}, u32[]{:S(2)}) collective-permute-start(f32[4,5,2,8,128]{4,3,2,1,0:T(8,128)S(1)} %join_slots.1.m_ref), channel_id=1, source_target_pairs={{0,6},{2,0},{4,2},{6,4},{1,7},{3,1},{5,3},{7,5},{8,14},{10,8},{12,... | collective-permute-start | bytes 491528 | tf_op jit(solution)/shard_map/ppermute | solution.py:555
  16.1 0.0 collective-permute-start.4
  16.1 3.8 %collective-permute-done.5.a_ref = f32[4,5,2,8,128]{4,3,2,1,0:T(8,128)S(1)} collective-permute-done((f32[4,5,2,8,128]{4,3,2,1,0:T(8,128)S(1)}, f32[4,5,2,8,128]{4,3,2,1,0:T(8,128)S(1)}, u32[]{:S(2)}, u32[]{:S(2)}) %collective-permute-start.5) | collective-permute-done | bytes 163872 | tf_op jit(solution)/shard_map/ppermute | solution.py:555
  19.9 3.4 %collective-permute-done.4.b_ref = f32[4,5,2,8,128]{4,3,2,1,0:T(8,128)S(1)} collective-permute-done((f32[4,5,2,8,128]{4,3,2,1,0:T(8,128)S(1)}, f32[4,5,2,8,128]{4,3,2,1,0:T(8,128)S(1)}, u32[]{:S(2)}, u32[]{:S(2)}) %collective-permute-start.4) | collective-permute-done | bytes 163872 | tf_op jit(solution)/shard_map/ppermute | solution.py:554
  23.3 5.9 %run_steps.1 = (f32[4,8,128]{2,1,0:T(8,128)S(1)}, f32[4,8,128]{2,1,0:T(8,128)S(1)}, f32[4,8,128]{2,1,0:T(8,128)S(1)}, f32[4,8,128]{2,1,0:T(8,128)S(1)}) custom-call(f32[4,5,2,8,128]{4,3,2,1,0:T(8,128)S(1)} %collective-permute-done.4.b_ref, f32[4,5,2,8,128]{4,3,2,1,0:T(8,128)S(1)} %join_slots.1.m_ref, f32[4,5,2,8,128]{4,3,2,1,0:T(8,128)S(1)} %collective-permute-done.5.a_ref), custom_call_target="tpu_custom_call" | custom-call | tf_op jit(solution)/shard_map/run_steps/pallas_call | solution.py:487
  29.2 0.6 %collective-permute-start.6 = (f32[4,8,128]{2,1,0:T(8,128)S(1)}, f32[4,8,128]{2,1,0:T(8,128)S(1)}, u32[]{:S(2)}, u32[]{:S(2)}) collective-permute-start(f32[4,8,128]{2,1,0:T(8,128)S(1)} %get-tuple-element.15), channel_id=1, source_target_pairs={{0,8},{8,0},{16,24},{24,16},{1,9},{9,1},{17,25},{25,17},{2,10},{10... | collective-permute-start | bytes 49160 | tf_op jit(solution)/shard_map/ppermute | solution.py:559
  29.8 0.5 %collective-permute-start.7 = (f32[4,8,128]{2,1,0:T(8,128)S(1)}, f32[4,8,128]{2,1,0:T(8,128)S(1)}, u32[]{:S(2)}, u32[]{:S(2)}) collective-permute-start(f32[4,8,128]{2,1,0:T(8,128)S(1)} %get-tuple-element.16), channel_id=1, source_target_pairs={{0,16},{8,24},{16,0},{24,8},{1,17},{9,25},{17,1},{25,9},{2,18},{10... | collective-permute-start | bytes 49160 | tf_op jit(solution)/shard_map/ppermute | solution.py:559
  30.3 2.4 %collective-permute-start.8 = (f32[4,8,128]{2,1,0:T(8,128)S(1)}, f32[4,8,128]{2,1,0:T(8,128)S(1)}, u32[]{:S(2)}, u32[]{:S(2)}) collective-permute-start(f32[4,8,128]{2,1,0:T(8,128)S(1)} %get-tuple-element.17), channel_id=1, source_target_pairs={{0,24},{8,16},{16,8},{24,0},{1,25},{9,17},{17,9},{25,1},{2,26},{10... | collective-permute-start | bytes 49160 | tf_op jit(solution)/shard_map/ppermute | solution.py:559
  32.8 0.2 collective-permute-done.6.refs_1_
  33.0 0.5 %collective-permute-done.7.refs_2_ = f32[4,8,128]{2,1,0:T(8,128)S(1)} collective-permute-done((f32[4,8,128]{2,1,0:T(8,128)S(1)}, f32[4,8,128]{2,1,0:T(8,128)S(1)}, u32[]{:S(2)}, u32[]{:S(2)}) %collective-permute-start.7) | collective-permute-done | bytes 16416 | tf_op jit(solution)/shard_map/ppermute | solution.py:559
  33.5 1.4 %collective-permute-done.8.refs_3_ = f32[4,8,128]{2,1,0:T(8,128)S(1)} collective-permute-done((f32[4,8,128]{2,1,0:T(8,128)S(1)}, f32[4,8,128]{2,1,0:T(8,128)S(1)}, u32[]{:S(2)}, u32[]{:S(2)}) %collective-permute-start.8) | collective-permute-done | bytes 16416 | tf_op jit(solution)/shard_map/ppermute | solution.py:559
  35.0 0.8 %place_outputs.1 = (f32[4,8,128]{2,1,0:T(8,128)}, f32[3,4,8,128]{3,2,1,0:T(8,128)}) custom-call(f32[4,8,128]{2,1,0:T(8,128)S(1)} %get-tuple-element.14.refs_0_, f32[4,8,128]{2,1,0:T(8,128)S(1)} %collective-permute-done.6.refs_1_, f32[4,8,128]{2,1,0:T(8,128)S(1)} %collective-permute-done.7.refs_2_, f32[4,8,128]{2,1,0:T(8,128)S(1)} %collective-permute-done.8.refs_3_), custom_call_target="tpu_custom_call" | custom-call | tf_op jit(solution)/shard_map/place_outputs/pallas_call | solution.py:526
  (2 shorter events, 0.0 us)
Async XLA Ops:
  0.6 0.8 %copy-start = (f32[3,4,8,128]{3,2,1,0:T(8,128)S(1)}, f32[3,4,8,128]{3,2,1,0:T(8,128)}, u32[]{:S(2)}) copy-start(f32[3,4,8,128]{3,2,1,0:T(8,128)} %param.5) | copy-start | bytes 147460
  1.4 1.5 %collective-permute-start = (f32[5,4,8,128]{3,2,1,0:T(8,128)S(1)}, f32[5,4,8,128]{3,2,1,0:T(8,128)S(1)}, u32[]{:S(2)}, u32[]{:S(2)}) collective-permute-start(f32[5,4,8,128]{3,2,1,0:T(8,128)S(1)} %pad_maximum_fusion.v_ref), channel_id=1, source_target_pairs={{0,1},{1,0},{2,3},{3,2},{4,5},{5,4},{6,7},{7,6},{8,9},{9,8},{10,11... | collective-permute-start | bytes 245768 | tf_op jit(solution)/shard_map/ppermute | solution.py:547
  3.1 4.9 %collective-permute-start.1 = (f32[5,2,8,128]{3,2,1,0:T(8,128)S(1)}, f32[5,2,8,128]{3,2,1,0:T(8,128)S(1)}, u32[]{:S(2)}, u32[]{:S(2)}) collective-permute-start(f32[5,2,8,128]{3,2,1,0:T(8,128)S(1)} %get-tuple-element.11), channel_id=1, source_target_pairs={{0,8},{8,0},{16,24},{24,16},{1,9},{9,1},{17,25},{25,17},{2,10},{10... | collective-permute-start | bytes 122888 | tf_op jit(solution)/shard_map/ppermute | solution.py:552
  6.0 4.0 %collective-permute-start.2 = (f32[5,2,8,128]{3,2,1,0:T(8,128)S(1)}, f32[5,2,8,128]{3,2,1,0:T(8,128)S(1)}, u32[]{:S(2)}, u32[]{:S(2)}) collective-permute-start(f32[5,2,8,128]{3,2,1,0:T(8,128)S(1)} %get-tuple-element.12), channel_id=1, source_target_pairs={{0,16},{8,24},{16,0},{24,8},{1,17},{9,25},{17,1},{25,9},{2,18},{10... | collective-permute-start | bytes 122888 | tf_op jit(solution)/shard_map/ppermute | solution.py:552
  7.5 4.9 %collective-permute-start.3 = (f32[5,2,8,128]{3,2,1,0:T(8,128)S(1)}, f32[5,2,8,128]{3,2,1,0:T(8,128)S(1)}, u32[]{:S(2)}, u32[]{:S(2)}) collective-permute-start(f32[5,2,8,128]{3,2,1,0:T(8,128)S(1)} %get-tuple-element.13), channel_id=1, source_target_pairs={{0,24},{8,16},{16,8},{24,0},{1,25},{9,17},{17,9},{25,1},{2,26},{10... | collective-permute-start | bytes 122888 | tf_op jit(solution)/shard_map/ppermute | solution.py:552
  12.4 7.5 %collective-permute-start.5 = (f32[4,5,2,8,128]{4,3,2,1,0:T(8,128)S(1)}, f32[4,5,2,8,128]{4,3,2,1,0:T(8,128)S(1)}, u32[]{:S(2)}, u32[]{:S(2)}) collective-permute-start(f32[4,5,2,8,128]{4,3,2,1,0:T(8,128)S(1)} %join_slots.1.m_ref), channel_id=1, source_target_pairs={{0,6},{2,0},{4,2},{6,4},{1,7},{3,1},{5,3},{7,5},{8,14},{10,8},{12,... | collective-permute-start | bytes 491528 | tf_op jit(solution)/shard_map/ppermute | solution.py:555
  16.1 7.3 %collective-permute-start.4 = (f32[4,5,2,8,128]{4,3,2,1,0:T(8,128)S(1)}, f32[4,5,2,8,128]{4,3,2,1,0:T(8,128)S(1)}, u32[]{:S(2)}, u32[]{:S(2)}) collective-permute-start(f32[4,5,2,8,128]{4,3,2,1,0:T(8,128)S(1)} %join_slots.1.m_ref), channel_id=1, source_target_pairs={{0,2},{2,4},{4,6},{6,0},{1,3},{3,5},{5,7},{7,1},{8,10},{10,12},{12... | collective-permute-start | bytes 491528 | tf_op jit(solution)/shard_map/ppermute | solution.py:554
  29.2 3.8 %collective-permute-start.6 = (f32[4,8,128]{2,1,0:T(8,128)S(1)}, f32[4,8,128]{2,1,0:T(8,128)S(1)}, u32[]{:S(2)}, u32[]{:S(2)}) collective-permute-start(f32[4,8,128]{2,1,0:T(8,128)S(1)} %get-tuple-element.15), channel_id=1, source_target_pairs={{0,8},{8,0},{16,24},{24,16},{1,9},{9,1},{17,25},{25,17},{2,10},{10... | collective-permute-start | bytes 49160 | tf_op jit(solution)/shard_map/ppermute | solution.py:559
  29.8 3.7 %collective-permute-start.7 = (f32[4,8,128]{2,1,0:T(8,128)S(1)}, f32[4,8,128]{2,1,0:T(8,128)S(1)}, u32[]{:S(2)}, u32[]{:S(2)}) collective-permute-start(f32[4,8,128]{2,1,0:T(8,128)S(1)} %get-tuple-element.16), channel_id=1, source_target_pairs={{0,16},{8,24},{16,0},{24,8},{1,17},{9,25},{17,1},{25,9},{2,18},{10... | collective-permute-start | bytes 49160 | tf_op jit(solution)/shard_map/ppermute | solution.py:559
  30.3 4.6 %collective-permute-start.8 = (f32[4,8,128]{2,1,0:T(8,128)S(1)}, f32[4,8,128]{2,1,0:T(8,128)S(1)}, u32[]{:S(2)}, u32[]{:S(2)}) collective-permute-start(f32[4,8,128]{2,1,0:T(8,128)S(1)} %get-tuple-element.17), channel_id=1, source_target_pairs={{0,24},{8,16},{16,8},{24,0},{1,25},{9,17},{17,9},{25,1},{2,26},{10... | collective-permute-start | bytes 49160 | tf_op jit(solution)/shard_map/ppermute | solution.py:559

commit v4 on v3

--- a/solution.py
+++ b/solution.py
@@ -14,8 +14,11 @@
 
 START_ROWS = 12
 WEIGH_ROWS = 12
+ADVANCE_ROWS = 12
+AHEAD = 2
 PAD = 2
-PIPELINE = False
+ADVANCE_ROWS = 10
+AHEAD = 2
 
 
 C = np.array(
@@ -286,7 +289,7 @@
 
     def body(b_ref, m_ref, a_ref, *rest):
         outs = rest[: sh.nx]
-        raw, first, second, psi_ref, solid_ref, force_ref, post_ref, done = rest[sh.nx :]
+        raw, first, second, psi_ref, solid_ref, force_ref, done = rest[sh.nx :]
         k = lax.axis_index("gx")
         lane = lax.broadcasted_iota(jnp.int32, (subs, LANES), 1)
         low = lane < sh.width
@@ -401,41 +404,28 @@
             def load_forces(y):
                 return [[force_ref[n, p, y] for n in range(3)] for p in range(2)]
 
-            def load_posts():
-                return [[post_ref[i, p] for p in range(2)] for i in range(19)]
-
             rows = half - 1 - 2 * step
-            if PIPELINE:
-
-                def advance(n, _, lo=lo, push=push, stream=stream, settle=settle):
-                    y = lo + 1 + n
-                    forces = load_forces(y)
-                    stream(load_posts(), y - 1, False)
-                    push(y + 1)
-                    for p in range(2):
-                        post = settle(y, p, forces[p])
-                        for i in range(19):
-                            post_ref[i, p] = post[i]
-                    return 0
-
-                push(lo + 1)
-                lax.fori_loop(0, rows, advance, 0)
-                stream(load_posts(), last, True)
+            at_once = max(d for d in range(1, ADVANCE_ROWS + 1) if (rows - 1) % d == 0)
+
+            def advance(n, _, lo=lo, push=push, stream=stream, settle=settle, at_once=at_once):
+                ys = [lo + 1 + n * at_once + r for r in range(at_once)]
+                forces = [load_forces(y) for y in ys[:AHEAD]]
+                for r, y in enumerate(ys):
+                    force = forces[r] if r < AHEAD else load_forces(y)
+                    both = [settle(y, p, force[p]) for p in range(2)]
+                    push(y + AHEAD)
+                    stream(list(zip(*both)), y, False)
+                return 0
+
+            for r in range(AHEAD):
+                push(lo + 1 + r)
+            if at_once == rows - 1:
+                advance(0, 0)
             else:
-
-                def advance(n, _, lo=lo, push=push, stream=stream, settle=settle):
-                    y = lo + 1 + n
-                    forces = load_forces(y)
-                    push(y + 1)
-                    both = [settle(y, p, forces[p]) for p in range(2)]
-                    stream(list(zip(*both)), y, False)
-                    return 0
-
-                push(lo + 1)
-                lax.fori_loop(0, rows - 1, advance, 0)
-                forces = load_forces(last)
-                both = [settle(last, p, forces[p]) for p in range(2)]
-                stream(list(zip(*both)), last, True)
+                lax.fori_loop(0, (rows - 1) // at_once, advance, 0)
+            forces = load_forces(last)
+            both = [settle(last, p, forces[p]) for p in range(2)]
+            stream(list(zip(*both)), last, True)
             source, target = target, source
 
         quarter = sh.y // 2
@@ -479,7 +469,6 @@
         row,
         row,
         (3,) + row,
-        (19, 2, subs, LANES),
         (2, 4, 2, subs * sh.y // 2, LANES),
     ]
     piece = (4, sh.own * sh.y // 2, LANES)

time: 35.9 us -> 33.4 us (0.930)
  Pallas kernels: 6.83 us -> 4.37 us
    pallas_call x1, Pallas kernels: 5.88 us -> 3.42 us  [run_steps(): pl.pallas_call(body, name='run_steps', out_shape=[jax.ShapeDtypeStruct(pi...]
where the time goes in v4:
time: 33.4 us; the launch traced here: 33.3 us
  waiting for transfers between devices  15.2 us (46%)
  starting transfers between devices  12.2 us (37%)
  Pallas kernels  4.37 us (13%)
  other arithmetic  0.78 us (2%)
  between operations  0.67 us (2%)
    ppermute x3, waiting for transfers between devices, on_device(): got.append(lax.ppermute(slabs[slot], 'gx', sh.perm(slot)))  4.88 us
    ppermute x3, starting transfers between devices, on_device(): got.append(lax.ppermute(slabs[slot], 'gx', sh.perm(slot)))  4.43 us
    ppermute x1, waiting for transfers between devices, on_device(): above = lax.ppermute(middle, 'gy', ring(sh.ny, -1))  3.82 us
    ppermute x1, starting transfers between devices, on_device(): above = lax.ppermute(middle, 'gy', ring(sh.ny, -1))  3.65 us
    ppermute x3, starting transfers between devices, on_device(): back.append(lax.ppermute(pieces[slot], 'gx', sh.perm(slot)))  3.55 us
    ppermute x1, waiting for transfers between devices, on_device(): below = lax.ppermute(middle, 'gy', ring(sh.ny, 1))  3.43 us
    pallas_call x1, Pallas kernels, run_steps(): pl.pallas_call(body, name='run_steps', out_shape=[jax.ShapeDtypeStruct(pi...  3.42 us
    ppermute x3, waiting for transfers between devices, on_device(): back.append(lax.ppermute(pieces[slot], 'gx', sh.perm(slot)))  2.19 us
  transfers between devices with their start and end apart: 9, of which 9 were waited for; matrix products, arithmetic and copies ran while one was open for 0% of the time, Pallas kernels for 0%

profile of v4, /device:TPU:0, one launch (start us, length us, event | category | flops | bytes accessed | tf_op | source)
XLA Modules:
  0.0 33.3 jit_solution(2483692465557202282)
XLA Ops:
  0.6 0.0 copy-start
  0.6 0.8 %select_bitcast_fusion = (f32[1,4,8,128]{3,2,1,0:T(8,128)S(1)}, f32[1,4,8,128]{3,2,1,0:T(8,128)S(1)}) fusion(s32[4,8,128]{2,1,0:T(8,128)} %param.7, f32[4,8,128]{2,1,0:T(8,128)} %param.4, s32[4,8,128]{2,1,0:T(8,128)} %param.6), kind=kLoop, calls=%fused_computation.1 | loop fusion | flops 20480 | bytes 81920 | tf_op jit(solution)/shard_map/broadcast_in_dim | solution.py:252
  1.4 0.0 copy-done
  1.4 0.5 %collective-permute-start = (f32[5,4,8,128]{3,2,1,0:T(8,128)S(1)}, f32[5,4,8,128]{3,2,1,0:T(8,128)S(1)}, u32[]{:S(2)}, u32[]{:S(2)}) collective-permute-start(f32[5,4,8,128]{3,2,1,0:T(8,128)S(1)} %pad_maximum_fusion.v_ref), channel_id=1, source_target_pairs={{0,1},{1,0},{2,3},{3,2},{4,5},{5,4},{6,7},{7,6},{8,9},{9,8},{10,11... | collective-permute-start | bytes 245768 | tf_op jit(solution)/shard_map/ppermute | solution.py:536
  2.0 0.9 %collective-permute-done.b_ref.a_ref = f32[5,4,8,128]{3,2,1,0:T(8,128)S(1)} collective-permute-done((f32[5,4,8,128]{3,2,1,0:T(8,128)S(1)}, f32[5,4,8,128]{3,2,1,0:T(8,128)S(1)}, u32[]{:S(2)}, u32[]{:S(2)}) %collective-permute-start) | collective-permute-done | bytes 81952 | tf_op jit(solution)/shard_map/ppermute | solution.py:536
  2.9 0.2 cut_slabs.1
  3.1 2.9 %collective-permute-start.1 = (f32[5,2,8,128]{3,2,1,0:T(8,128)S(1)}, f32[5,2,8,128]{3,2,1,0:T(8,128)S(1)}, u32[]{:S(2)}, u32[]{:S(2)}) collective-permute-start(f32[5,2,8,128]{3,2,1,0:T(8,128)S(1)} %get-tuple-element.11), channel_id=1, source_target_pairs={{0,8},{8,0},{16,24},{24,16},{1,9},{9,1},{17,25},{25,17},{2,10},{10... | collective-permute-start | bytes 122888 | tf_op jit(solution)/shard_map/ppermute | solution.py:541
  6.0 1.5 %collective-permute-start.2 = (f32[5,2,8,128]{3,2,1,0:T(8,128)S(1)}, f32[5,2,8,128]{3,2,1,0:T(8,128)S(1)}, u32[]{:S(2)}, u32[]{:S(2)}) collective-permute-start(f32[5,2,8,128]{3,2,1,0:T(8,128)S(1)} %get-tuple-element.12), channel_id=1, source_target_pairs={{0,16},{8,24},{16,0},{24,8},{1,17},{9,25},{17,1},{25,9},{2,18},{10... | collective-permute-start | bytes 122888 | tf_op jit(solution)/shard_map/ppermute | solution.py:541
  7.5 0.0 collective-permute-start.3
  7.5 0.4 %collective-permute-done.1.refs_1_ = f32[5,2,8,128]{3,2,1,0:T(8,128)S(1)} collective-permute-done((f32[5,2,8,128]{3,2,1,0:T(8,128)S(1)}, f32[5,2,8,128]{3,2,1,0:T(8,128)S(1)}, u32[]{:S(2)}, u32[]{:S(2)}) %collective-permute-start.1) | collective-permute-done | bytes 40992 | tf_op jit(solution)/shard_map/ppermute | solution.py:541
  8.0 2.0 %collective-permute-done.2.refs_2_ = f32[5,2,8,128]{3,2,1,0:T(8,128)S(1)} collective-permute-done((f32[5,2,8,128]{3,2,1,0:T(8,128)S(1)}, f32[5,2,8,128]{3,2,1,0:T(8,128)S(1)}, u32[]{:S(2)}, u32[]{:S(2)}) %collective-permute-start.2) | collective-permute-done | bytes 40992 | tf_op jit(solution)/shard_map/ppermute | solution.py:541
  10.0 2.4 %collective-permute-done.3.refs_3_ = f32[5,2,8,128]{3,2,1,0:T(8,128)S(1)} collective-permute-done((f32[5,2,8,128]{3,2,1,0:T(8,128)S(1)}, f32[5,2,8,128]{3,2,1,0:T(8,128)S(1)}, u32[]{:S(2)}, u32[]{:S(2)}) %collective-permute-start.3) | collective-permute-done | bytes 40992 | tf_op jit(solution)/shard_map/ppermute | solution.py:541
  12.4 3.7 %collective-permute-start.5 = (f32[4,5,2,8,128]{4,3,2,1,0:T(8,128)S(1)}, f32[4,5,2,8,128]{4,3,2,1,0:T(8,128)S(1)}, u32[]{:S(2)}, u32[]{:S(2)}) collective-permute-start(f32[4,5,2,8,128]{4,3,2,1,0:T(8,128)S(1)} %join_slots.1.m_ref), channel_id=1, source_target_pairs={{0,6},{2,0},{4,2},{6,4},{1,7},{3,1},{5,3},{7,5},{8,14},{10,8},{12,... | collective-permute-start | bytes 491528 | tf_op jit(solution)/shard_map/ppermute | solution.py:544
  16.1 0.0 collective-permute-start.4
  16.1 3.8 %collective-permute-done.5.a_ref = f32[4,5,2,8,128]{4,3,2,1,0:T(8,128)S(1)} collective-permute-done((f32[4,5,2,8,128]{4,3,2,1,0:T(8,128)S(1)}, f32[4,5,2,8,128]{4,3,2,1,0:T(8,128)S(1)}, u32[]{:S(2)}, u32[]{:S(2)}) %collective-permute-start.5) | collective-permute-done | bytes 163872 | tf_op jit(solution)/shard_map/ppermute | solution.py:544
  19.9 3.4 %collective-permute-done.4.b_ref = f32[4,5,2,8,128]{4,3,2,1,0:T(8,128)S(1)} collective-permute-done((f32[4,5,2,8,128]{4,3,2,1,0:T(8,128)S(1)}, f32[4,5,2,8,128]{4,3,2,1,0:T(8,128)S(1)}, u32[]{:S(2)}, u32[]{:S(2)}) %collective-permute-start.4) | collective-permute-done | bytes 163872 | tf_op jit(solution)/shard_map/ppermute | solution.py:543
  23.3 3.4 %run_steps.1 = (f32[4,8,128]{2,1,0:T(8,128)S(1)}, f32[4,8,128]{2,1,0:T(8,128)S(1)}, f32[4,8,128]{2,1,0:T(8,128)S(1)}, f32[4,8,128]{2,1,0:T(8,128)S(1)}) custom-call(f32[4,5,2,8,128]{4,3,2,1,0:T(8,128)S(1)} %collective-permute-done.4.b_ref, f32[4,5,2,8,128]{4,3,2,1,0:T(8,128)S(1)} %join_slots.1.m_ref, f32[4,5,2,8,128]{4,3,2,1,0:T(8,128)S(1)} %collective-permute-done.5.a_ref), custom_call_target="tpu_custom_call" | custom-call | tf_op jit(solution)/shard_map/run_steps/pallas_call | solution.py:476
  26.8 0.6 %collective-permute-start.6 = (f32[4,8,128]{2,1,0:T(8,128)S(1)}, f32[4,8,128]{2,1,0:T(8,128)S(1)}, u32[]{:S(2)}, u32[]{:S(2)}) collective-permute-start(f32[4,8,128]{2,1,0:T(8,128)S(1)} %get-tuple-element.15), channel_id=1, source_target_pairs={{0,8},{8,0},{16,24},{24,16},{1,9},{9,1},{17,25},{25,17},{2,10},{10... | collective-permute-start | bytes 49160 | tf_op jit(solution)/shard_map/ppermute | solution.py:548
  27.4 0.5 %collective-permute-start.7 = (f32[4,8,128]{2,1,0:T(8,128)S(1)}, f32[4,8,128]{2,1,0:T(8,128)S(1)}, u32[]{:S(2)}, u32[]{:S(2)}) collective-permute-start(f32[4,8,128]{2,1,0:T(8,128)S(1)} %get-tuple-element.16), channel_id=1, source_target_pairs={{0,16},{8,24},{16,0},{24,8},{1,17},{9,25},{17,1},{25,9},{2,18},{10... | collective-permute-start | bytes 49160 | tf_op jit(solution)/shard_map/ppermute | solution.py:548
  27.9 2.4 %collective-permute-start.8 = (f32[4,8,128]{2,1,0:T(8,128)S(1)}, f32[4,8,128]{2,1,0:T(8,128)S(1)}, u32[]{:S(2)}, u32[]{:S(2)}) collective-permute-start(f32[4,8,128]{2,1,0:T(8,128)S(1)} %get-tuple-element.17), channel_id=1, source_target_pairs={{0,24},{8,16},{16,8},{24,0},{1,25},{9,17},{17,9},{25,1},{2,26},{10... | collective-permute-start | bytes 49160 | tf_op jit(solution)/shard_map/ppermute | solution.py:548
  30.3 0.2 collective-permute-done.6.refs_1_
  30.6 0.5 %collective-permute-done.7.refs_2_ = f32[4,8,128]{2,1,0:T(8,128)S(1)} collective-permute-done((f32[4,8,128]{2,1,0:T(8,128)S(1)}, f32[4,8,128]{2,1,0:T(8,128)S(1)}, u32[]{:S(2)}, u32[]{:S(2)}) %collective-permute-start.7) | collective-permute-done | bytes 16416 | tf_op jit(solution)/shard_map/ppermute | solution.py:548
  31.1 1.4 %collective-permute-done.8.refs_3_ = f32[4,8,128]{2,1,0:T(8,128)S(1)} collective-permute-done((f32[4,8,128]{2,1,0:T(8,128)S(1)}, f32[4,8,128]{2,1,0:T(8,128)S(1)}, u32[]{:S(2)}, u32[]{:S(2)}) %collective-permute-start.8) | collective-permute-done | bytes 16416 | tf_op jit(solution)/shard_map/ppermute | solution.py:548
  32.5 0.8 %place_outputs.1 = (f32[4,8,128]{2,1,0:T(8,128)}, f32[3,4,8,128]{3,2,1,0:T(8,128)}) custom-call(f32[4,8,128]{2,1,0:T(8,128)S(1)} %get-tuple-element.14.refs_0_, f32[4,8,128]{2,1,0:T(8,128)S(1)} %collective-permute-done.6.refs_1_, f32[4,8,128]{2,1,0:T(8,128)S(1)} %collective-permute-done.7.refs_2_, f32[4,8,128]{2,1,0:T(8,128)S(1)} %collective-permute-done.8.refs_3_), custom_call_target="tpu_custom_call" | custom-call | tf_op jit(solution)/shard_map/place_outputs/pallas_call | solution.py:515
  (2 shorter events, 0.0 us)
Async XLA Ops:
  0.6 0.8 %copy-start = (f32[3,4,8,128]{3,2,1,0:T(8,128)S(1)}, f32[3,4,8,128]{3,2,1,0:T(8,128)}, u32[]{:S(2)}) copy-start(f32[3,4,8,128]{3,2,1,0:T(8,128)} %param.5) | copy-start | bytes 147460
  1.4 1.5 %collective-permute-start = (f32[5,4,8,128]{3,2,1,0:T(8,128)S(1)}, f32[5,4,8,128]{3,2,1,0:T(8,128)S(1)}, u32[]{:S(2)}, u32[]{:S(2)}) collective-permute-start(f32[5,4,8,128]{3,2,1,0:T(8,128)S(1)} %pad_maximum_fusion.v_ref), channel_id=1, source_target_pairs={{0,1},{1,0},{2,3},{3,2},{4,5},{5,4},{6,7},{7,6},{8,9},{9,8},{10,11... | collective-permute-start | bytes 245768 | tf_op jit(solution)/shard_map/ppermute | solution.py:536
  3.1 4.9 %collective-permute-start.1 = (f32[5,2,8,128]{3,2,1,0:T(8,128)S(1)}, f32[5,2,8,128]{3,2,1,0:T(8,128)S(1)}, u32[]{:S(2)}, u32[]{:S(2)}) collective-permute-start(f32[5,2,8,128]{3,2,1,0:T(8,128)S(1)} %get-tuple-element.11), channel_id=1, source_target_pairs={{0,8},{8,0},{16,24},{24,16},{1,9},{9,1},{17,25},{25,17},{2,10},{10... | collective-permute-start | bytes 122888 | tf_op jit(solution)/shard_map/ppermute | solution.py:541
  6.0 4.0 %collective-permute-start.2 = (f32[5,2,8,128]{3,2,1,0:T(8,128)S(1)}, f32[5,2,8,128]{3,2,1,0:T(8,128)S(1)}, u32[]{:S(2)}, u32[]{:S(2)}) collective-permute-start(f32[5,2,8,128]{3,2,1,0:T(8,128)S(1)} %get-tuple-element.12), channel_id=1, source_target_pairs={{0,16},{8,24},{16,0},{24,8},{1,17},{9,25},{17,1},{25,9},{2,18},{10... | collective-permute-start | bytes 122888 | tf_op jit(solution)/shard_map/ppermute | solution.py:541
  7.5 4.9 %collective-permute-start.3 = (f32[5,2,8,128]{3,2,1,0:T(8,128)S(1)}, f32[5,2,8,128]{3,2,1,0:T(8,128)S(1)}, u32[]{:S(2)}, u32[]{:S(2)}) collective-permute-start(f32[5,2,8,128]{3,2,1,0:T(8,128)S(1)} %get-tuple-element.13), channel_id=1, source_target_pairs={{0,24},{8,16},{16,8},{24,0},{1,25},{9,17},{17,9},{25,1},{2,26},{10... | collective-permute-start | bytes 122888 | tf_op jit(solution)/shard_map/ppermute | solution.py:541
  12.4 7.5 %collective-permute-start.5 = (f32[4,5,2,8,128]{4,3,2,1,0:T(8,128)S(1)}, f32[4,5,2,8,128]{4,3,2,1,0:T(8,128)S(1)}, u32[]{:S(2)}, u32[]{:S(2)}) collective-permute-start(f32[4,5,2,8,128]{4,3,2,1,0:T(8,128)S(1)} %join_slots.1.m_ref), channel_id=1, source_target_pairs={{0,6},{2,0},{4,2},{6,4},{1,7},{3,1},{5,3},{7,5},{8,14},{10,8},{12,... | collective-permute-start | bytes 491528 | tf_op jit(solution)/shard_map/ppermute | solution.py:544
  16.1 7.3 %collective-permute-start.4 = (f32[4,5,2,8,128]{4,3,2,1,0:T(8,128)S(1)}, f32[4,5,2,8,128]{4,3,2,1,0:T(8,128)S(1)}, u32[]{:S(2)}, u32[]{:S(2)}) collective-permute-start(f32[4,5,2,8,128]{4,3,2,1,0:T(8,128)S(1)} %join_slots.1.m_ref), channel_id=1, source_target_pairs={{0,2},{2,4},{4,6},{6,0},{1,3},{3,5},{5,7},{7,1},{8,10},{10,12},{12... | collective-permute-start | bytes 491528 | tf_op jit(solution)/shard_map/ppermute | solution.py:543
  26.8 3.8 %collective-permute-start.6 = (f32[4,8,128]{2,1,0:T(8,128)S(1)}, f32[4,8,128]{2,1,0:T(8,128)S(1)}, u32[]{:S(2)}, u32[]{:S(2)}) collective-permute-start(f32[4,8,128]{2,1,0:T(8,128)S(1)} %get-tuple-element.15), channel_id=1, source_target_pairs={{0,8},{8,0},{16,24},{24,16},{1,9},{9,1},{17,25},{25,17},{2,10},{10... | collective-permute-start | bytes 49160 | tf_op jit(solution)/shard_map/ppermute | solution.py:548
  27.4 3.7 %collective-permute-start.7 = (f32[4,8,128]{2,1,0:T(8,128)S(1)}, f32[4,8,128]{2,1,0:T(8,128)S(1)}, u32[]{:S(2)}, u32[]{:S(2)}) collective-permute-start(f32[4,8,128]{2,1,0:T(8,128)S(1)} %get-tuple-element.16), channel_id=1, source_target_pairs={{0,16},{8,24},{16,0},{24,8},{1,17},{9,25},{17,1},{25,9},{2,18},{10... | collective-permute-start | bytes 49160 | tf_op jit(solution)/shard_map/ppermute | solution.py:548
  27.9 4.6 %collective-permute-start.8 = (f32[4,8,128]{2,1,0:T(8,128)S(1)}, f32[4,8,128]{2,1,0:T(8,128)S(1)}, u32[]{:S(2)}, u32[]{:S(2)}) collective-permute-start(f32[4,8,128]{2,1,0:T(8,128)S(1)} %get-tuple-element.17), channel_id=1, source_target_pairs={{0,24},{8,16},{16,8},{24,0},{1,25},{9,17},{17,9},{25,1},{2,26},{10... | collective-permute-start | bytes 49160 | tf_op jit(solution)/shard_map/ppermute | solution.py:548

commit v5 on v4

--- a/solution.py
+++ b/solution.py
@@ -12,12 +12,6 @@
 HALO = 2 * STEPS
 LANES = 128
 
-START_ROWS = 12
-WEIGH_ROWS = 12
-ADVANCE_ROWS = 12
-AHEAD = 2
-PAD = 2
-ADVANCE_ROWS = 10
 AHEAD = 2
 
 
@@ -207,6 +201,8 @@
         self.groups = 2
         self.own = self.x // self.groups
         self.subs = self.x * self.nx // self.groups
+        self.span = self.slab + 2 * HALO
+        self.tiles = -(-5 * self.x * self.span // LANES)
         self.rows = self.y + 2 * HALO
         assert self.z == LANES and self.slab * self.nx == self.z
         assert self.slab + 2 * HALO <= self.width and 2 * self.slab <= self.width
@@ -221,6 +217,9 @@
             self.sender = lambda k, slot: lax.rem(k + self.nx - slot, self.nx)
             self.perm = lambda slot: [(i, (i + slot) % self.nx) for i in range(self.nx)]
 
+    def window(self, n, x):
+        return divmod((n * self.x + x) * self.span, LANES)
+
 
 def vmem(n):
     return [pl.BlockSpec(memory_space=pltpu.VMEM)] * n
@@ -256,193 +255,275 @@
     def body(v_ref, b_ref, a_ref, *outs):
         k = lax.axis_index("gx")
         lane = lax.broadcasted_iota(jnp.int32, (sh.y, LANES), 1)
-        group = lane // sh.width
         for slot, out in enumerate(outs):
             q = sh.peer(k, slot)
             low = (lane >= LANES - HALO) & (q == 0)
             high = (lane < HALO) & (q == sh.nx - 1)
             start = HALO - q * sh.slab + 2 * LANES
+            tile = None
             for n in range(5):
-                for m in range(sh.own):
-                    merged = None
-                    for g in range(sh.groups):
-                        x = m * sh.groups + g
-                        plane = jnp.where(low, b_ref[n, x], v_ref[n, x])
-                        plane = jnp.where(high, a_ref[n, x], plane)
-                        plane = pltpu.roll(plane, lax.rem(start + g * sh.width, LANES), 1)
-                        merged = plane if g == 0 else jnp.where(group == g, plane, merged)
-                    out[n, m] = merged
-
+                for x in range(sh.x):
+                    plane = jnp.where(low, b_ref[n, x], v_ref[n, x])
+                    plane = jnp.where(high, a_ref[n, x], plane)
+                    at, off = sh.window(n, x)
+                    plane = pltpu.roll(plane, lax.rem(start + off, LANES), 1)
+                    tile = plane if tile is None else jnp.where(lane >= off, plane, tile)
+                    if off + sh.span >= LANES:
+                        out[at] = tile
+                        tile = plane if off + sh.span > LANES else None
+            if tile is not None:
+                out[sh.tiles - 1] = tile
+
+    shape = (sh.tiles, sh.y, LANES)
     return pl.pallas_call(
         body,
         name="cut_slabs",
-        out_shape=[jax.ShapeDtypeStruct((5, sh.own, sh.y, LANES), jnp.float32)] * sh.nx,
+        out_shape=[jax.ShapeDtypeStruct(shape, jnp.float32)] * sh.nx,
         in_specs=vmem(3),
         out_specs=vmem(sh.nx),
-        compiler_params=grant((15 + 20) * math.prod(values.shape)),
+        compiler_params=grant(3 * math.prod(values.shape) + sh.nx * math.prod(shape)),
     )(values, before, after)
 
 
-def run_steps(below, middle, above, sh):
-    half, subs = sh.rows // 2, sh.subs
-    last = PAD + half - 1
-
-    def body(b_ref, m_ref, a_ref, *rest):
-        outs = rest[: sh.nx]
-        raw, first, second, psi_ref, solid_ref, force_ref, done = rest[sh.nx :]
+class Rows:
+    def __init__(self, sh):
+        self.sh = sh
+        self.half, self.own = sh.rows // 2, HALO
+        self.last = self.half - 1
+        self.shape = lambda *lead: pltpu.VMEM(lead + (sh.subs, LANES), jnp.float32)
+        self.out = lambda *lead: jax.ShapeDtypeStruct(lead + (sh.subs, LANES), jnp.float32)
+        lane = lax.broadcasted_iota(jnp.int32, (sh.subs, LANES), 1)
+        self.low = lane < sh.width
+        self.early = [s for s in range(STEPS) if self.own + 2 * s + 1 <= self.last]
+
+    def split(self, step):
+        return self.own + 2 * step + 1 if step in self.early else self.half
+
+    def writer(self, i, y):
+        cy = int(C[i, 1])
+        return self.last if y == self.last and cy == -1 else y - cy
+
+    def along_x(self, pair, cx):
+        if cx == 1:
+            return pltpu.roll(pair[1], 1, 0), pair[0]
+        if cx == -1:
+            return pair[1], pltpu.roll(pair[0], self.sh.subs - 1, 0)
+        return pair
+
+    def along_z(self, value, cz):
+        return pltpu.roll(value, cz % LANES, 1) if cz % LANES else value
+
+    def unpack(self, raw, parts, k):
+        sh = self.sh
+        wide = lax.broadcasted_iota(jnp.int32, (sh.y, LANES), 1)
+        near_half = lax.broadcasted_iota(jnp.int32, (sh.y, LANES), 0) < sh.y // 2
+        rows = len(parts) * sh.y
+        for slot in range(sh.nx):
+            base = sh.sender(k, slot) * (sh.own * rows)
+            for part, ref in enumerate(parts):
+                for n in range(5):
+                    for x in range(sh.x):
+                        at, off = sh.window(n, x)
+                        value = ref[slot, at]
+                        if off + sh.span > LANES:
+                            value = jnp.where(wide >= off, value, ref[slot, at + 1])
+                        to_low = lambda: self.along_z(value, -off)
+                        to_high = lambda: self.along_z(value, sh.width - off)
+                        if len(parts) == 1:
+                            value = jnp.where(near_half, to_low(), to_high())
+                        else:
+                            value = to_high() if part else to_low()
+                        m, p = divmod(x, 2)
+                        to = pl.multiple_of(base + m * rows + part * sh.y, 8)
+                        raw[n, p, pl.ds(to, sh.y), :] = value
+
+    def start(self, raw, rows, n, p):
+        near, far = (
+            [raw[v, p, pl.ds(at, self.sh.subs, stride=rows), :] for v in range(5)]
+            for at in (n, rows - 1 - n)
+        )
+        far[2] = -far[2]
+        return [jnp.where(self.low, a, b) for a, b in zip(near, far)]
+
+    def weigh(self, f, solid):
+        return potential(sum(f[1:], f[0]), solid > 0.5)
+
+    def reflect(self, value):
+        return self.along_z(value, self.sh.width)
+
+    def push(self, psi, y):
+        along_x, along_z = self.along_x, self.along_z
+        here, up, down = ([psi(p, at) for p in range(2)] for at in (y, y + 1, y - 1))
+        rise = [up[p] - down[p] for p in range(2)]
+        doubled = [2.0 * here[p] + (up[p] + down[p]) for p in range(2)]
+        before, after = along_x(here, 1), along_x(here, -1)
+        rise_x = [a + b for a, b in zip(along_x(rise, 1), along_x(rise, -1))]
+        z_sum = [doubled[p] + (along_z(here[p], 1) + along_z(here[p], -1)) for p in range(2)]
+        x_sum = [doubled[p] + (before[p] + after[p]) for p in range(2)]
+        fx = [a - b for a, b in zip(along_x(z_sum, -1), along_x(z_sum, 1))]
+        forces = []
+        for p in range(2):
+            fy = (2.0 * rise[p] + rise_x[p]) + (along_z(rise[p], 1) + along_z(rise[p], -1))
+            fz = along_z(x_sum[p], -1) - along_z(x_sum[p], 1)
+            scale = here[p] * (1.0 / 36.0)
+            forces.append([scale * value for value in (fx[p], fy, fz)])
+        return forces
+
+    def collide_rows(self, ys, psi, f, solid, store, force_ref):
+        def form(y):
+            for p, force in enumerate(self.push(psi, y)):
+                for n in range(3):
+                    force_ref[n, p, y] = force[n]
+
+        for y in ys[:AHEAD]:
+            form(y)
+        for at, y in enumerate(ys):
+            both = []
+            for p in range(2):
+                force = [force_ref[n, p, y] for n in range(3)]
+                both.append(collide([f(i, p, y) for i in range(19)], force, solid(p, y) > 0.5))
+            if at + AHEAD < len(ys):
+                form(ys[at + AHEAD])
+            for i, pair in enumerate(zip(*both)):
+                cx, cy, cz = (int(c) for c in C[i])
+                to, row = i, y + cy
+                if y == self.last and cy == 1:
+                    to, row, cz = MIRROR[i], y, cz + self.sh.width
+                for p, value in enumerate(self.along_x(pair, cx)):
+                    store(to, p, row, self.along_z(value, cz))
+
+
+def kernel_call(body, name, operands, outs, scratch, flops):
+    words = sum(math.prod(a.shape) for a in list(operands) + list(outs) + list(scratch))
+    return pl.pallas_call(
+        body,
+        name=name,
+        out_shape=outs,
+        in_specs=vmem(len(operands)),
+        out_specs=vmem(len(outs)),
+        scratch_shapes=scratch,
+        compiler_params=grant(words),
+        cost_estimate=pl.CostEstimate(flops=flops, transcendentals=0, bytes_accessed=words * 4),
+    )(*operands)
+
+
+def prepare(middle, sh):
+    rows = Rows(sh)
+    own, last, early = rows.own, rows.last, rows.early
+    count = rows.half - own
+
+    def body(m_ref, solid_ref, first, *rest):
+        psis, targets = rest[: len(early)], rest[len(early) : 2 * len(early)]
+        raw, force_ref = rest[2 * len(early) :]
+        low = Rows(sh)
+        low.unpack(raw, [m_ref], lax.axis_index("gx"))
+        solid = lambda p, y: solid_ref[p, y - own]
+        for n in range(count):
+            for p in range(2):
+                rho, ux, uy, uz, wall = low.start(raw, sh.y, n, p)
+                solid_ref[p, n] = wall
+                for i, row in enumerate(equilibrium(rho, [ux, uy, uz])):
+                    first[i, p, n] = row
+        source, base = first, own
+        for step in early:
+            psi_ref, target, top = psis[step], targets[step], own + 2 * step
+            f = lambda i, p, y, source=source, base=base: source[i, p, y - base]
+            psi = lambda p, y, psi_ref=psi_ref, top=top: psi_ref[p, y - top]
+            for p in range(2):
+                for y in range(top, last + 1):
+                    psi_ref[p, y - top] = low.weigh([f(i, p, y) for i in range(19)], solid(p, y))
+                psi_ref[p, last + 1 - top] = low.reflect(psi_ref[p, last - top])
+
+            def store(i, p, y, value, target=target, top=top):
+                target[i, p, y - top] = value
+
+            low.collide_rows(list(range(top + 1, last + 1)), psi, f, solid, store, force_ref)
+            source, base = target, top
+
+    lengths = [rows.half - own - 2 * step for step in early]
+    outs = [rows.out(2, count), rows.out(19, 2, count)]
+    outs += [rows.out(2, n + 1) for n in lengths] + [rows.out(19, 2, n) for n in lengths]
+    scratch = [
+        pltpu.VMEM((5, 2, sh.subs * sh.y, LANES), jnp.float32),
+        rows.shape(3, 2, rows.half + 1),
+    ]
+    return kernel_call(body, "prepare", (middle,), outs, scratch, 5_000_000)
+
+
+def run_steps(below, above, prepared, sh):
+    rows = Rows(sh)
+    half, own, last, early = rows.half, rows.own, rows.last, rows.early
+
+    def body(b_ref, a_ref, solid_own, first_own, *rest):
+        psis, gifts = rest[: len(early)], rest[len(early) : 2 * len(early)]
+        outs = rest[2 * len(early) : 2 * len(early) + sh.nx]
+        raw, one, other, psi_ref, solid_ref, force_ref, done = rest[2 * len(early) + sh.nx :]
         k = lax.axis_index("gx")
-        lane = lax.broadcasted_iota(jnp.int32, (subs, LANES), 1)
-        low = lane < sh.width
-
-        for slot in range(sh.nx):
-            base = sh.sender(k, slot) * (sh.own * sh.rows)
-            for part, ref in enumerate((b_ref, m_ref, a_ref)):
-                for n in range(5):
-                    for m in range(sh.own):
-                        at = pl.multiple_of(base + m * sh.rows + part * sh.y, 8)
-                        raw[n, pl.ds(at, sh.y), :] = ref[slot, n, m]
-
-        def along_x(pair, cx):
-            if cx == 1:
-                return pltpu.roll(pair[1], 1, 0), pair[0]
-            if cx == -1:
-                return pair[1], pltpu.roll(pair[0], subs - 1, 0)
-            return pair
-
-        def along_z(value, cz):
-            return pltpu.roll(value, cz % LANES, 1) if cz % LANES else value
-
-        def over(count, at_once, step):
-            at_once = min(at_once, count)
-            while count % at_once:
-                at_once -= 1
-
-            def trip(n, _):
-                for r in range(at_once):
-                    step(n * at_once + r)
-                return 0
-
-            if count == at_once:
-                trip(0, 0)
-            else:
-                lax.fori_loop(0, count // at_once, trip, 0)
-
-        def weigh(f, y, p):
-            psi_ref[p, y] = potential(sum(f[1:], f[0]), solid_ref[p, y] > 0.5)
-
-        def reflect():
+        low = Rows(sh)
+        low.unpack(raw, [b_ref, a_ref], k)
+
+        def solid(p, y):
+            return solid_ref[p, y] if y < own else solid_own[p, y - own]
+
+        for y in range(own):
             for p in range(2):
-                psi_ref[p, last + 1] = pltpu.roll(psi_ref[p, last], sh.width, 1)
-
-        def start(n):
-            y = PAD + n
-            pairs = []
-            for v in range(5):
-                near = raw[v, pl.ds(n, subs, stride=sh.rows), :]
-                far = raw[v, pl.ds(sh.rows - 1 - n, subs, stride=sh.rows), :]
-                far = -far if v == 2 else far
-                even = jnp.where(low, near, pltpu.roll(far, sh.width, 1))
-                odd = jnp.where(low, pltpu.roll(near, sh.width, 1), far)
-                pairs.append((even, odd))
-            for p in range(2):
-                rho, ux, uy, uz, solid = (pair[p] for pair in pairs)
+                rho, ux, uy, uz, wall = low.start(raw, 2 * sh.y, y, p)
                 f = equilibrium(rho, [ux, uy, uz])
-                solid_ref[p, y] = solid
+                solid_ref[p, y] = wall
                 for i in range(19):
-                    first[i, p, y] = f[i]
-                weigh(f, y, p)
-
-        over(half, START_ROWS, start)
-
-        source, target = first, second
+                    one[i, p, y] = f[i]
+                psi_ref[p, y] = low.weigh(f, wall)
+
+        source, target = one, other
         for step in range(STEPS):
-            lo = PAD + 2 * step
+            top = own + 2 * step
+
+            def f(i, p, y, step=step, source=source):
+                if step == 0 and y >= own:
+                    return first_own[i, p, y - own]
+                if step > 0 and rows.writer(i, y) >= rows.split(step - 1):
+                    return gifts[step - 1][i, p, y - (top_of(step - 1))]
+                return source[i, p, y]
+
+            def top_of(step):
+                return own + 2 * step
+
+            def psi(p, y, step=step):
+                if step in early and y >= top_of(step):
+                    return psis[step][p, y - top_of(step)]
+                return psi_ref[p, y]
+
+            stop = top if step in early else half
             if step > 0:
-
-                def weigh_again(n, source=source, lo=lo):
+                for y in range(2 * step, stop):
                     for p in range(2):
-                        weigh([source[i, p, lo + n] for i in range(19)], lo + n, p)
-
-                over(half - 2 * step, WEIGH_ROWS, weigh_again)
-            reflect()
-
-            def push(y):
-                here, up, down = (
-                    [psi_ref[p, at] for p in range(2)] for at in (y, y + 1, y - 1)
-                )
-                rise = [up[p] - down[p] for p in range(2)]
-                doubled = [2.0 * here[p] + (up[p] + down[p]) for p in range(2)]
-                before, after = along_x(here, 1), along_x(here, -1)
-                rise_x = [a + b for a, b in zip(along_x(rise, 1), along_x(rise, -1))]
-                z_sum = [
-                    doubled[p] + (along_z(here[p], 1) + along_z(here[p], -1)) for p in range(2)
-                ]
-                x_sum = [doubled[p] + (before[p] + after[p]) for p in range(2)]
-                fx = [a - b for a, b in zip(along_x(z_sum, -1), along_x(z_sum, 1))]
+                        psi_ref[p, y] = low.weigh([f(i, p, y) for i in range(19)], solid(p, y))
+            if step not in early:
                 for p in range(2):
-                    fy = (2.0 * rise[p] + rise_x[p]) + (
-                        along_z(rise[p], 1) + along_z(rise[p], -1)
-                    )
-                    fz = along_z(x_sum[p], -1) - along_z(x_sum[p], 1)
-                    scale = here[p] * (1.0 / 36.0)
-                    for n, value in enumerate((fx[p], fy, fz)):
-                        force_ref[n, p, y] = scale * value
-
-            def stream(posts, y, at_end, target=target):
-                for i in range(19):
-                    cx, cy, cz = (int(c) for c in C[i])
-                    to, row = i, y + cy
-                    if at_end and cy == 1:
-                        to, row, cz = MIRROR[i], y, cz + sh.width
-                    for p, value in enumerate(along_x(posts[i], cx)):
-                        target[to, p, row] = along_z(value, cz)
-
-            def settle(y, p, forces, source=source):
-                f = [source[i, p, y] for i in range(19)]
-                return collide(f, forces, solid_ref[p, y] > 0.5)
-
-            def load_forces(y):
-                return [[force_ref[n, p, y] for n in range(3)] for p in range(2)]
-
-            rows = half - 1 - 2 * step
-            at_once = max(d for d in range(1, ADVANCE_ROWS + 1) if (rows - 1) % d == 0)
-
-            def advance(n, _, lo=lo, push=push, stream=stream, settle=settle, at_once=at_once):
-                ys = [lo + 1 + n * at_once + r for r in range(at_once)]
-                forces = [load_forces(y) for y in ys[:AHEAD]]
-                for r, y in enumerate(ys):
-                    force = forces[r] if r < AHEAD else load_forces(y)
-                    both = [settle(y, p, force[p]) for p in range(2)]
-                    push(y + AHEAD)
-                    stream(list(zip(*both)), y, False)
-                return 0
-
-            for r in range(AHEAD):
-                push(lo + 1 + r)
-            if at_once == rows - 1:
-                advance(0, 0)
-            else:
-                lax.fori_loop(0, (rows - 1) // at_once, advance, 0)
-            forces = load_forces(last)
-            both = [settle(last, p, forces[p]) for p in range(2)]
-            stream(list(zip(*both)), last, True)
+                    psi_ref[p, half] = low.reflect(psi_ref[p, last])
+
+            def store(i, p, y, value, target=target):
+                target[i, p, y] = value
+
+            ys = list(range(2 * step + 1, rows.split(step)))
+            low.collide_rows(ys, psi, f, solid, store, force_ref)
             source, target = target, source
 
         quarter = sh.y // 2
         for n in range(quarter):
-            y = PAD + HALO + n
+            y = own + n
             for p in range(2):
                 f = [source[i, p, y] for i in range(19)]
                 rho = sum(f[1:], f[0])
-                fluid = solid_ref[p, y] < 0.5
+                fluid = solid(p, y) < 0.5
                 jx, jy, jz = moments(f)
                 inverse = math.sqrt(3.0) / rho
                 results = [rho * (1.0 / LIQUID), jx * inverse, jy * inverse, jz * inverse]
                 for v, value in enumerate(results):
                     value = jnp.where(fluid, value, 0.0)
-                    done[0, v, p, pl.ds(n, subs, stride=quarter), :] = value
+                    done[0, v, p, pl.ds(n, sh.subs, stride=quarter), :] = value
                     value = -value if v == 2 else value
-                    done[1, v, p, pl.ds(quarter - 1 - n, subs, stride=quarter), :] = value
+                    done[1, v, p, pl.ds(quarter - 1 - n, sh.subs, stride=quarter), :] = value
 
         size = sh.own * quarter
         lane = lax.broadcasted_iota(jnp.int32, (size, LANES), 1)
@@ -456,32 +537,22 @@
                 ]
                 out[v] = jnp.where(
                     odd,
-                    along_z(even_odd[1], sh.slab - HALO),
-                    along_z(even_odd[0], -HALO),
+                    low.along_z(even_odd[1], sh.slab - HALO),
+                    low.along_z(even_odd[0], -HALO),
                 )
 
-    padded = half + 2 * PAD
-    row = (2, padded, subs, LANES)
     scratch = [
-        (5, subs * sh.rows, LANES),
-        (19,) + row,
-        (19,) + row,
-        row,
-        row,
-        (3,) + row,
-        (2, 4, 2, subs * sh.y // 2, LANES),
+        pltpu.VMEM((5, 2, sh.subs * 2 * sh.y, LANES), jnp.float32),
+        rows.shape(19, 2, half),
+        rows.shape(19, 2, half),
+        rows.shape(2, half + 1),
+        rows.shape(2, own),
+        rows.shape(3, 2, half + 1),
+        pltpu.VMEM((2, 4, 2, sh.subs * sh.y // 2, LANES), jnp.float32),
     ]
-    piece = (4, sh.own * sh.y // 2, LANES)
-    words = sum(math.prod(shape) for shape in scratch)
-    return pl.pallas_call(
-        body,
-        name="run_steps",
-        out_shape=[jax.ShapeDtypeStruct(piece, jnp.float32)] * sh.nx,
-        in_specs=vmem(3),
-        out_specs=vmem(sh.nx),
-        scratch_shapes=[pltpu.VMEM(shape, jnp.float32) for shape in scratch],
-        compiler_params=grant(words + 3 * math.prod(middle.shape) + sh.nx * math.prod(piece)),
-    )(below, middle, above)
+    piece = jax.ShapeDtypeStruct((4, sh.own * sh.y // 2, LANES), jnp.float32)
+    operands = (below, above) + tuple(prepared)
+    return kernel_call(body, "run_steps", operands, [piece] * sh.nx, scratch, 50_000_000)
 
 
 def place_outputs(pieces, sh):
@@ -542,7 +613,7 @@
         middle = join_slots(got)
         below = lax.ppermute(middle, "gy", ring(sh.ny, 1))
         above = lax.ppermute(middle, "gy", ring(sh.ny, -1))
-        pieces = run_steps(below, middle, above, sh)
+        pieces = run_steps(below, above, prepare(middle, sh), sh)
         back = [pieces[0]]
         for slot in range(1, sh.nx):
             back.append(lax.ppermute(pieces[slot], "gx", sh.perm(slot)))

time: 33.4 us -> 32.6 us (0.976)
  waiting for transfers between devices: 15.2 us -> 13.7 us
  Pallas kernels: 4.37 us -> 5 us
    ppermute x1, waiting for transfers between devices: 3.82 us -> 1.85 us  [on_device(): above = lax.ppermute(middle, 'gy', ring(sh.ny, -1))]
    pallas_call x2 -> x3, Pallas kernels: 3.59 us -> 4.22 us  [the longest x2 4.05 us: kernel_call(): pl.pallas_call(body, name=name, out_shape=outs, in_specs=vmem(len(operand...]
    ppermute x1, waiting for transfers between devices: 3.43 us -> 3.99 us  [on_device(): below = lax.ppermute(middle, 'gy', ring(sh.ny, 1))]
  transfers between devices with their start and end apart: 9 -> 9, of which waited for: 9 -> 9; matrix products, arithmetic and copies ran while one was open for 0% -> 0% of each run, Pallas kernels for 0% -> 3%
where the time goes in v5:
time: 32.6 us; the launch traced here: 32.4 us
  waiting for transfers between devices  13.7 us (42%)
  starting transfers between devices  12.2 us (37%)
  Pallas kernels  5 us (15%)
  other arithmetic  0.78 us (2%)
  between operations  0.67 us (2%)
    ppermute x3, waiting for transfers between devices, on_device(): got.append(lax.ppermute(slabs[slot], 'gx', sh.perm(slot)))  4.79 us
    ppermute x3, starting transfers between devices, on_device(): got.append(lax.ppermute(slabs[slot], 'gx', sh.perm(slot)))  4.43 us
    pallas_call x2, Pallas kernels, kernel_call(): pl.pallas_call(body, name=name, out_shape=outs, in_specs=vmem(len(operand...  4.05 us
    ppermute x1, waiting for transfers between devices, on_device(): below = lax.ppermute(middle, 'gy', ring(sh.ny, 1))  3.99 us
    ppermute x1, starting transfers between devices, on_device(): above = lax.ppermute(middle, 'gy', ring(sh.ny, -1))  3.65 us
    ppermute x3, starting transfers between devices, on_device(): back.append(lax.ppermute(pieces[slot], 'gx', sh.perm(slot)))  3.55 us
    ppermute x3, waiting for transfers between devices, on_device(): back.append(lax.ppermute(pieces[slot], 'gx', sh.perm(slot)))  2.19 us
    ppermute x1, waiting for transfers between devices, on_device(): above = lax.ppermute(middle, 'gy', ring(sh.ny, -1))  1.85 us
  transfers between devices with their start and end apart: 9, of which 9 were waited for; matrix products, arithmetic and copies ran while one was open for 0% of the time, Pallas kernels for 3%

profile of v5, /device:TPU:0, one launch (start us, length us, event | category | flops | bytes accessed | tf_op | source)
XLA Modules:
  0.0 32.4 jit_solution(2983013629791304673)
XLA Ops:
  0.6 0.8 %select_bitcast_fusion = (f32[1,4,8,128]{3,2,1,0:T(8,128)S(1)}, f32[1,4,8,128]{3,2,1,0:T(8,128)S(1)}) fusion(s32[4,8,128]{2,1,0:T(8,128)} %param.7, f32[4,8,128]{2,1,0:T(8,128)} %param.4, s32[4,8,128]{2,1,0:T(8,128)} %param.6), kind=kLoop, calls=%fused_computation.1 | loop fusion | flops 20480 | bytes 81920 | tf_op jit(solution)/shard_map/broadcast_in_dim | solution.py:251
  1.4 0.0 copy-done
  1.4 0.5 %collective-permute-start = (f32[5,4,8,128]{3,2,1,0:T(8,128)S(1)}, f32[5,4,8,128]{3,2,1,0:T(8,128)S(1)}, u32[]{:S(2)}, u32[]{:S(2)}) collective-permute-start(f32[5,4,8,128]{3,2,1,0:T(8,128)S(1)} %pad_maximum_fusion.v_ref), channel_id=1, source_target_pairs={{0,1},{1,0},{2,3},{3,2},{4,5},{5,4},{6,7},{7,6},{8,9},{9,8},{10,11... | collective-permute-start | bytes 245768 | tf_op jit(solution)/shard_map/ppermute | solution.py:607
  2.0 0.9 %collective-permute-done.b_ref.a_ref = f32[5,4,8,128]{3,2,1,0:T(8,128)S(1)} collective-permute-done((f32[5,4,8,128]{3,2,1,0:T(8,128)S(1)}, f32[5,4,8,128]{3,2,1,0:T(8,128)S(1)}, u32[]{:S(2)}, u32[]{:S(2)}) %collective-permute-start) | collective-permute-done | bytes 81952 | tf_op jit(solution)/shard_map/ppermute | solution.py:607
  2.9 0.2 cut_slabs.1
  3.1 2.9 %collective-permute-start.1 = (f32[8,8,128]{2,1,0:T(8,128)S(1)}, f32[8,8,128]{2,1,0:T(8,128)S(1)}, u32[]{:S(2)}, u32[]{:S(2)}) collective-permute-start(f32[8,8,128]{2,1,0:T(8,128)S(1)} %get-tuple-element.17), channel_id=1, source_target_pairs={{0,8},{8,0},{16,24},{24,16},{1,9},{9,1},{17,25},{25,17},{2,10},{10... | collective-permute-start | bytes 98312 | tf_op jit(solution)/shard_map/ppermute | solution.py:612
  6.0 1.5 %collective-permute-start.2 = (f32[8,8,128]{2,1,0:T(8,128)S(1)}, f32[8,8,128]{2,1,0:T(8,128)S(1)}, u32[]{:S(2)}, u32[]{:S(2)}) collective-permute-start(f32[8,8,128]{2,1,0:T(8,128)S(1)} %get-tuple-element.18), channel_id=1, source_target_pairs={{0,16},{8,24},{16,0},{24,8},{1,17},{9,25},{17,1},{25,9},{2,18},{10... | collective-permute-start | bytes 98312 | tf_op jit(solution)/shard_map/ppermute | solution.py:612
  7.5 0.0 collective-permute-start.3
  7.5 0.4 %collective-permute-done.1.refs_1_ = f32[8,8,128]{2,1,0:T(8,128)S(1)} collective-permute-done((f32[8,8,128]{2,1,0:T(8,128)S(1)}, f32[8,8,128]{2,1,0:T(8,128)S(1)}, u32[]{:S(2)}, u32[]{:S(2)}) %collective-permute-start.1) | collective-permute-done | bytes 32800 | tf_op jit(solution)/shard_map/ppermute | solution.py:612
  7.9 2.0 %collective-permute-done.2.refs_2_ = f32[8,8,128]{2,1,0:T(8,128)S(1)} collective-permute-done((f32[8,8,128]{2,1,0:T(8,128)S(1)}, f32[8,8,128]{2,1,0:T(8,128)S(1)}, u32[]{:S(2)}, u32[]{:S(2)}) %collective-permute-start.2) | collective-permute-done | bytes 32800 | tf_op jit(solution)/shard_map/ppermute | solution.py:612
  9.9 2.4 %collective-permute-done.3.refs_3_ = f32[8,8,128]{2,1,0:T(8,128)S(1)} collective-permute-done((f32[8,8,128]{2,1,0:T(8,128)S(1)}, f32[8,8,128]{2,1,0:T(8,128)S(1)}, u32[]{:S(2)}, u32[]{:S(2)}) %collective-permute-start.3) | collective-permute-done | bytes 32800 | tf_op jit(solution)/shard_map/ppermute | solution.py:612
  12.3 3.7 %collective-permute-start.5 = (f32[4,8,8,128]{3,2,1,0:T(8,128)S(1)}, f32[4,8,8,128]{3,2,1,0:T(8,128)S(1)}, u32[]{:S(2)}, u32[]{:S(2)}) collective-permute-start(f32[4,8,8,128]{3,2,1,0:T(8,128)S(1)} %join_slots.1.m_ref), channel_id=1, source_target_pairs={{0,6},{2,0},{4,2},{6,4},{1,7},{3,1},{5,3},{7,5},{8,14},{10,8},{12,... | collective-permute-start | bytes 393224 | tf_op jit(solution)/shard_map/ppermute | solution.py:615
  16.0 0.0 collective-permute-start.4
  16.0 0.9 %prepare.1 = (f32[2,4,8,128]{3,2,1,0:T(8,128)S(1)}, f32[19,2,4,8,128]{4,3,2,1,0:T(8,128)S(1)}, f32[2,5,8,128]{3,2,1,0:T(8,128)S(1)}, f32[2,3,8,128]{3,2,1,0:T(8,...) custom-call(f32[4,8,8,128]{3,2,1,0:T(8,128)S(1)} %join_slots.1.m_ref), custom_call_target="tpu_custom_call" | custom-call | flops 5000000 | bytes 2433024 | tf_op jit(solution)/shard_map/prepare/pallas_call | solution.py:398
  16.9 1.8 %collective-permute-done.5.a_ref = f32[4,8,8,128]{3,2,1,0:T(8,128)S(1)} collective-permute-done((f32[4,8,8,128]{3,2,1,0:T(8,128)S(1)}, f32[4,8,8,128]{3,2,1,0:T(8,128)S(1)}, u32[]{:S(2)}, u32[]{:S(2)}) %collective-permute-start.5) | collective-permute-done | bytes 131104 | tf_op jit(solution)/shard_map/ppermute | solution.py:615
  18.7 4.0 %collective-permute-done.4.b_ref = f32[4,8,8,128]{3,2,1,0:T(8,128)S(1)} collective-permute-done((f32[4,8,8,128]{3,2,1,0:T(8,128)S(1)}, f32[4,8,8,128]{3,2,1,0:T(8,128)S(1)}, u32[]{:S(2)}, u32[]{:S(2)}) %collective-permute-start.4) | collective-permute-done | bytes 131104 | tf_op jit(solution)/shard_map/ppermute | solution.py:614
  22.7 3.1 %run_steps.1 = (f32[4,8,128]{2,1,0:T(8,128)S(1)}, f32[4,8,128]{2,1,0:T(8,128)S(1)}, f32[4,8,128]{2,1,0:T(8,128)S(1)}, f32[4,8,128]{2,1,0:T(8,128)S(1)}) custom-call(f32[4,8,8,128]{3,2,1,0:T(8,128)S(1)} %collective-permute-done.4.b_ref, f32[4,8,8,128]{3,2,1,0:T(8,128)S(1)} %collective-permute-done.5.a_ref, f32[2,4,8,128]{3,2,1,0:T(8,128)S(1)} %get-tuple-element.20.solid_own, ...), custom_call_target="tpu_custom_call" | custom-call | flops 50000000 | bytes 7127040 | tf_op jit(solution)/shard_map/run_steps/pallas_call | solution.py:398
  25.9 0.6 %collective-permute-start.6 = (f32[4,8,128]{2,1,0:T(8,128)S(1)}, f32[4,8,128]{2,1,0:T(8,128)S(1)}, u32[]{:S(2)}, u32[]{:S(2)}) collective-permute-start(f32[4,8,128]{2,1,0:T(8,128)S(1)} %get-tuple-element.27), channel_id=1, source_target_pairs={{0,8},{8,0},{16,24},{24,16},{1,9},{9,1},{17,25},{25,17},{2,10},{10... | collective-permute-start | bytes 49160 | tf_op jit(solution)/shard_map/ppermute | solution.py:619
  26.5 0.5 %collective-permute-start.7 = (f32[4,8,128]{2,1,0:T(8,128)S(1)}, f32[4,8,128]{2,1,0:T(8,128)S(1)}, u32[]{:S(2)}, u32[]{:S(2)}) collective-permute-start(f32[4,8,128]{2,1,0:T(8,128)S(1)} %get-tuple-element.28), channel_id=1, source_target_pairs={{0,16},{8,24},{16,0},{24,8},{1,17},{9,25},{17,1},{25,9},{2,18},{10... | collective-permute-start | bytes 49160 | tf_op jit(solution)/shard_map/ppermute | solution.py:619
  27.0 2.4 %collective-permute-start.8 = (f32[4,8,128]{2,1,0:T(8,128)S(1)}, f32[4,8,128]{2,1,0:T(8,128)S(1)}, u32[]{:S(2)}, u32[]{:S(2)}) collective-permute-start(f32[4,8,128]{2,1,0:T(8,128)S(1)} %get-tuple-element.29), channel_id=1, source_target_pairs={{0,24},{8,16},{16,8},{24,0},{1,25},{9,17},{17,9},{25,1},{2,26},{10... | collective-permute-start | bytes 49160 | tf_op jit(solution)/shard_map/ppermute | solution.py:619
  29.4 0.2 collective-permute-done.6.refs_1_
  29.7 0.5 %collective-permute-done.7.refs_2_ = f32[4,8,128]{2,1,0:T(8,128)S(1)} collective-permute-done((f32[4,8,128]{2,1,0:T(8,128)S(1)}, f32[4,8,128]{2,1,0:T(8,128)S(1)}, u32[]{:S(2)}, u32[]{:S(2)}) %collective-permute-start.7) | collective-permute-done | bytes 16416 | tf_op jit(solution)/shard_map/ppermute | solution.py:619
  30.2 1.4 %collective-permute-done.8.refs_3_ = f32[4,8,128]{2,1,0:T(8,128)S(1)} collective-permute-done((f32[4,8,128]{2,1,0:T(8,128)S(1)}, f32[4,8,128]{2,1,0:T(8,128)S(1)}, u32[]{:S(2)}, u32[]{:S(2)}) %collective-permute-start.8) | collective-permute-done | bytes 16416 | tf_op jit(solution)/shard_map/ppermute | solution.py:619
  31.6 0.8 %place_outputs.1 = (f32[4,8,128]{2,1,0:T(8,128)}, f32[3,4,8,128]{3,2,1,0:T(8,128)}) custom-call(f32[4,8,128]{2,1,0:T(8,128)S(1)} %get-tuple-element.26.refs_0_, f32[4,8,128]{2,1,0:T(8,128)S(1)} %collective-permute-done.6.refs_1_, f32[4,8,128]{2,1,0:T(8,128)S(1)} %collective-permute-done.7.refs_2_, f32[4,8,128]{2,1,0:T(8,128)S(1)} %collective-permute-done.8.refs_3_), custom_call_target="tpu_custom_call" | custom-call | tf_op jit(solution)/shard_map/place_outputs/pallas_call | solution.py:586
  (3 shorter events, 0.0 us)
Async XLA Ops:
  0.6 0.8 %copy-start = (f32[3,4,8,128]{3,2,1,0:T(8,128)S(1)}, f32[3,4,8,128]{3,2,1,0:T(8,128)}, u32[]{:S(2)}) copy-start(f32[3,4,8,128]{3,2,1,0:T(8,128)} %param.5) | copy-start | bytes 147460
  1.4 1.5 %collective-permute-start = (f32[5,4,8,128]{3,2,1,0:T(8,128)S(1)}, f32[5,4,8,128]{3,2,1,0:T(8,128)S(1)}, u32[]{:S(2)}, u32[]{:S(2)}) collective-permute-start(f32[5,4,8,128]{3,2,1,0:T(8,128)S(1)} %pad_maximum_fusion.v_ref), channel_id=1, source_target_pairs={{0,1},{1,0},{2,3},{3,2},{4,5},{5,4},{6,7},{7,6},{8,9},{9,8},{10,11... | collective-permute-start | bytes 245768 | tf_op jit(solution)/shard_map/ppermute | solution.py:607
  3.1 4.8 %collective-permute-start.1 = (f32[8,8,128]{2,1,0:T(8,128)S(1)}, f32[8,8,128]{2,1,0:T(8,128)S(1)}, u32[]{:S(2)}, u32[]{:S(2)}) collective-permute-start(f32[8,8,128]{2,1,0:T(8,128)S(1)} %get-tuple-element.17), channel_id=1, source_target_pairs={{0,8},{8,0},{16,24},{24,16},{1,9},{9,1},{17,25},{25,17},{2,10},{10... | collective-permute-start | bytes 98312 | tf_op jit(solution)/shard_map/ppermute | solution.py:612
  6.0 3.9 %collective-permute-start.2 = (f32[8,8,128]{2,1,0:T(8,128)S(1)}, f32[8,8,128]{2,1,0:T(8,128)S(1)}, u32[]{:S(2)}, u32[]{:S(2)}) collective-permute-start(f32[8,8,128]{2,1,0:T(8,128)S(1)} %get-tuple-element.18), channel_id=1, source_target_pairs={{0,16},{8,24},{16,0},{24,8},{1,17},{9,25},{17,1},{25,9},{2,18},{10... | collective-permute-start | bytes 98312 | tf_op jit(solution)/shard_map/ppermute | solution.py:612
  7.5 4.8 %collective-permute-start.3 = (f32[8,8,128]{2,1,0:T(8,128)S(1)}, f32[8,8,128]{2,1,0:T(8,128)S(1)}, u32[]{:S(2)}, u32[]{:S(2)}) collective-permute-start(f32[8,8,128]{2,1,0:T(8,128)S(1)} %get-tuple-element.19), channel_id=1, source_target_pairs={{0,24},{8,16},{16,8},{24,0},{1,25},{9,17},{17,9},{25,1},{2,26},{10... | collective-permute-start | bytes 98312 | tf_op jit(solution)/shard_map/ppermute | solution.py:612
  12.3 6.4 %collective-permute-start.5 = (f32[4,8,8,128]{3,2,1,0:T(8,128)S(1)}, f32[4,8,8,128]{3,2,1,0:T(8,128)S(1)}, u32[]{:S(2)}, u32[]{:S(2)}) collective-permute-start(f32[4,8,8,128]{3,2,1,0:T(8,128)S(1)} %join_slots.1.m_ref), channel_id=1, source_target_pairs={{0,6},{2,0},{4,2},{6,4},{1,7},{3,1},{5,3},{7,5},{8,14},{10,8},{12,... | collective-permute-start | bytes 393224 | tf_op jit(solution)/shard_map/ppermute | solution.py:615
  16.0 6.8 %collective-permute-start.4 = (f32[4,8,8,128]{3,2,1,0:T(8,128)S(1)}, f32[4,8,8,128]{3,2,1,0:T(8,128)S(1)}, u32[]{:S(2)}, u32[]{:S(2)}) collective-permute-start(f32[4,8,8,128]{3,2,1,0:T(8,128)S(1)} %join_slots.1.m_ref), channel_id=1, source_target_pairs={{0,2},{2,4},{4,6},{6,0},{1,3},{3,5},{5,7},{7,1},{8,10},{10,12},{12... | collective-permute-start | bytes 393224 | tf_op jit(solution)/shard_map/ppermute | solution.py:614
  25.9 3.8 %collective-permute-start.6 = (f32[4,8,128]{2,1,0:T(8,128)S(1)}, f32[4,8,128]{2,1,0:T(8,128)S(1)}, u32[]{:S(2)}, u32[]{:S(2)}) collective-permute-start(f32[4,8,128]{2,1,0:T(8,128)S(1)} %get-tuple-element.27), channel_id=1, source_target_pairs={{0,8},{8,0},{16,24},{24,16},{1,9},{9,1},{17,25},{25,17},{2,10},{10... | collective-permute-start | bytes 49160 | tf_op jit(solution)/shard_map/ppermute | solution.py:619
  26.5 3.7 %collective-permute-start.7 = (f32[4,8,128]{2,1,0:T(8,128)S(1)}, f32[4,8,128]{2,1,0:T(8,128)S(1)}, u32[]{:S(2)}, u32[]{:S(2)}) collective-permute-start(f32[4,8,128]{2,1,0:T(8,128)S(1)} %get-tuple-element.28), channel_id=1, source_target_pairs={{0,16},{8,24},{16,0},{24,8},{1,17},{9,25},{17,1},{25,9},{2,18},{10... | collective-permute-start | bytes 49160 | tf_op jit(solution)/shard_map/ppermute | solution.py:619
  27.0 4.6 %collective-permute-start.8 = (f32[4,8,128]{2,1,0:T(8,128)S(1)}, f32[4,8,128]{2,1,0:T(8,128)S(1)}, u32[]{:S(2)}, u32[]{:S(2)}) collective-permute-start(f32[4,8,128]{2,1,0:T(8,128)S(1)} %get-tuple-element.29), channel_id=1, source_target_pairs={{0,24},{8,16},{16,8},{24,0},{1,25},{9,17},{17,9},{25,1},{2,26},{10... | collective-permute-start | bytes 49160 | tf_op jit(solution)/shard_map/ppermute | solution.py:619

commit v6 on v5

v6 whole, which is shorter than its diff:
```python
import math

import jax
import jax.numpy as jnp
import numpy as np
from jax import lax
from jax.experimental import pallas as pl
from jax.experimental.pallas import tpu as pltpu
from jax.sharding import PartitionSpec as P

STEPS = 4
HALO = 2 * STEPS
LANES = 128

AHEAD = 2


C = np.array(
    [
        [0, 0, 0],
        [1, 0, 0],
        [-1, 0, 0],
        [0, 1, 0],
        [0, -1, 0],
        [0, 0, 1],
        [0, 0, -1],
        [1, 1, 0],
        [-1, -1, 0],
        [1, -1, 0],
        [-1, 1, 0],
        [1, 0, 1],
        [-1, 0, -1],
        [1, 0, -1],
        [-1, 0, 1],
        [0, 1, 1],
        [0, -1, -1],
        [0, 1, -1],
        [0, -1, 1],
    ]
)
WEIGHTS = [1.0 / 3.0] + [1.0 / 18.0] * 6 + [1.0 / 36.0] * 12
OPPOSITE = [0, 2, 1, 4, 3, 6, 5, 8, 7, 10, 9, 12, 11, 14, 13, 16, 15, 18, 17]
LIQUID = 0.28
VAPOUR = 0.06
WALL_POTENTIAL = 0.5
ATTRACTION = 1.0
TEMPERATURE = 0.06

KEEP_E = 1.0 - 1.19
KEEP_P = 1.0 - 1.4
KEEP_Q = 1.0 - 1.2
KEEP_N = 1.0 - 1.25
KEEP_M = 1.0 - 1.98


def equilibrium(rho, u):
    rest = 1.0 - 1.5 * (u[0] * u[0] + u[1] * u[1] + u[2] * u[2])
    rows = [(rho * WEIGHTS[0]) * rest]
    scaled = [None, rho * WEIGHTS[1], rho * WEIGHTS[7]]
    still = [None] + [w * rest for w in scaled[1:]]
    triple = [None] + [3.0 * w for w in scaled[1:]]
    for i in range(1, 19, 2):
        terms = [u[k] if C[i, k] > 0 else -u[k] for k in range(3) if C[i, k] != 0]
        n = len(terms)
        along = terms[0] if n == 1 else terms[0] + terms[1]
        odd = triple[n] * along
        even = still[n] + (1.5 * odd) * along
        rows += [even + odd, even - odd]
    return rows


def potential(rho):
    square = rho * rho
    gap = 1.0 - rho
    pressure = (
        rho * TEMPERATURE * (1.0 + rho + square - square * rho) / (gap * gap * gap)
        - ATTRACTION * square
    )
    return jnp.sqrt(6.0 * (rho * (1.0 / 3.0) - pressure))


def times(c, value):
    c = float(np.float32(c))
    return value if c == 1.0 else -value if c == -1.0 else c * value


def moments(f):
    d = [None] + [f[i] - f[i + 1] for i in range(1, 19, 2)]
    jx = d[1] + ((d[4] + d[5]) + (d[6] + d[7]))
    jy = d[2] + ((d[4] - d[5]) + (d[8] + d[9]))
    jz = d[3] + ((d[6] - d[7]) + (d[8] - d[9]))
    return jx, jy, jz


def collide(f, force, solid):
    s = [None] + [f[i] + f[i + 1] for i in range(1, 19, 2)]
    d = [None] + [f[i] - f[i + 1] for i in range(1, 19, 2)]
    xy, xz, yz = s[4] + s[5], s[6] + s[7], s[8] + s[9]
    axes = s[1] + s[2] + s[3]
    diagonals = xy + xz + yz
    rho = f[0] + axes + diagonals
    p_xy, q_xy = d[4] + d[5], d[4] - d[5]
    p_xz, q_xz = d[6] + d[7], d[6] - d[7]
    p_yz, q_yz = d[8] + d[9], d[8] - d[9]
    j = [d[1] + (p_xy + p_xz), d[2] + (q_xy + p_yz), d[3] + (q_xz + q_yz)]
    inverse = 1.0 / rho
    u = [j[k] * inverse for k in range(3)]
    moved = [j[k] + force[k] for k in range(3)]
    v = [moved[k] * inverse for k in range(3)]
    uu = [j[k] * u[k] for k in range(3)]
    vv = [moved[k] * v[k] for k in range(3)]
    u2 = uu[0] + uu[1] + uu[2]
    v2 = vv[0] + vv[1] + vv[2]

    def isotropic(of_energy, of_epsilon):
        parts = (
            (1.0 / 19.0 - of_energy * (11.0 + 19.0 * KEEP_E) + of_epsilon * (3.0 + 9.0 * KEEP_P), rho),
            (of_energy * 19.0 * KEEP_E - of_epsilon * 16.0 * KEEP_P, axes),
            (of_energy * 38.0 * KEEP_E - of_epsilon * 11.0 * KEEP_P, diagonals),
            (of_energy * 19.0 - of_epsilon * 5.5, v2),
            (-of_energy * 19.0 * KEEP_E + of_epsilon * 5.5 * KEEP_P, u2),
        )
        return sum((c * value for c, value in parts[1:]), parts[0][0] * parts[0][1])

    even_axis = isotropic(-11.0 / 2394.0, -4.0 / 252.0)
    even_diag = isotropic(8.0 / 2394.0, 1.0 / 252.0)
    even_rest = rho - 6.0 * even_axis - 12.0 * even_diag

    def stress(a, b, at_v, at_u, scale):
        on_axis = (
            ((KEEP_N + 2.0 * KEEP_P) * scale) * a
            + ((KEEP_N - KEEP_P) * scale) * b
            + (1.5 * scale) * at_v
            - ((KEEP_N + 0.5 * KEEP_P) * scale) * at_u
        )
        half = 0.5 * scale
        on_diagonal = (
            ((2.0 * KEEP_N - 2.0 * KEEP_P) * half) * a
            + ((2.0 * KEEP_N + KEEP_P) * half) * b
            + (1.5 * half) * at_v
            - ((2.0 * KEEP_N - 0.5 * KEEP_P) * half) * at_u
        )
        return on_axis, on_diagonal

    h, g = stress(
        3.0 * s[1] - axes,
        diagonals - 3.0 * yz,
        3.0 * vv[0] - v2,
        3.0 * uu[0] - u2,
        1.0 / 36.0,
    )
    k, l = stress(s[2] - s[3], xy - xz, vv[1] - vv[2], uu[1] - uu[2], 1.0 / 12.0)

    quarter = [None, 0.25 * v[1], 0.25 * v[2]]

    def shear(a, b, pair):
        return (0.25 * KEEP_N) * (pair - j[a] * u[b]) + moved[a] * quarter[b]

    t_xy = shear(0, 1, s[4] - s[5])
    t_xz = shear(0, 2, s[6] - s[7])
    t_yz = shear(1, 2, s[8] - s[9])

    flux = [
        times(-5.0 * KEEP_Q, d[n + 1])
        + (times(KEEP_Q * 5.0 / 3.0 - 2.0 / 3.0, moved[n]) - (KEEP_Q * 5.0 / 3.0) * force[n])
        for n in range(3)
    ]
    tenth = [0.1 * moved[n] for n in range(3)]
    axis_odd = [tenth[n] - 0.1 * flux[n] for n in range(3)]
    diag_odd = [tenth[n] + 0.025 * flux[n] for n in range(3)]
    third = KEEP_M / 8.0
    mx, my, mz = third * (p_xy - p_xz), third * (p_yz - q_xy), third * (q_xz - q_yz)

    twist = even_axis - h
    evens = [even_axis + 2.0 * h, twist + k, twist - k]
    ring = even_diag + g
    e_xy, e_xz, e_yz = ring + l, ring - l, even_diag - 2.0 * g
    a, b = diag_odd[0] + mx, diag_odd[1] - my
    odd_xy = (a + b, a - b)
    a, b = diag_odd[0] - mx, diag_odd[2] + mz
    odd_xz = (a + b, a - b)
    a, b = diag_odd[1] + my, diag_odd[2] - mz
    odd_yz = (a + b, a - b)

    post = [even_rest]
    for n in range(3):
        post += [evens[n] + axis_odd[n], evens[n] - axis_odd[n]]
    for even, t, odd in ((e_xy, t_xy, odd_xy), (e_xz, t_xz, odd_xz), (e_yz, t_yz, odd_yz)):
        same, cross = even + t, even - t
        post += [same + odd[0], same - odd[0], cross + odd[1], cross - odd[1]]
    return [jnp.where(solid, f[OPPOSITE[i]], post[i]) for i in range(19)]


class Shape:
    def __init__(self, mesh, block):
        self.nx, self.ny, self.nz = (mesh.shape[a] for a in ("gx", "gy", "gz"))
        self.x, self.y, self.z = block
        self.slab = self.z // self.nx
        self.width = LANES // 2
        self.groups = 2
        self.own = self.x // self.groups
        self.subs = self.x * self.nx // self.groups
        self.span = self.slab + 2 * HALO
        self.tiles = -(-5 * self.x * self.span // LANES)
        self.rows = self.y + 2 * HALO
        assert self.z == LANES and self.slab * self.nx == self.z
        assert self.slab + 2 * HALO <= self.width and 2 * self.slab <= self.width
        assert self.y == HALO and self.own * self.groups == self.x
        assert self.subs % 8 == 0
        if self.nx & (self.nx - 1) == 0:
            self.peer = lambda k, slot: jnp.bitwise_xor(k, slot)
            self.perm = lambda slot: [(i, i ^ slot) for i in range(self.nx)]
            self.sender = self.peer
        else:
            self.peer = lambda k, slot: lax.rem(k + slot, self.nx)
            self.sender = lambda k, slot: lax.rem(k + self.nx - slot, self.nx)
            self.perm = lambda slot: [(i, (i + slot) % self.nx) for i in range(self.nx)]

    def window(self, n, x):
        return divmod((n * self.x + x) * self.span, LANES)


def vmem(n):
    return [pl.BlockSpec(memory_space=pltpu.VMEM)] * n


def grant(words):
    return pltpu.CompilerParams(vmem_limit_bytes=(words * 4 * 5) // 4 + (1 << 20))


def join_slots(parts):
    def body(*refs):
        for n, ref in enumerate(refs[:-1]):
            refs[-1][n] = ref[...]

    block = parts[0].shape
    return pl.pallas_call(
        body,
        name="join_slots",
        out_shape=jax.ShapeDtypeStruct((len(parts),) + block, jnp.float32),
        in_specs=vmem(len(parts)),
        out_specs=vmem(1)[0],
        compiler_params=grant(2 * len(parts) * math.prod(block)),
    )(*parts)


def gather_inputs(scatter, velocity, bubbles, walls):
    rho = jnp.where(bubbles == 1, VAPOUR, LIQUID) * scatter
    solid = jnp.where(walls == 1, 1.0, 0.0)
    return jnp.concatenate([rho[None], velocity, solid[None]])


def cut_slabs(values, before, after, sh):
    def body(v_ref, b_ref, a_ref, *outs):
        k = lax.axis_index("gx")
        lane = lax.broadcasted_iota(jnp.int32, (sh.y, LANES), 1)
        for slot, out in enumerate(outs):
            q = sh.peer(k, slot)
            low = (lane >= LANES - HALO) & (q == 0)
            high = (lane < HALO) & (q == sh.nx - 1)
            start = HALO - q * sh.slab + 2 * LANES
            tile = None
            for n in range(5):
                for x in range(sh.x):
                    plane = jnp.where(low, b_ref[n, x], v_ref[n, x])
                    plane = jnp.where(high, a_ref[n, x], plane)
                    at, off = sh.window(n, x)
                    plane = pltpu.roll(plane, lax.rem(start + off, LANES), 1)
                    tile = plane if tile is None else jnp.where(lane >= off, plane, tile)
                    if off + sh.span >= LANES:
                        out[at] = tile
                        tile = plane if off + sh.span > LANES else None
            if tile is not None:
                out[sh.tiles - 1] = tile

    shape = (sh.tiles, sh.y, LANES)
    return pl.pallas_call(
        body,
        name="cut_slabs",
        out_shape=[jax.ShapeDtypeStruct(shape, jnp.float32)] * sh.nx,
        in_specs=vmem(3),
        out_specs=vmem(sh.nx),
        compiler_params=grant(3 * math.prod(values.shape) + sh.nx * math.prod(shape)),
    )(values, before, after)


STAGES = ("own", "above", "below")


class Rows:
    def __init__(self, sh):
        self.sh = sh
        self.own, self.end = HALO, HALO + sh.y
        lane = lax.broadcasted_iota(jnp.int32, (sh.subs, LANES), 1)
        self.odd = lane >= sh.width

    def inputs(self, stage):
        first = {"own": self.own, "above": self.end, "below": 0}[stage]
        return first, first + self.sh.y - 1

    def weighed(self, stage, s):
        own, end, rows = self.own, self.end, self.sh.rows
        return {
            "own": (own + 2 * s, end - 1 - 2 * s),
            "above": (max(own + 2 * s, end - 2 * s), rows - 1 - 2 * s),
            "below": (2 * s, own - 1 + 2 * s),
        }[stage]

    def collided(self, stage, s):
        own, end, rows = self.own, self.end, self.sh.rows
        return {
            "own": (own + 1 + 2 * s, end - 2 - 2 * s),
            "above": (max(own + 1 + 2 * s, end - 1 - 2 * s), rows - 2 - 2 * s),
            "below": (1 + 2 * s, own + 2 * s),
        }[stage]

    def steps(self, stage):
        ranges = [self.collided(stage, s) for s in range(STEPS)]
        return [s for s, (first, last) in enumerate(ranges) if first <= last]

    def buffers(self, stage):
        left = {("solid",): ((),) + self.inputs(stage), ("f", 0): ((19,),) + self.inputs(stage)}
        for s in self.steps(stage):
            left["psi", s] = ((),) + self.weighed(stage, s)
            first, last = self.collided(stage, s)
            left["f", s + 1] = ((19,), first - 1, last + 1)
        return left

    def shapes(self, stage):
        return [
            lead + (last + 1 - first, self.sh.subs, LANES)
            for lead, first, last in self.buffers(stage).values()
        ]

    def shifted(self, value, cx, cz):
        if cx == 1:
            value = jnp.where(self.odd, pltpu.roll(value, 1, 0), value)
        if cx == -1:
            value = jnp.where(self.odd, value, pltpu.roll(value, self.sh.subs - 1, 0))
        turn = (cx * self.sh.width + cz) % LANES
        return pltpu.roll(value, turn, 1) if turn else value

    def unpack(self, raw, ref, k):
        sh = self.sh
        wide = lax.broadcasted_iota(jnp.int32, (sh.y, LANES), 1)

        def plane(slot, n, x):
            at, off = sh.window(n, x)
            value = ref[slot, at]
            if off + sh.span > LANES:
                value = jnp.where(wide >= off, value, ref[slot, at + 1])
            turn = (x % 2 * sh.width - off) % LANES
            return pltpu.roll(value, turn, 1) if turn else value

        for slot in range(sh.nx):
            base = sh.sender(k, slot) * (sh.own * sh.y)
            for n in range(5):
                for m in range(sh.own):
                    value = jnp.where(
                        wide < sh.width, plane(slot, n, 2 * m), plane(slot, n, 2 * m + 1)
                    )
                    raw[n, pl.ds(pl.multiple_of(base + m * sh.y, 8), sh.y), :] = value

    def push(self, psi, y):
        shifted = self.shifted
        here, up, down = psi(y), psi(y + 1), psi(y - 1)
        rise = up - down
        doubled = 2.0 * here + (up + down)
        z_sum = doubled + (shifted(here, 0, 1) + shifted(here, 0, -1))
        x_sum = doubled + (shifted(here, 1, 0) + shifted(here, -1, 0))
        fy = (2.0 * rise + (shifted(rise, 1, 0) + shifted(rise, -1, 0))) + (
            shifted(rise, 0, 1) + shifted(rise, 0, -1)
        )
        fx = shifted(z_sum, -1, 0) - shifted(z_sum, 1, 0)
        fz = shifted(x_sum, 0, -1) - shifted(x_sum, 0, 1)
        scale = here * (1.0 / 36.0)
        return [scale * value for value in (fx, fy, fz)]

    def run(self, stage, held, raw, force_ref, fresh, k):
        sh = self.sh
        table = {other: self.buffers(other) for other in STAGES}

        def at(owner, name, y):
            return held[owner, name], y - table[owner][name][1]

        def owner_of(ranges, y):
            for other in STAGES:
                first, last = ranges(other)
                if first <= y <= last:
                    return other
            raise AssertionError(y)

        def solid(y):
            ref, row = at(owner_of(self.inputs, y), ("solid",), y)
            return ref[row] > 0.5

        def psi_of(s):
            def psi(y):
                ref, row = at(owner_of(lambda o: self.weighed(o, s), y), ("psi", s), y)
                return ref[row]

            return psi

        def f(s, i, y):
            if s == 0:
                owner = owner_of(self.inputs, y)
            else:
                from_row = y - int(C[i, 1])
                owner = owner_of(lambda o: self.collided(o, s - 1), from_row)
            ref, row = at(owner, ("f", s), y)
            return ref[i, row]

        self.unpack(raw, fresh, k)
        first, last = self.inputs(stage)
        for n in range(sh.y):
            rho, ux, uy, uz, wall = (raw[v, pl.ds(n, sh.subs, stride=sh.y), :] for v in range(5))
            held[stage, ("solid",)][n] = wall
            for i, row in enumerate(equilibrium(rho, [ux, uy, uz])):
                held[stage, ("f", 0)][i, n] = row

        for s in self.steps(stage):
            first, last = self.weighed(stage, s)
            for y in range(first, last + 1):
                rows = [f(s, i, y) for i in range(19)]
                held[stage, ("psi", s)][y - first] = jnp.where(
                    solid(y), WALL_POTENTIAL, potential(sum(rows[1:], rows[0]))
                )
            first, last = self.collided(stage, s)
            psi, ys = psi_of(s), list(range(first, last + 1))

            def form(y, psi=psi):
                for n, value in enumerate(self.push(psi, y)):
                    force_ref[n, y] = value

            for y in ys[:AHEAD]:
                form(y)
            for n, y in enumerate(ys):
                force = [force_ref[axis, y] for axis in range(3)]
                post = collide([f(s, i, y) for i in range(19)], force, solid(y))
                if n + AHEAD < len(ys):
                    form(ys[n + AHEAD])
                for i in range(19):
                    cx, cy, cz = (int(c) for c in C[i])
                    held[stage, ("f", s + 1)][i, y + cy - (first - 1)] = self.shifted(
                        post[i], cx, cz
                    )
        return f, solid


def run_stage(stage, fresh, left, sh, flops):
    rows = Rows(sh)
    before = STAGES[: STAGES.index(stage)]
    names = [(o, name) for o in before for name in rows.buffers(o)]
    own = [(stage, name) for name in rows.buffers(stage)]
    last_stage = stage == STAGES[-1]

    def body(fresh_ref, *refs):
        held = dict(zip(names, refs))
        refs = refs[len(names) :]
        outs = ()
        if last_stage:
            outs, refs = refs[: sh.nx], refs[sh.nx :]
        held.update(zip(own, refs))
        raw, force_ref, done = refs[len(own) :]
        k = lax.axis_index("gx")
        low = Rows(sh)
        f, solid = low.run(stage, held, raw, force_ref, fresh_ref, k)
        if not last_stage:
            return
        for n in range(sh.y):
            y = low.own + n
            g = [f(STEPS, i, y) for i in range(19)]
            rho, wall = sum(g[1:], g[0]), solid(y)
            inverse = math.sqrt(3.0) / rho
            results = [rho * (1.0 / LIQUID)] + [c * inverse for c in moments(g)]
            for v, value in enumerate(results):
                done[v, pl.ds(n, sh.subs, stride=sh.y), :] = jnp.where(wall, 0.0, value)
        lane = lax.broadcasted_iota(jnp.int32, (sh.y, LANES), 1)
        place = (lane % sh.width) // sh.slab
        for slot, out in enumerate(outs):
            base = sh.peer(k, slot) * (sh.own * sh.y)
            for v in range(4):
                merged = None
                for m in range(sh.own):
                    value = done[v, pl.ds(pl.multiple_of(base + m * sh.y, 8), sh.y), :]
                    value = pltpu.roll(value, (m * sh.slab - HALO) % LANES, 1)
                    merged = value if m == 0 else jnp.where(place == m, value, merged)
                out[v] = merged

    shapes = rows.shapes(stage)
    piece = jax.ShapeDtypeStruct((4, sh.y, LANES), jnp.float32)
    scratch = [pltpu.VMEM(shape, jnp.float32) for shape in shapes]
    extra = [
        pltpu.VMEM((5, sh.subs * sh.y, LANES), jnp.float32),
        pltpu.VMEM((3, sh.rows, sh.subs, LANES), jnp.float32),
        pltpu.VMEM((4, sh.subs * sh.y, LANES), jnp.float32),
    ]
    outs = [jax.ShapeDtypeStruct(shape, jnp.float32) for shape in shapes]
    if last_stage:
        outs, extra = [piece] * sh.nx, scratch + extra
    operands = (fresh,) + tuple(left)
    words = sum(math.prod(a.shape) for a in list(operands) + list(outs) + list(extra))
    return pl.pallas_call(
        body,
        name="stage_" + stage,
        out_shape=outs,
        in_specs=vmem(len(operands)),
        out_specs=vmem(len(outs)),
        scratch_shapes=extra,
        compiler_params=grant(words),
        cost_estimate=pl.CostEstimate(flops=flops, transcendentals=0, bytes_accessed=words * 4),
    )(*operands)


def place_outputs(pieces, sh):
    def body(*refs):
        ins, (density, velocity) = refs[: sh.nx], refs[sh.nx :]
        k = lax.axis_index("gx")
        place = lax.broadcasted_iota(jnp.int32, (sh.y, LANES), 1) // sh.slab
        for v in range(4):
            for x in range(sh.x):
                m, g = divmod(x, 2)
                merged = None
                for slot, ref in enumerate(ins):
                    q = sh.sender(k, slot)
                    turn = (q - m) * sh.slab - g * sh.width + 2 * LANES
                    value = pltpu.roll(ref[v], lax.rem(turn, LANES), 1)
                    merged = value if slot == 0 else jnp.where(place == q, value, merged)
                if v == 0:
                    density[x] = merged
                else:
                    velocity[v - 1, x] = merged

    block = (sh.x, sh.y, sh.z)
    return pl.pallas_call(
        body,
        name="place_outputs",
        out_shape=[
            jax.ShapeDtypeStruct(block, jnp.float32),
            jax.ShapeDtypeStruct((3,) + block, jnp.float32),
        ],
        in_specs=vmem(sh.nx),
        out_specs=vmem(2),
        compiler_params=grant(8 * sh.nx * sh.y * LANES + 8 * math.prod(block)),
    )(*pieces)


def ring(size, step):
    return [(i, (i + step) % size) for i in range(size)]


def solution(mesh):
    def on_device(density_scatter, initial_velocity, bubble_mask, wall_flags):
        sh = Shape(mesh, wall_flags.shape)
        values = gather_inputs(density_scatter, initial_velocity, bubble_mask, wall_flags)
        before = lax.ppermute(values, "gz", ring(sh.nz, 1))
        after = before if sh.nz == 2 else lax.ppermute(values, "gz", ring(sh.nz, -1))
        slabs = cut_slabs(values, before, after, sh)
        got = [slabs[0]]
        for slot in range(1, sh.nx):
            got.append(lax.ppermute(slabs[slot], "gx", sh.perm(slot)))
        middle = join_slots(got)
        below = lax.ppermute(middle, "gy", ring(sh.ny, 1))
        above = lax.ppermute(middle, "gy", ring(sh.ny, -1))
        left = run_stage("own", middle, (), sh, 5_000_000)
        left = left + run_stage("above", above, left, sh, 20_000_000)
        pieces = run_stage("below", below, left, sh, 30_000_000)
        back = [pieces[0]]
        for slot in range(1, sh.nx):
            back.append(lax.ppermute(pieces[slot], "gx", sh.perm(slot)))
        return tuple(place_outputs(back, sh))

    in_specs = (
        P("gx", "gy", "gz"),
        P(None, "gx", "gy", "gz"),
        P("gx", "gy", "gz"),
        P("gx", "gy", "gz"),
    )
    out_specs = (P("gx", "gy", "gz"), P(None, "gx", "gy", "gz"))
    return jax.shard_map(
        on_device, mesh=mesh, in_specs=in_specs, out_specs=out_specs, check_vma=False
    )
```

time: 32.6 us -> 31.6 us (0.969)
  waiting for transfers between devices: 13.7 us -> 12 us
  Pallas kernels: 5 us -> 5.69 us
    ppermute x1, waiting for transfers between devices: 3.99 us -> 2.21 us  [on_device(): below = lax.ppermute(middle, 'gy', ring(sh.ny, 1))]
    pallas_call x2 -> x3, Pallas kernels: 4.05 us -> 4.74 us  [run_stage(): pl.pallas_call(body, name='stage_' + stage, out_shape=outs, in_specs=vmem...]
  transfers between devices with their start and end apart: 9 -> 9, of which waited for: 9 -> 9; matrix products, arithmetic and copies ran while one was open for 0% -> 0% of each run, Pallas kernels for 3% -> 8%
where the time goes in v6:
time: 31.6 us; the launch traced here: 31.4 us
  starting transfers between devices  12.2 us (39%)
  waiting for transfers between devices  12 us (38%)
  Pallas kernels  5.69 us (18%)
  other arithmetic  0.78 us (2%)
  between operations  0.67 us (2%)
    ppermute x3, waiting for transfers between devices, on_device(): got.append(lax.ppermute(slabs[slot], 'gx', sh.perm(slot)))  4.79 us
    pallas_call x3, Pallas kernels, run_stage(): pl.pallas_call(body, name='stage_' + stage, out_shape=outs, in_specs=vmem...  4.74 us
    ppermute x3, starting transfers between devices, on_device(): got.append(lax.ppermute(slabs[slot], 'gx', sh.perm(slot)))  4.43 us
    ppermute x1, starting transfers between devices, on_device(): above = lax.ppermute(middle, 'gy', ring(sh.ny, -1))  3.65 us
    ppermute x3, starting transfers between devices, on_device(): back.append(lax.ppermute(pieces[slot], 'gx', sh.perm(slot)))  3.55 us
    ppermute x1, waiting for transfers between devices, on_device(): below = lax.ppermute(middle, 'gy', ring(sh.ny, 1))  2.21 us
    ppermute x3, waiting for transfers between devices, on_device(): back.append(lax.ppermute(pieces[slot], 'gx', sh.perm(slot)))  2.19 us
    ppermute x1, waiting for transfers between devices, on_device(): above = lax.ppermute(middle, 'gy', ring(sh.ny, -1))  1.92 us
  transfers between devices with their start and end apart: 9, of which 9 were waited for; matrix products, arithmetic and copies ran while one was open for 0% of the time, Pallas kernels for 8%

profile of v6, /device:TPU:0, one launch (start us, length us, event | category | flops | bytes accessed | tf_op | source)
XLA Modules:
  0.0 31.4 jit_solution(12375679724284644823)
XLA Ops:
  0.6 0.8 %select_bitcast_fusion = (f32[1,4,8,128]{3,2,1,0:T(8,128)S(1)}, f32[1,4,8,128]{3,2,1,0:T(8,128)S(1)}) fusion(s32[4,8,128]{2,1,0:T(8,128)} %param.7, f32[4,8,128]{2,1,0:T(8,128)} %param.4, s32[4,8,128]{2,1,0:T(8,128)} %param.6), kind=kLoop, calls=%fused_computation.1 | loop fusion | flops 20480 | bytes 81920 | tf_op jit(solution)/shard_map/broadcast_in_dim | solution.py:250
  1.4 0.0 copy-done
  1.4 0.5 %collective-permute-start = (f32[5,4,8,128]{3,2,1,0:T(8,128)S(1)}, f32[5,4,8,128]{3,2,1,0:T(8,128)S(1)}, u32[]{:S(2)}, u32[]{:S(2)}) collective-permute-start(f32[5,4,8,128]{3,2,1,0:T(8,128)S(1)} %pad_maximum_fusion.v_ref), channel_id=1, source_target_pairs={{0,1},{1,0},{2,3},{3,2},{4,5},{5,4},{6,7},{7,6},{8,9},{9,8},{10,11... | collective-permute-start | bytes 245768 | tf_op jit(solution)/shard_map/ppermute | solution.py:556
  2.0 0.9 %collective-permute-done.b_ref.a_ref = f32[5,4,8,128]{3,2,1,0:T(8,128)S(1)} collective-permute-done((f32[5,4,8,128]{3,2,1,0:T(8,128)S(1)}, f32[5,4,8,128]{3,2,1,0:T(8,128)S(1)}, u32[]{:S(2)}, u32[]{:S(2)}) %collective-permute-start) | collective-permute-done | bytes 81952 | tf_op jit(solution)/shard_map/ppermute | solution.py:556
  2.9 0.2 cut_slabs.1
  3.1 2.9 %collective-permute-start.1 = (f32[8,8,128]{2,1,0:T(8,128)S(1)}, f32[8,8,128]{2,1,0:T(8,128)S(1)}, u32[]{:S(2)}, u32[]{:S(2)}) collective-permute-start(f32[8,8,128]{2,1,0:T(8,128)S(1)} %get-tuple-element.27), channel_id=1, source_target_pairs={{0,8},{8,0},{16,24},{24,16},{1,9},{9,1},{17,25},{25,17},{2,10},{10... | collective-permute-start | bytes 98312 | tf_op jit(solution)/shard_map/ppermute | solution.py:561
  6.0 1.5 %collective-permute-start.2 = (f32[8,8,128]{2,1,0:T(8,128)S(1)}, f32[8,8,128]{2,1,0:T(8,128)S(1)}, u32[]{:S(2)}, u32[]{:S(2)}) collective-permute-start(f32[8,8,128]{2,1,0:T(8,128)S(1)} %get-tuple-element.28), channel_id=1, source_target_pairs={{0,16},{8,24},{16,0},{24,8},{1,17},{9,25},{17,1},{25,9},{2,18},{10... | collective-permute-start | bytes 98312 | tf_op jit(solution)/shard_map/ppermute | solution.py:561
  7.5 0.0 collective-permute-start.3
  7.5 0.4 %collective-permute-done.1.refs_1_ = f32[8,8,128]{2,1,0:T(8,128)S(1)} collective-permute-done((f32[8,8,128]{2,1,0:T(8,128)S(1)}, f32[8,8,128]{2,1,0:T(8,128)S(1)}, u32[]{:S(2)}, u32[]{:S(2)}) %collective-permute-start.1) | collective-permute-done | bytes 32800 | tf_op jit(solution)/shard_map/ppermute | solution.py:561
  7.9 2.0 %collective-permute-done.2.refs_2_ = f32[8,8,128]{2,1,0:T(8,128)S(1)} collective-permute-done((f32[8,8,128]{2,1,0:T(8,128)S(1)}, f32[8,8,128]{2,1,0:T(8,128)S(1)}, u32[]{:S(2)}, u32[]{:S(2)}) %collective-permute-start.2) | collective-permute-done | bytes 32800 | tf_op jit(solution)/shard_map/ppermute | solution.py:561
  9.9 2.4 %collective-permute-done.3.refs_3_ = f32[8,8,128]{2,1,0:T(8,128)S(1)} collective-permute-done((f32[8,8,128]{2,1,0:T(8,128)S(1)}, f32[8,8,128]{2,1,0:T(8,128)S(1)}, u32[]{:S(2)}, u32[]{:S(2)}) %collective-permute-start.3) | collective-permute-done | bytes 32800 | tf_op jit(solution)/shard_map/ppermute | solution.py:561
  12.3 3.7 %collective-permute-start.5 = (f32[4,8,8,128]{3,2,1,0:T(8,128)S(1)}, f32[4,8,8,128]{3,2,1,0:T(8,128)S(1)}, u32[]{:S(2)}, u32[]{:S(2)}) collective-permute-start(f32[4,8,8,128]{3,2,1,0:T(8,128)S(1)} %join_slots.1.fresh_ref), channel_id=1, source_target_pairs={{0,6},{2,0},{4,2},{6,4},{1,7},{3,1},{5,3},{7,5},{8,14},{10,8},{12,... | collective-permute-start | bytes 393224 | tf_op jit(solution)/shard_map/ppermute | solution.py:564
  16.0 0.8 %stage_own.1 = (f32[8,8,128]{2,1,0:T(8,128)S(1)}, f32[19,8,8,128]{3,2,1,0:T(8,128)S(1)}, f32[8,8,128]{2,1,0:T(8,128)S(1)}, f32[19,8,8,128]{3,2,1,0:T(8,128)S(1)}...) custom-call(f32[4,8,8,128]{3,2,1,0:T(8,128)S(1)} %join_slots.1.fresh_ref), custom_call_target="tpu_custom_call" | custom-call | flops 5000000 | bytes 2359296 | tf_op jit(solution)/shard_map/stage_own/pallas_call | solution.py:503
  16.8 1.9 %collective-permute-done.5.fresh_ref = f32[4,8,8,128]{3,2,1,0:T(8,128)S(1)} collective-permute-done((f32[4,8,8,128]{3,2,1,0:T(8,128)S(1)}, f32[4,8,8,128]{3,2,1,0:T(8,128)S(1)}, u32[]{:S(2)}, u32[]{:S(2)}) %collective-permute-start.5) | collective-permute-done | bytes 131104 | tf_op jit(solution)/shard_map/ppermute | solution.py:564
  18.7 1.8 %stage_above.1 = (f32[8,8,128]{2,1,0:T(8,128)S(1)}, f32[19,8,8,128]{3,2,1,0:T(8,128)S(1)}, f32[8,8,128]{2,1,0:T(8,128)S(1)}, f32[19,10,8,128]{3,2,1,0:T(8,128)S(...) custom-call(f32[4,8,8,128]{3,2,1,0:T(8,128)S(1)} %collective-permute, ...), custom_call_target="tpu_custom_call" | custom-call | flops 20000000 | bytes 5619712 | tf_op jit(solution)/shard_map/stage_above/pallas_call | solution.py:503
  20.5 2.2 %collective-permute-done.4.fresh_ref = f32[4,8,8,128]{3,2,1,0:T(8,128)S(1)} collective-permute-done((f32[4,8,8,128]{3,2,1,0:T(8,128)S(1)}, f32[4,8,8,128]{3,2,1,0:T(8,128)S(1)}, u32[]{:S(2)}, u32[]{:S(2)}) %collective-permute-start.4) | collective-permute-done | bytes 131104 | tf_op jit(solution)/shard_map/ppermute | solution.py:563
  22.7 2.1 %stage_below.1 = (f32[4,8,128]{2,1,0:T(8,128)S(1)}, f32[4,8,128]{2,1,0:T(8,128)S(1)}, f32[4,8,128]{2,1,0:T(8,128)S(1)}, f32[4,8,128]{2,1,0:T(8,128)S(1)}) custom-call(f32[4,8,8,128]{3,2,1,0:T(8,128)S(1)} %collective-permute-done.4.fresh_ref, f32[8,8,128]{2,1,0:T(8,128)S(1)} %get-tuple-element.30.refs_0_, f32[19,8,8,128]{3,2,1,0:T(8,128)S(1)} %get-tuple-element.31.refs_1_, ...), custom_call_target="tpu_custom_call" | custom-call | flops 30000000 | bytes 9584640 | tf_op jit(solution)/shard_map/stage_below/pallas_call | solution.py:503
  24.9 0.6 %collective-permute-start.6 = (f32[4,8,128]{2,1,0:T(8,128)S(1)}, f32[4,8,128]{2,1,0:T(8,128)S(1)}, u32[]{:S(2)}, u32[]{:S(2)}) collective-permute-start(f32[4,8,128]{2,1,0:T(8,128)S(1)} %get-tuple-element.47), channel_id=1, source_target_pairs={{0,8},{8,0},{16,24},{24,16},{1,9},{9,1},{17,25},{25,17},{2,10},{10... | collective-permute-start | bytes 49160 | tf_op jit(solution)/shard_map/ppermute | solution.py:570
  25.5 0.5 %collective-permute-start.7 = (f32[4,8,128]{2,1,0:T(8,128)S(1)}, f32[4,8,128]{2,1,0:T(8,128)S(1)}, u32[]{:S(2)}, u32[]{:S(2)}) collective-permute-start(f32[4,8,128]{2,1,0:T(8,128)S(1)} %get-tuple-element.48), channel_id=1, source_target_pairs={{0,16},{8,24},{16,0},{24,8},{1,17},{9,25},{17,1},{25,9},{2,18},{10... | collective-permute-start | bytes 49160 | tf_op jit(solution)/shard_map/ppermute | solution.py:570
  26.0 2.4 %collective-permute-start.8 = (f32[4,8,128]{2,1,0:T(8,128)S(1)}, f32[4,8,128]{2,1,0:T(8,128)S(1)}, u32[]{:S(2)}, u32[]{:S(2)}) collective-permute-start(f32[4,8,128]{2,1,0:T(8,128)S(1)} %get-tuple-element.49), channel_id=1, source_target_pairs={{0,24},{8,16},{16,8},{24,0},{1,25},{9,17},{17,9},{25,1},{2,26},{10... | collective-permute-start | bytes 49160 | tf_op jit(solution)/shard_map/ppermute | solution.py:570
  28.4 0.2 collective-permute-done.6.refs_1_
  28.7 0.5 %collective-permute-done.7.refs_2_ = f32[4,8,128]{2,1,0:T(8,128)S(1)} collective-permute-done((f32[4,8,128]{2,1,0:T(8,128)S(1)}, f32[4,8,128]{2,1,0:T(8,128)S(1)}, u32[]{:S(2)}, u32[]{:S(2)}) %collective-permute-start.7) | collective-permute-done | bytes 16416 | tf_op jit(solution)/shard_map/ppermute | solution.py:570
  29.2 1.4 %collective-permute-done.8.refs_3_ = f32[4,8,128]{2,1,0:T(8,128)S(1)} collective-permute-done((f32[4,8,128]{2,1,0:T(8,128)S(1)}, f32[4,8,128]{2,1,0:T(8,128)S(1)}, u32[]{:S(2)}, u32[]{:S(2)}) %collective-permute-start.8) | collective-permute-done | bytes 16416 | tf_op jit(solution)/shard_map/ppermute | solution.py:570
  30.6 0.8 %place_outputs.1 = (f32[4,8,128]{2,1,0:T(8,128)}, f32[3,4,8,128]{3,2,1,0:T(8,128)}) custom-call(f32[4,8,128]{2,1,0:T(8,128)S(1)} %get-tuple-element.46.refs_0_, f32[4,8,128]{2,1,0:T(8,128)S(1)} %collective-permute-done.6.refs_1_, f32[4,8,128]{2,1,0:T(8,128)S(1)} %collective-permute-done.7.refs_2_, f32[4,8,128]{2,1,0:T(8,128)S(1)} %collective-permute-done.8.refs_3_), custom_call_target="tpu_custom_call" | custom-call | tf_op jit(solution)/shard_map/place_outputs/pallas_call | solution.py:535
  (4 shorter events, 0.0 us)
Async XLA Ops:
  0.6 0.8 %copy-start = (f32[3,4,8,128]{3,2,1,0:T(8,128)S(1)}, f32[3,4,8,128]{3,2,1,0:T(8,128)}, u32[]{:S(2)}) copy-start(f32[3,4,8,128]{3,2,1,0:T(8,128)} %param.5) | copy-start | bytes 147460
  1.4 1.5 %collective-permute-start = (f32[5,4,8,128]{3,2,1,0:T(8,128)S(1)}, f32[5,4,8,128]{3,2,1,0:T(8,128)S(1)}, u32[]{:S(2)}, u32[]{:S(2)}) collective-permute-start(f32[5,4,8,128]{3,2,1,0:T(8,128)S(1)} %pad_maximum_fusion.v_ref), channel_id=1, source_target_pairs={{0,1},{1,0},{2,3},{3,2},{4,5},{5,4},{6,7},{7,6},{8,9},{9,8},{10,11... | collective-permute-start | bytes 245768 | tf_op jit(solution)/shard_map/ppermute | solution.py:556
  3.1 4.8 %collective-permute-start.1 = (f32[8,8,128]{2,1,0:T(8,128)S(1)}, f32[8,8,128]{2,1,0:T(8,128)S(1)}, u32[]{:S(2)}, u32[]{:S(2)}) collective-permute-start(f32[8,8,128]{2,1,0:T(8,128)S(1)} %get-tuple-element.27), channel_id=1, source_target_pairs={{0,8},{8,0},{16,24},{24,16},{1,9},{9,1},{17,25},{25,17},{2,10},{10... | collective-permute-start | bytes 98312 | tf_op jit(solution)/shard_map/ppermute | solution.py:561
  6.0 3.9 %collective-permute-start.2 = (f32[8,8,128]{2,1,0:T(8,128)S(1)}, f32[8,8,128]{2,1,0:T(8,128)S(1)}, u32[]{:S(2)}, u32[]{:S(2)}) collective-permute-start(f32[8,8,128]{2,1,0:T(8,128)S(1)} %get-tuple-element.28), channel_id=1, source_target_pairs={{0,16},{8,24},{16,0},{24,8},{1,17},{9,25},{17,1},{25,9},{2,18},{10... | collective-permute-start | bytes 98312 | tf_op jit(solution)/shard_map/ppermute | solution.py:561
  7.5 4.8 %collective-permute-start.3 = (f32[8,8,128]{2,1,0:T(8,128)S(1)}, f32[8,8,128]{2,1,0:T(8,128)S(1)}, u32[]{:S(2)}, u32[]{:S(2)}) collective-permute-start(f32[8,8,128]{2,1,0:T(8,128)S(1)} %get-tuple-element.29), channel_id=1, source_target_pairs={{0,24},{8,16},{16,8},{24,0},{1,25},{9,17},{17,9},{25,1},{2,26},{10... | collective-permute-start | bytes 98312 | tf_op jit(solution)/shard_map/ppermute | solution.py:561
  12.3 6.4 %collective-permute-start.5 = (f32[4,8,8,128]{3,2,1,0:T(8,128)S(1)}, f32[4,8,8,128]{3,2,1,0:T(8,128)S(1)}, u32[]{:S(2)}, u32[]{:S(2)}) collective-permute-start(f32[4,8,8,128]{3,2,1,0:T(8,128)S(1)} %join_slots.1.fresh_ref), channel_id=1, source_target_pairs={{0,6},{2,0},{4,2},{6,4},{1,7},{3,1},{5,3},{7,5},{8,14},{10,8},{12,... | collective-permute-start | bytes 393224 | tf_op jit(solution)/shard_map/ppermute | solution.py:564
  16.0 6.8 %collective-permute-start.4 = (f32[4,8,8,128]{3,2,1,0:T(8,128)S(1)}, f32[4,8,8,128]{3,2,1,0:T(8,128)S(1)}, u32[]{:S(2)}, u32[]{:S(2)}) collective-permute-start(f32[4,8,8,128]{3,2,1,0:T(8,128)S(1)} %join_slots.1.fresh_ref), channel_id=1, source_target_pairs={{0,2},{2,4},{4,6},{6,0},{1,3},{3,5},{5,7},{7,1},{8,10},{10,12},{12... | collective-permute-start | bytes 393224 | tf_op jit(solution)/shard_map/ppermute | solution.py:563
  24.9 3.8 %collective-permute-start.6 = (f32[4,8,128]{2,1,0:T(8,128)S(1)}, f32[4,8,128]{2,1,0:T(8,128)S(1)}, u32[]{:S(2)}, u32[]{:S(2)}) collective-permute-start(f32[4,8,128]{2,1,0:T(8,128)S(1)} %get-tuple-element.47), channel_id=1, source_target_pairs={{0,8},{8,0},{16,24},{24,16},{1,9},{9,1},{17,25},{25,17},{2,10},{10... | collective-permute-start | bytes 49160 | tf_op jit(solution)/shard_map/ppermute | solution.py:570
  25.5 3.7 %collective-permute-start.7 = (f32[4,8,128]{2,1,0:T(8,128)S(1)}, f32[4,8,128]{2,1,0:T(8,128)S(1)}, u32[]{:S(2)}, u32[]{:S(2)}) collective-permute-start(f32[4,8,128]{2,1,0:T(8,128)S(1)} %get-tuple-element.48), channel_id=1, source_target_pairs={{0,16},{8,24},{16,0},{24,8},{1,17},{9,25},{17,1},{25,9},{2,18},{10... | collective-permute-start | bytes 49160 | tf_op jit(solution)/shard_map/ppermute | solution.py:570
  26.0 4.6 %collective-permute-start.8 = (f32[4,8,128]{2,1,0:T(8,128)S(1)}, f32[4,8,128]{2,1,0:T(8,128)S(1)}, u32[]{:S(2)}, u32[]{:S(2)}) collective-permute-start(f32[4,8,128]{2,1,0:T(8,128)S(1)} %get-tuple-element.49), channel_id=1, source_target_pairs={{0,24},{8,16},{16,8},{24,0},{1,25},{9,17},{17,9},{25,1},{2,26},{10... | collective-permute-start | bytes 49160 | tf_op jit(solution)/shard_map/ppermute | solution.py:570

commit v7 on v6

--- a/solution.py
+++ b/solution.py
@@ -12,6 +12,7 @@
 HALO = 2 * STEPS
 LANES = 128
 
+LAG = 4
 AHEAD = 2
 
 
@@ -376,7 +377,7 @@
         scale = here * (1.0 / 36.0)
         return [scale * value for value in (fx, fy, fz)]
 
-    def run(self, stage, held, raw, force_ref, fresh, k):
+    def run(self, stage, held, raw, force_ref, fresh, k, finish):
         sh = self.sh
         table = {other: self.buffers(other) for other in STAGES}
 
@@ -410,41 +411,68 @@
             ref, row = at(owner, ("f", s), y)
             return ref[i, row]
 
-        self.unpack(raw, fresh, k)
-        first, last = self.inputs(stage)
-        for n in range(sh.y):
+        def begin(y):
+            n = y - self.inputs(stage)[0]
             rho, ux, uy, uz, wall = (raw[v, pl.ds(n, sh.subs, stride=sh.y), :] for v in range(5))
             held[stage, ("solid",)][n] = wall
             for i, row in enumerate(equilibrium(rho, [ux, uy, uz])):
                 held[stage, ("f", 0)][i, n] = row
 
+        def weigh(s, y):
+            rows = [f(s, i, y) for i in range(19)]
+            psi = potential(sum(rows[1:], rows[0]))
+            to = held[stage, ("psi", s)]
+            to[y - self.weighed(stage, s)[0]] = jnp.where(solid(y), WALL_POTENTIAL, psi)
+
+        def form(s, y):
+            for n, value in enumerate(self.push(psi_of(s), y)):
+                force_ref[s, n, y] = value
+
+        def advance(s, y):
+            force = [force_ref[s, axis, y] for axis in range(3)]
+            post = collide([f(s, i, y) for i in range(19)], force, solid(y))
+            base = self.collided(stage, s)[0] - 1
+            for i in range(19):
+                cx, cy, cz = (int(c) for c in C[i])
+                held[stage, ("f", s + 1)][i, y + cy - base] = self.shifted(post[i], cx, cz)
+
+        self.unpack(raw, fresh, k)
+        if stage == STAGES[-1]:
+            count = sh.y
+
+            def at_tick(tick):
+                items = [(s, self.own + 2 * s - (tick - LAG * s)) for s in range(STEPS)]
+                return [(s, y) for s, y in items if 0 <= tick - LAG * s < count]
+
+            for tick in range(-1, count + LAG * (STEPS - 1)):
+                for s, y in at_tick(tick + 1):
+                    if s == 0:
+                        begin(y - 1)
+                    weigh(s, y - 1)
+                    form(s, y)
+                for s, y in at_tick(tick):
+                    advance(s, y)
+                row = self.end - 1 - (tick - LAG * (STEPS - 1) - 1)
+                if self.own <= row < self.end:
+                    finish(f, solid, row)
+            finish(f, solid, self.own)
+            return
+
+        first, last = self.inputs(stage)
+        for y in range(first, last + 1):
+            begin(y)
         for s in self.steps(stage):
             first, last = self.weighed(stage, s)
             for y in range(first, last + 1):
-                rows = [f(s, i, y) for i in range(19)]
-                held[stage, ("psi", s)][y - first] = jnp.where(
-                    solid(y), WALL_POTENTIAL, potential(sum(rows[1:], rows[0]))
-                )
+                weigh(s, y)
             first, last = self.collided(stage, s)
-            psi, ys = psi_of(s), list(range(first, last + 1))
-
-            def form(y, psi=psi):
-                for n, value in enumerate(self.push(psi, y)):
-                    force_ref[n, y] = value
-
+            ys = list(range(first, last + 1))
             for y in ys[:AHEAD]:
-                form(y)
+                form(s, y)
             for n, y in enumerate(ys):
-                force = [force_ref[axis, y] for axis in range(3)]
-                post = collide([f(s, i, y) for i in range(19)], force, solid(y))
+                advance(s, y)
                 if n + AHEAD < len(ys):
-                    form(ys[n + AHEAD])
-                for i in range(19):
-                    cx, cy, cz = (int(c) for c in C[i])
-                    held[stage, ("f", s + 1)][i, y + cy - (first - 1)] = self.shifted(
-                        post[i], cx, cz
-                    )
-        return f, solid
+                    form(s, ys[n + AHEAD])
 
 
 def run_stage(stage, fresh, left, sh, flops):
@@ -464,17 +492,19 @@
         raw, force_ref, done = refs[len(own) :]
         k = lax.axis_index("gx")
         low = Rows(sh)
-        f, solid = low.run(stage, held, raw, force_ref, fresh_ref, k)
-        if not last_stage:
-            return
-        for n in range(sh.y):
-            y = low.own + n
+
+        def finish(f, solid, y):
             g = [f(STEPS, i, y) for i in range(19)]
             rho, wall = sum(g[1:], g[0]), solid(y)
             inverse = math.sqrt(3.0) / rho
             results = [rho * (1.0 / LIQUID)] + [c * inverse for c in moments(g)]
             for v, value in enumerate(results):
-                done[v, pl.ds(n, sh.subs, stride=sh.y), :] = jnp.where(wall, 0.0, value)
+                at = pl.ds(y - low.own, sh.subs, stride=sh.y)
+                done[v, at, :] = jnp.where(wall, 0.0, value)
+
+        low.run(stage, held, raw, force_ref, fresh_ref, k, finish)
+        if not last_stage:
+            return
         lane = lax.broadcasted_iota(jnp.int32, (sh.y, LANES), 1)
         place = (lane % sh.width) // sh.slab
         for slot, out in enumerate(outs):
@@ -492,7 +522,7 @@
     scratch = [pltpu.VMEM(shape, jnp.float32) for shape in shapes]
     extra = [
         pltpu.VMEM((5, sh.subs * sh.y, LANES), jnp.float32),
-        pltpu.VMEM((3, sh.rows, sh.subs, LANES), jnp.float32),
+        pltpu.VMEM((STEPS, 3, sh.rows, sh.subs, LANES), jnp.float32),
         pltpu.VMEM((4, sh.subs * sh.y, LANES), jnp.float32),
     ]
     outs = [jax.ShapeDtypeStruct(shape, jnp.float32) for shape in shapes]

time: 31.6 us -> 31.4 us (level)
  no operation moved by 1% of the time
where the time goes in v7:
time: 31.4 us; the launch traced here: 31.2 us
  starting transfers between devices  12.2 us (39%)
  waiting for transfers between devices  12 us (38%)
  Pallas kernels  5.55 us (18%)
  other arithmetic  0.78 us (2%)
  between operations  0.67 us (2%)
    ppermute x3, waiting for transfers between devices, on_device(): got.append(lax.ppermute(slabs[slot], 'gx', sh.perm(slot)))  4.79 us
    pallas_call x3, Pallas kernels, run_stage(): pl.pallas_call(body, name='stage_' + stage, out_shape=outs, in_specs=vmem...  4.6 us
    ppermute x3, starting transfers between devices, on_device(): got.append(lax.ppermute(slabs[slot], 'gx', sh.perm(slot)))  4.43 us
    ppermute x1, starting transfers between devices, on_device(): above = lax.ppermute(middle, 'gy', ring(sh.ny, -1))  3.65 us
    ppermute x3, starting transfers between devices, on_device(): back.append(lax.ppermute(pieces[slot], 'gx', sh.perm(slot)))  3.55 us
    ppermute x1, waiting for transfers between devices, on_device(): below = lax.ppermute(middle, 'gy', ring(sh.ny, 1))  2.21 us
    ppermute x3, waiting for transfers between devices, on_device(): back.append(lax.ppermute(pieces[slot], 'gx', sh.perm(slot)))  2.19 us
    ppermute x1, waiting for transfers between devices, on_device(): above = lax.ppermute(middle, 'gy', ring(sh.ny, -1))  1.92 us
  transfers between devices with their start and end apart: 9, of which 9 were waited for; matrix products, arithmetic and copies ran while one was open for 0% of the time, Pallas kernels for 8%

profile of v7, /device:TPU:0, one launch (start us, length us, event | category | flops | bytes accessed | tf_op | source)
XLA Modules:
  0.0 31.2 jit_solution(12649919975892618199)
XLA Ops:
  0.6 0.8 %select_bitcast_fusion = (f32[1,4,8,128]{3,2,1,0:T(8,128)S(1)}, f32[1,4,8,128]{3,2,1,0:T(8,128)S(1)}) fusion(s32[4,8,128]{2,1,0:T(8,128)} %param.7, f32[4,8,128]{2,1,0:T(8,128)} %param.4, s32[4,8,128]{2,1,0:T(8,128)} %param.6), kind=kLoop, calls=%fused_computation.1 | loop fusion | flops 20480 | bytes 81920 | tf_op jit(solution)/shard_map/broadcast_in_dim | solution.py:251
  1.4 0.0 copy-done
  1.4 0.5 %collective-permute-start = (f32[5,4,8,128]{3,2,1,0:T(8,128)S(1)}, f32[5,4,8,128]{3,2,1,0:T(8,128)S(1)}, u32[]{:S(2)}, u32[]{:S(2)}) collective-permute-start(f32[5,4,8,128]{3,2,1,0:T(8,128)S(1)} %pad_maximum_fusion.v_ref), channel_id=1, source_target_pairs={{0,1},{1,0},{2,3},{3,2},{4,5},{5,4},{6,7},{7,6},{8,9},{9,8},{10,11... | collective-permute-start | bytes 245768 | tf_op jit(solution)/shard_map/ppermute | solution.py:586
  2.0 0.9 %collective-permute-done.b_ref.a_ref = f32[5,4,8,128]{3,2,1,0:T(8,128)S(1)} collective-permute-done((f32[5,4,8,128]{3,2,1,0:T(8,128)S(1)}, f32[5,4,8,128]{3,2,1,0:T(8,128)S(1)}, u32[]{:S(2)}, u32[]{:S(2)}) %collective-permute-start) | collective-permute-done | bytes 81952 | tf_op jit(solution)/shard_map/ppermute | solution.py:586
  2.9 0.2 cut_slabs.1
  3.1 2.9 %collective-permute-start.1 = (f32[8,8,128]{2,1,0:T(8,128)S(1)}, f32[8,8,128]{2,1,0:T(8,128)S(1)}, u32[]{:S(2)}, u32[]{:S(2)}) collective-permute-start(f32[8,8,128]{2,1,0:T(8,128)S(1)} %get-tuple-element.27), channel_id=1, source_target_pairs={{0,8},{8,0},{16,24},{24,16},{1,9},{9,1},{17,25},{25,17},{2,10},{10... | collective-permute-start | bytes 98312 | tf_op jit(solution)/shard_map/ppermute | solution.py:591
  6.0 1.5 %collective-permute-start.2 = (f32[8,8,128]{2,1,0:T(8,128)S(1)}, f32[8,8,128]{2,1,0:T(8,128)S(1)}, u32[]{:S(2)}, u32[]{:S(2)}) collective-permute-start(f32[8,8,128]{2,1,0:T(8,128)S(1)} %get-tuple-element.28), channel_id=1, source_target_pairs={{0,16},{8,24},{16,0},{24,8},{1,17},{9,25},{17,1},{25,9},{2,18},{10... | collective-permute-start | bytes 98312 | tf_op jit(solution)/shard_map/ppermute | solution.py:591
  7.5 0.0 collective-permute-start.3
  7.5 0.4 %collective-permute-done.1.refs_1_ = f32[8,8,128]{2,1,0:T(8,128)S(1)} collective-permute-done((f32[8,8,128]{2,1,0:T(8,128)S(1)}, f32[8,8,128]{2,1,0:T(8,128)S(1)}, u32[]{:S(2)}, u32[]{:S(2)}) %collective-permute-start.1) | collective-permute-done | bytes 32800 | tf_op jit(solution)/shard_map/ppermute | solution.py:591
  7.9 2.0 %collective-permute-done.2.refs_2_ = f32[8,8,128]{2,1,0:T(8,128)S(1)} collective-permute-done((f32[8,8,128]{2,1,0:T(8,128)S(1)}, f32[8,8,128]{2,1,0:T(8,128)S(1)}, u32[]{:S(2)}, u32[]{:S(2)}) %collective-permute-start.2) | collective-permute-done | bytes 32800 | tf_op jit(solution)/shard_map/ppermute | solution.py:591
  9.9 2.4 %collective-permute-done.3.refs_3_ = f32[8,8,128]{2,1,0:T(8,128)S(1)} collective-permute-done((f32[8,8,128]{2,1,0:T(8,128)S(1)}, f32[8,8,128]{2,1,0:T(8,128)S(1)}, u32[]{:S(2)}, u32[]{:S(2)}) %collective-permute-start.3) | collective-permute-done | bytes 32800 | tf_op jit(solution)/shard_map/ppermute | solution.py:591
  12.3 3.7 %collective-permute-start.5 = (f32[4,8,8,128]{3,2,1,0:T(8,128)S(1)}, f32[4,8,8,128]{3,2,1,0:T(8,128)S(1)}, u32[]{:S(2)}, u32[]{:S(2)}) collective-permute-start(f32[4,8,8,128]{3,2,1,0:T(8,128)S(1)} %join_slots.1.fresh_ref), channel_id=1, source_target_pairs={{0,6},{2,0},{4,2},{6,4},{1,7},{3,1},{5,3},{7,5},{8,14},{10,8},{12,... | collective-permute-start | bytes 393224 | tf_op jit(solution)/shard_map/ppermute | solution.py:594
  16.0 0.8 %stage_own.1 = (f32[8,8,128]{2,1,0:T(8,128)S(1)}, f32[19,8,8,128]{3,2,1,0:T(8,128)S(1)}, f32[8,8,128]{2,1,0:T(8,128)S(1)}, f32[19,8,8,128]{3,2,1,0:T(8,128)S(1)}...) custom-call(f32[4,8,8,128]{3,2,1,0:T(8,128)S(1)} %join_slots.1.fresh_ref), custom_call_target="tpu_custom_call" | custom-call | flops 5000000 | bytes 3244032 | tf_op jit(solution)/shard_map/stage_own/pallas_call | solution.py:533
  16.8 1.9 %collective-permute-done.5.fresh_ref = f32[4,8,8,128]{3,2,1,0:T(8,128)S(1)} collective-permute-done((f32[4,8,8,128]{3,2,1,0:T(8,128)S(1)}, f32[4,8,8,128]{3,2,1,0:T(8,128)S(1)}, u32[]{:S(2)}, u32[]{:S(2)}) %collective-permute-start.5) | collective-permute-done | bytes 131104 | tf_op jit(solution)/shard_map/ppermute | solution.py:594
  18.7 1.8 %stage_above.1 = (f32[8,8,128]{2,1,0:T(8,128)S(1)}, f32[19,8,8,128]{3,2,1,0:T(8,128)S(1)}, f32[8,8,128]{2,1,0:T(8,128)S(1)}, f32[19,10,8,128]{3,2,1,0:T(8,128)S(...) custom-call(f32[4,8,8,128]{3,2,1,0:T(8,128)S(1)} %collective-permute, ...), custom_call_target="tpu_custom_call" | custom-call | flops 20000000 | bytes 6504448 | tf_op jit(solution)/shard_map/stage_above/pallas_call | solution.py:533
  20.5 2.2 %collective-permute-done.4.fresh_ref = f32[4,8,8,128]{3,2,1,0:T(8,128)S(1)} collective-permute-done((f32[4,8,8,128]{3,2,1,0:T(8,128)S(1)}, f32[4,8,8,128]{3,2,1,0:T(8,128)S(1)}, u32[]{:S(2)}, u32[]{:S(2)}) %collective-permute-start.4) | collective-permute-done | bytes 131104 | tf_op jit(solution)/shard_map/ppermute | solution.py:593
  22.7 2.0 %stage_below.1 = (f32[4,8,128]{2,1,0:T(8,128)S(1)}, f32[4,8,128]{2,1,0:T(8,128)S(1)}, f32[4,8,128]{2,1,0:T(8,128)S(1)}, f32[4,8,128]{2,1,0:T(8,128)S(1)}) custom-call(f32[4,8,8,128]{3,2,1,0:T(8,128)S(1)} %collective-permute-done.4.fresh_ref, f32[8,8,128]{2,1,0:T(8,128)S(1)} %get-tuple-element.30.refs_0_, f32[19,8,8,128]{3,2,1,0:T(8,128)S(1)} %get-tuple-element.31.refs_1_, ...), custom_call_target="tpu_custom_call" | custom-call | flops 30000000 | bytes 10469376 | tf_op jit(solution)/shard_map/stage_below/pallas_call | solution.py:533
  24.7 0.6 %collective-permute-start.6 = (f32[4,8,128]{2,1,0:T(8,128)S(1)}, f32[4,8,128]{2,1,0:T(8,128)S(1)}, u32[]{:S(2)}, u32[]{:S(2)}) collective-permute-start(f32[4,8,128]{2,1,0:T(8,128)S(1)} %get-tuple-element.47), channel_id=1, source_target_pairs={{0,8},{8,0},{16,24},{24,16},{1,9},{9,1},{17,25},{25,17},{2,10},{10... | collective-permute-start | bytes 49160 | tf_op jit(solution)/shard_map/ppermute | solution.py:600
  25.3 0.5 %collective-permute-start.7 = (f32[4,8,128]{2,1,0:T(8,128)S(1)}, f32[4,8,128]{2,1,0:T(8,128)S(1)}, u32[]{:S(2)}, u32[]{:S(2)}) collective-permute-start(f32[4,8,128]{2,1,0:T(8,128)S(1)} %get-tuple-element.48), channel_id=1, source_target_pairs={{0,16},{8,24},{16,0},{24,8},{1,17},{9,25},{17,1},{25,9},{2,18},{10... | collective-permute-start | bytes 49160 | tf_op jit(solution)/shard_map/ppermute | solution.py:600
  25.8 2.4 %collective-permute-start.8 = (f32[4,8,128]{2,1,0:T(8,128)S(1)}, f32[4,8,128]{2,1,0:T(8,128)S(1)}, u32[]{:S(2)}, u32[]{:S(2)}) collective-permute-start(f32[4,8,128]{2,1,0:T(8,128)S(1)} %get-tuple-element.49), channel_id=1, source_target_pairs={{0,24},{8,16},{16,8},{24,0},{1,25},{9,17},{17,9},{25,1},{2,26},{10... | collective-permute-start | bytes 49160 | tf_op jit(solution)/shard_map/ppermute | solution.py:600
  28.3 0.2 collective-permute-done.6.refs_1_
  28.5 0.5 %collective-permute-done.7.refs_2_ = f32[4,8,128]{2,1,0:T(8,128)S(1)} collective-permute-done((f32[4,8,128]{2,1,0:T(8,128)S(1)}, f32[4,8,128]{2,1,0:T(8,128)S(1)}, u32[]{:S(2)}, u32[]{:S(2)}) %collective-permute-start.7) | collective-permute-done | bytes 16416 | tf_op jit(solution)/shard_map/ppermute | solution.py:600
  29.1 1.4 %collective-permute-done.8.refs_3_ = f32[4,8,128]{2,1,0:T(8,128)S(1)} collective-permute-done((f32[4,8,128]{2,1,0:T(8,128)S(1)}, f32[4,8,128]{2,1,0:T(8,128)S(1)}, u32[]{:S(2)}, u32[]{:S(2)}) %collective-permute-start.8) | collective-permute-done | bytes 16416 | tf_op jit(solution)/shard_map/ppermute | solution.py:600
  30.5 0.8 %place_outputs.1 = (f32[4,8,128]{2,1,0:T(8,128)}, f32[3,4,8,128]{3,2,1,0:T(8,128)}) custom-call(f32[4,8,128]{2,1,0:T(8,128)S(1)} %get-tuple-element.46.refs_0_, f32[4,8,128]{2,1,0:T(8,128)S(1)} %collective-permute-done.6.refs_1_, f32[4,8,128]{2,1,0:T(8,128)S(1)} %collective-permute-done.7.refs_2_, f32[4,8,128]{2,1,0:T(8,128)S(1)} %collective-permute-done.8.refs_3_), custom_call_target="tpu_custom_call" | custom-call | tf_op jit(solution)/shard_map/place_outputs/pallas_call | solution.py:565
  (4 shorter events, 0.0 us)
Async XLA Ops:
  0.6 0.8 %copy-start = (f32[3,4,8,128]{3,2,1,0:T(8,128)S(1)}, f32[3,4,8,128]{3,2,1,0:T(8,128)}, u32[]{:S(2)}) copy-start(f32[3,4,8,128]{3,2,1,0:T(8,128)} %param.5) | copy-start | bytes 147460
  1.4 1.5 %collective-permute-start = (f32[5,4,8,128]{3,2,1,0:T(8,128)S(1)}, f32[5,4,8,128]{3,2,1,0:T(8,128)S(1)}, u32[]{:S(2)}, u32[]{:S(2)}) collective-permute-start(f32[5,4,8,128]{3,2,1,0:T(8,128)S(1)} %pad_maximum_fusion.v_ref), channel_id=1, source_target_pairs={{0,1},{1,0},{2,3},{3,2},{4,5},{5,4},{6,7},{7,6},{8,9},{9,8},{10,11... | collective-permute-start | bytes 245768 | tf_op jit(solution)/shard_map/ppermute | solution.py:586
  3.1 4.8 %collective-permute-start.1 = (f32[8,8,128]{2,1,0:T(8,128)S(1)}, f32[8,8,128]{2,1,0:T(8,128)S(1)}, u32[]{:S(2)}, u32[]{:S(2)}) collective-permute-start(f32[8,8,128]{2,1,0:T(8,128)S(1)} %get-tuple-element.27), channel_id=1, source_target_pairs={{0,8},{8,0},{16,24},{24,16},{1,9},{9,1},{17,25},{25,17},{2,10},{10... | collective-permute-start | bytes 98312 | tf_op jit(solution)/shard_map/ppermute | solution.py:591
  6.0 3.9 %collective-permute-start.2 = (f32[8,8,128]{2,1,0:T(8,128)S(1)}, f32[8,8,128]{2,1,0:T(8,128)S(1)}, u32[]{:S(2)}, u32[]{:S(2)}) collective-permute-start(f32[8,8,128]{2,1,0:T(8,128)S(1)} %get-tuple-element.28), channel_id=1, source_target_pairs={{0,16},{8,24},{16,0},{24,8},{1,17},{9,25},{17,1},{25,9},{2,18},{10... | collective-permute-start | bytes 98312 | tf_op jit(solution)/shard_map/ppermute | solution.py:591
  7.5 4.8 %collective-permute-start.3 = (f32[8,8,128]{2,1,0:T(8,128)S(1)}, f32[8,8,128]{2,1,0:T(8,128)S(1)}, u32[]{:S(2)}, u32[]{:S(2)}) collective-permute-start(f32[8,8,128]{2,1,0:T(8,128)S(1)} %get-tuple-element.29), channel_id=1, source_target_pairs={{0,24},{8,16},{16,8},{24,0},{1,25},{9,17},{17,9},{25,1},{2,26},{10... | collective-permute-start | bytes 98312 | tf_op jit(solution)/shard_map/ppermute | solution.py:591
  12.3 6.4 %collective-permute-start.5 = (f32[4,8,8,128]{3,2,1,0:T(8,128)S(1)}, f32[4,8,8,128]{3,2,1,0:T(8,128)S(1)}, u32[]{:S(2)}, u32[]{:S(2)}) collective-permute-start(f32[4,8,8,128]{3,2,1,0:T(8,128)S(1)} %join_slots.1.fresh_ref), channel_id=1, source_target_pairs={{0,6},{2,0},{4,2},{6,4},{1,7},{3,1},{5,3},{7,5},{8,14},{10,8},{12,... | collective-permute-start | bytes 393224 | tf_op jit(solution)/shard_map/ppermute | solution.py:594
  16.0 6.8 %collective-permute-start.4 = (f32[4,8,8,128]{3,2,1,0:T(8,128)S(1)}, f32[4,8,8,128]{3,2,1,0:T(8,128)S(1)}, u32[]{:S(2)}, u32[]{:S(2)}) collective-permute-start(f32[4,8,8,128]{3,2,1,0:T(8,128)S(1)} %join_slots.1.fresh_ref), channel_id=1, source_target_pairs={{0,2},{2,4},{4,6},{6,0},{1,3},{3,5},{5,7},{7,1},{8,10},{10,12},{12... | collective-permute-start | bytes 393224 | tf_op jit(solution)/shard_map/ppermute | solution.py:593
  24.7 3.8 %collective-permute-start.6 = (f32[4,8,128]{2,1,0:T(8,128)S(1)}, f32[4,8,128]{2,1,0:T(8,128)S(1)}, u32[]{:S(2)}, u32[]{:S(2)}) collective-permute-start(f32[4,8,128]{2,1,0:T(8,128)S(1)} %get-tuple-element.47), channel_id=1, source_target_pairs={{0,8},{8,0},{16,24},{24,16},{1,9},{9,1},{17,25},{25,17},{2,10},{10... | collective-permute-start | bytes 49160 | tf_op jit(solution)/shard_map/ppermute | solution.py:600
  25.3 3.7 %collective-permute-start.7 = (f32[4,8,128]{2,1,0:T(8,128)S(1)}, f32[4,8,128]{2,1,0:T(8,128)S(1)}, u32[]{:S(2)}, u32[]{:S(2)}) collective-permute-start(f32[4,8,128]{2,1,0:T(8,128)S(1)} %get-tuple-element.48), channel_id=1, source_target_pairs={{0,16},{8,24},{16,0},{24,8},{1,17},{9,25},{17,1},{25,9},{2,18},{10... | collective-permute-start | bytes 49160 | tf_op jit(solution)/shard_map/ppermute | solution.py:600
  25.8 4.6 %collective-permute-start.8 = (f32[4,8,128]{2,1,0:T(8,128)S(1)}, f32[4,8,128]{2,1,0:T(8,128)S(1)}, u32[]{:S(2)}, u32[]{:S(2)}) collective-permute-start(f32[4,8,128]{2,1,0:T(8,128)S(1)} %get-tuple-element.49), channel_id=1, source_target_pairs={{0,24},{8,16},{16,8},{24,0},{1,25},{9,17},{17,9},{25,1},{2,26},{10... | collective-permute-start | bytes 49160 | tf_op jit(solution)/shard_map/ppermute | solution.py:600

commit v8 on v7

--- a/solution.py
+++ b/solution.py
@@ -211,10 +211,11 @@
         if self.nx & (self.nx - 1) == 0:
             self.peer = lambda k, slot: jnp.bitwise_xor(k, slot)
             self.perm = lambda slot: [(i, i ^ slot) for i in range(self.nx)]
-            self.sender = self.peer
+            self.sender = self.slot_of = self.peer
         else:
             self.peer = lambda k, slot: lax.rem(k + slot, self.nx)
             self.sender = lambda k, slot: lax.rem(k + self.nx - slot, self.nx)
+            self.slot_of = self.sender
             self.perm = lambda slot: [(i, (i + slot) % self.nx) for i in range(self.nx)]
 
     def window(self, n, x):
@@ -353,14 +354,15 @@
             turn = (x % 2 * sh.width - off) % LANES
             return pltpu.roll(value, turn, 1) if turn else value
 
-        for slot in range(sh.nx):
-            base = sh.sender(k, slot) * (sh.own * sh.y)
-            for n in range(5):
+        slots = [sh.slot_of(k, q) for q in range(sh.nx)]
+        for n in range(5):
+            for q, slot in enumerate(slots):
                 for m in range(sh.own):
                     value = jnp.where(
                         wide < sh.width, plane(slot, n, 2 * m), plane(slot, n, 2 * m + 1)
                     )
-                    raw[n, pl.ds(pl.multiple_of(base + m * sh.y, 8), sh.y), :] = value
+                    at = (q * sh.own + m) * sh.y
+                    raw[n, at : at + sh.y, :] = value
 
     def push(self, psi, y):
         shifted = self.shifted

time: 31.4 us -> 31.4 us (level)
  transfers between devices with their start and end apart: 9 -> 9, of which waited for: 9 -> 9; matrix products, arithmetic and copies ran while one was open for 0% -> 0% of each run, Pallas kernels for 8% -> 9%
where the time goes in v8:
time: 31.4 us; the launch traced here: 31.2 us
  starting transfers between devices  12.2 us (39%)
  waiting for transfers between devices  12 us (38%)
  Pallas kernels  5.6 us (18%)
  other arithmetic  0.78 us (2%)
  between operations  0.68 us (2%)
    ppermute x3, waiting for transfers between devices, on_device(): got.append(lax.ppermute(slabs[slot], 'gx', sh.perm(slot)))  4.79 us
    pallas_call x3, Pallas kernels, run_stage(): pl.pallas_call(body, name='stage_' + stage, out_shape=outs, in_specs=vmem...  4.65 us
    ppermute x3, starting transfers between devices, on_device(): got.append(lax.ppermute(slabs[slot], 'gx', sh.perm(slot)))  4.43 us
    ppermute x1, starting transfers between devices, on_device(): above = lax.ppermute(middle, 'gy', ring(sh.ny, -1))  3.65 us
    ppermute x3, starting transfers between devices, on_device(): back.append(lax.ppermute(pieces[slot], 'gx', sh.perm(slot)))  3.55 us
    ppermute x1, waiting for transfers between devices, on_device(): below = lax.ppermute(middle, 'gy', ring(sh.ny, 1))  2.21 us
    ppermute x3, waiting for transfers between devices, on_device(): back.append(lax.ppermute(pieces[slot], 'gx', sh.perm(slot)))  2.19 us
    ppermute x1, waiting for transfers between devices, on_device(): above = lax.ppermute(middle, 'gy', ring(sh.ny, -1))  1.86 us
  transfers between devices with their start and end apart: 9, of which 9 were waited for; matrix products, arithmetic and copies ran while one was open for 0% of the time, Pallas kernels for 9%

profile of v8, /device:TPU:0, one launch (start us, length us, event | category | flops | bytes accessed | tf_op | source)
XLA Modules:
  0.0 31.2 jit_solution(10310568560492522453)
XLA Ops:
  0.6 0.8 %select_bitcast_fusion = (f32[1,4,8,128]{3,2,1,0:T(8,128)S(1)}, f32[1,4,8,128]{3,2,1,0:T(8,128)S(1)}) fusion(s32[4,8,128]{2,1,0:T(8,128)} %param.7, f32[4,8,128]{2,1,0:T(8,128)} %param.4, s32[4,8,128]{2,1,0:T(8,128)} %param.6), kind=kLoop, calls=%fused_computation.1 | loop fusion | flops 20480 | bytes 81920 | tf_op jit(solution)/shard_map/broadcast_in_dim | solution.py:252
  1.4 0.0 copy-done
  1.4 0.5 %collective-permute-start = (f32[5,4,8,128]{3,2,1,0:T(8,128)S(1)}, f32[5,4,8,128]{3,2,1,0:T(8,128)S(1)}, u32[]{:S(2)}, u32[]{:S(2)}) collective-permute-start(f32[5,4,8,128]{3,2,1,0:T(8,128)S(1)} %pad_maximum_fusion.v_ref), channel_id=1, source_target_pairs={{0,1},{1,0},{2,3},{3,2},{4,5},{5,4},{6,7},{7,6},{8,9},{9,8},{10,11... | collective-permute-start | bytes 245768 | tf_op jit(solution)/shard_map/ppermute | solution.py:588
  2.0 0.9 %collective-permute-done.b_ref.a_ref = f32[5,4,8,128]{3,2,1,0:T(8,128)S(1)} collective-permute-done((f32[5,4,8,128]{3,2,1,0:T(8,128)S(1)}, f32[5,4,8,128]{3,2,1,0:T(8,128)S(1)}, u32[]{:S(2)}, u32[]{:S(2)}) %collective-permute-start) | collective-permute-done | bytes 81952 | tf_op jit(solution)/shard_map/ppermute | solution.py:588
  2.9 0.2 cut_slabs.1
  3.1 2.9 %collective-permute-start.1 = (f32[8,8,128]{2,1,0:T(8,128)S(1)}, f32[8,8,128]{2,1,0:T(8,128)S(1)}, u32[]{:S(2)}, u32[]{:S(2)}) collective-permute-start(f32[8,8,128]{2,1,0:T(8,128)S(1)} %get-tuple-element.27), channel_id=1, source_target_pairs={{0,8},{8,0},{16,24},{24,16},{1,9},{9,1},{17,25},{25,17},{2,10},{10... | collective-permute-start | bytes 98312 | tf_op jit(solution)/shard_map/ppermute | solution.py:593
  6.0 1.5 %collective-permute-start.2 = (f32[8,8,128]{2,1,0:T(8,128)S(1)}, f32[8,8,128]{2,1,0:T(8,128)S(1)}, u32[]{:S(2)}, u32[]{:S(2)}) collective-permute-start(f32[8,8,128]{2,1,0:T(8,128)S(1)} %get-tuple-element.28), channel_id=1, source_target_pairs={{0,16},{8,24},{16,0},{24,8},{1,17},{9,25},{17,1},{25,9},{2,18},{10... | collective-permute-start | bytes 98312 | tf_op jit(solution)/shard_map/ppermute | solution.py:593
  7.5 0.0 collective-permute-start.3
  7.5 0.4 %collective-permute-done.1.refs_1_ = f32[8,8,128]{2,1,0:T(8,128)S(1)} collective-permute-done((f32[8,8,128]{2,1,0:T(8,128)S(1)}, f32[8,8,128]{2,1,0:T(8,128)S(1)}, u32[]{:S(2)}, u32[]{:S(2)}) %collective-permute-start.1) | collective-permute-done | bytes 32800 | tf_op jit(solution)/shard_map/ppermute | solution.py:593
  7.9 2.0 %collective-permute-done.2.refs_2_ = f32[8,8,128]{2,1,0:T(8,128)S(1)} collective-permute-done((f32[8,8,128]{2,1,0:T(8,128)S(1)}, f32[8,8,128]{2,1,0:T(8,128)S(1)}, u32[]{:S(2)}, u32[]{:S(2)}) %collective-permute-start.2) | collective-permute-done | bytes 32800 | tf_op jit(solution)/shard_map/ppermute | solution.py:593
  9.9 2.4 %collective-permute-done.3.refs_3_ = f32[8,8,128]{2,1,0:T(8,128)S(1)} collective-permute-done((f32[8,8,128]{2,1,0:T(8,128)S(1)}, f32[8,8,128]{2,1,0:T(8,128)S(1)}, u32[]{:S(2)}, u32[]{:S(2)}) %collective-permute-start.3) | collective-permute-done | bytes 32800 | tf_op jit(solution)/shard_map/ppermute | solution.py:593
  12.3 3.7 %collective-permute-start.5 = (f32[4,8,8,128]{3,2,1,0:T(8,128)S(1)}, f32[4,8,8,128]{3,2,1,0:T(8,128)S(1)}, u32[]{:S(2)}, u32[]{:S(2)}) collective-permute-start(f32[4,8,8,128]{3,2,1,0:T(8,128)S(1)} %join_slots.1.fresh_ref), channel_id=1, source_target_pairs={{0,6},{2,0},{4,2},{6,4},{1,7},{3,1},{5,3},{7,5},{8,14},{10,8},{12,... | collective-permute-start | bytes 393224 | tf_op jit(solution)/shard_map/ppermute | solution.py:596
  16.0 0.9 %stage_own.1 = (f32[8,8,128]{2,1,0:T(8,128)S(1)}, f32[19,8,8,128]{3,2,1,0:T(8,128)S(1)}, f32[8,8,128]{2,1,0:T(8,128)S(1)}, f32[19,8,8,128]{3,2,1,0:T(8,128)S(1)}...) custom-call(f32[4,8,8,128]{3,2,1,0:T(8,128)S(1)} %join_slots.1.fresh_ref), custom_call_target="tpu_custom_call" | custom-call | flops 5000000 | bytes 3244032 | tf_op jit(solution)/shard_map/stage_own/pallas_call | solution.py:535
  16.9 1.9 %collective-permute-done.5.fresh_ref = f32[4,8,8,128]{3,2,1,0:T(8,128)S(1)} collective-permute-done((f32[4,8,8,128]{3,2,1,0:T(8,128)S(1)}, f32[4,8,8,128]{3,2,1,0:T(8,128)S(1)}, u32[]{:S(2)}, u32[]{:S(2)}) %collective-permute-start.5) | collective-permute-done | bytes 131104 | tf_op jit(solution)/shard_map/ppermute | solution.py:596
  18.7 1.8 %stage_above.1 = (f32[8,8,128]{2,1,0:T(8,128)S(1)}, f32[19,8,8,128]{3,2,1,0:T(8,128)S(1)}, f32[8,8,128]{2,1,0:T(8,128)S(1)}, f32[19,10,8,128]{3,2,1,0:T(8,128)S(...) custom-call(f32[4,8,8,128]{3,2,1,0:T(8,128)S(1)} %collective-permute, ...), custom_call_target="tpu_custom_call" | custom-call | flops 20000000 | bytes 6504448 | tf_op jit(solution)/shard_map/stage_above/pallas_call | solution.py:535
  20.5 2.2 %collective-permute-done.4.fresh_ref = f32[4,8,8,128]{3,2,1,0:T(8,128)S(1)} collective-permute-done((f32[4,8,8,128]{3,2,1,0:T(8,128)S(1)}, f32[4,8,8,128]{3,2,1,0:T(8,128)S(1)}, u32[]{:S(2)}, u32[]{:S(2)}) %collective-permute-start.4) | collective-permute-done | bytes 131104 | tf_op jit(solution)/shard_map/ppermute | solution.py:595
  22.7 2.0 %stage_below.1 = (f32[4,8,128]{2,1,0:T(8,128)S(1)}, f32[4,8,128]{2,1,0:T(8,128)S(1)}, f32[4,8,128]{2,1,0:T(8,128)S(1)}, f32[4,8,128]{2,1,0:T(8,128)S(1)}) custom-call(f32[4,8,8,128]{3,2,1,0:T(8,128)S(1)} %collective-permute-done.4.fresh_ref, f32[8,8,128]{2,1,0:T(8,128)S(1)} %get-tuple-element.30.refs_0_, f32[19,8,8,128]{3,2,1,0:T(8,128)S(1)} %get-tuple-element.31.refs_1_, ...), custom_call_target="tpu_custom_call" | custom-call | flops 30000000 | bytes 10469376 | tf_op jit(solution)/shard_map/stage_below/pallas_call | solution.py:535
  24.7 0.6 %collective-permute-start.6 = (f32[4,8,128]{2,1,0:T(8,128)S(1)}, f32[4,8,128]{2,1,0:T(8,128)S(1)}, u32[]{:S(2)}, u32[]{:S(2)}) collective-permute-start(f32[4,8,128]{2,1,0:T(8,128)S(1)} %get-tuple-element.47), channel_id=1, source_target_pairs={{0,8},{8,0},{16,24},{24,16},{1,9},{9,1},{17,25},{25,17},{2,10},{10... | collective-permute-start | bytes 49160 | tf_op jit(solution)/shard_map/ppermute | solution.py:602
  25.3 0.5 %collective-permute-start.7 = (f32[4,8,128]{2,1,0:T(8,128)S(1)}, f32[4,8,128]{2,1,0:T(8,128)S(1)}, u32[]{:S(2)}, u32[]{:S(2)}) collective-permute-start(f32[4,8,128]{2,1,0:T(8,128)S(1)} %get-tuple-element.48), channel_id=1, source_target_pairs={{0,16},{8,24},{16,0},{24,8},{1,17},{9,25},{17,1},{25,9},{2,18},{10... | collective-permute-start | bytes 49160 | tf_op jit(solution)/shard_map/ppermute | solution.py:602
  25.8 2.4 %collective-permute-start.8 = (f32[4,8,128]{2,1,0:T(8,128)S(1)}, f32[4,8,128]{2,1,0:T(8,128)S(1)}, u32[]{:S(2)}, u32[]{:S(2)}) collective-permute-start(f32[4,8,128]{2,1,0:T(8,128)S(1)} %get-tuple-element.49), channel_id=1, source_target_pairs={{0,24},{8,16},{16,8},{24,0},{1,25},{9,17},{17,9},{25,1},{2,26},{10... | collective-permute-start | bytes 49160 | tf_op jit(solution)/shard_map/ppermute | solution.py:602
  28.3 0.2 collective-permute-done.6.refs_1_
  28.5 0.5 %collective-permute-done.7.refs_2_ = f32[4,8,128]{2,1,0:T(8,128)S(1)} collective-permute-done((f32[4,8,128]{2,1,0:T(8,128)S(1)}, f32[4,8,128]{2,1,0:T(8,128)S(1)}, u32[]{:S(2)}, u32[]{:S(2)}) %collective-permute-start.7) | collective-permute-done | bytes 16416 | tf_op jit(solution)/shard_map/ppermute | solution.py:602
  29.1 1.4 %collective-permute-done.8.refs_3_ = f32[4,8,128]{2,1,0:T(8,128)S(1)} collective-permute-done((f32[4,8,128]{2,1,0:T(8,128)S(1)}, f32[4,8,128]{2,1,0:T(8,128)S(1)}, u32[]{:S(2)}, u32[]{:S(2)}) %collective-permute-start.8) | collective-permute-done | bytes 16416 | tf_op jit(solution)/shard_map/ppermute | solution.py:602
  30.5 0.8 %place_outputs.1 = (f32[4,8,128]{2,1,0:T(8,128)}, f32[3,4,8,128]{3,2,1,0:T(8,128)}) custom-call(f32[4,8,128]{2,1,0:T(8,128)S(1)} %get-tuple-element.46.refs_0_, f32[4,8,128]{2,1,0:T(8,128)S(1)} %collective-permute-done.6.refs_1_, f32[4,8,128]{2,1,0:T(8,128)S(1)} %collective-permute-done.7.refs_2_, f32[4,8,128]{2,1,0:T(8,128)S(1)} %collective-permute-done.8.refs_3_), custom_call_target="tpu_custom_call" | custom-call | tf_op jit(solution)/shard_map/place_outputs/pallas_call | solution.py:567
  (4 shorter events, 0.0 us)
Async XLA Ops:
  0.6 0.8 %copy-start = (f32[3,4,8,128]{3,2,1,0:T(8,128)S(1)}, f32[3,4,8,128]{3,2,1,0:T(8,128)}, u32[]{:S(2)}) copy-start(f32[3,4,8,128]{3,2,1,0:T(8,128)} %param.5) | copy-start | bytes 147460
  1.4 1.5 %collective-permute-start = (f32[5,4,8,128]{3,2,1,0:T(8,128)S(1)}, f32[5,4,8,128]{3,2,1,0:T(8,128)S(1)}, u32[]{:S(2)}, u32[]{:S(2)}) collective-permute-start(f32[5,4,8,128]{3,2,1,0:T(8,128)S(1)} %pad_maximum_fusion.v_ref), channel_id=1, source_target_pairs={{0,1},{1,0},{2,3},{3,2},{4,5},{5,4},{6,7},{7,6},{8,9},{9,8},{10,11... | collective-permute-start | bytes 245768 | tf_op jit(solution)/shard_map/ppermute | solution.py:588
  3.1 4.8 %collective-permute-start.1 = (f32[8,8,128]{2,1,0:T(8,128)S(1)}, f32[8,8,128]{2,1,0:T(8,128)S(1)}, u32[]{:S(2)}, u32[]{:S(2)}) collective-permute-start(f32[8,8,128]{2,1,0:T(8,128)S(1)} %get-tuple-element.27), channel_id=1, source_target_pairs={{0,8},{8,0},{16,24},{24,16},{1,9},{9,1},{17,25},{25,17},{2,10},{10... | collective-permute-start | bytes 98312 | tf_op jit(solution)/shard_map/ppermute | solution.py:593
  6.0 3.9 %collective-permute-start.2 = (f32[8,8,128]{2,1,0:T(8,128)S(1)}, f32[8,8,128]{2,1,0:T(8,128)S(1)}, u32[]{:S(2)}, u32[]{:S(2)}) collective-permute-start(f32[8,8,128]{2,1,0:T(8,128)S(1)} %get-tuple-element.28), channel_id=1, source_target_pairs={{0,16},{8,24},{16,0},{24,8},{1,17},{9,25},{17,1},{25,9},{2,18},{10... | collective-permute-start | bytes 98312 | tf_op jit(solution)/shard_map/ppermute | solution.py:593
  7.5 4.8 %collective-permute-start.3 = (f32[8,8,128]{2,1,0:T(8,128)S(1)}, f32[8,8,128]{2,1,0:T(8,128)S(1)}, u32[]{:S(2)}, u32[]{:S(2)}) collective-permute-start(f32[8,8,128]{2,1,0:T(8,128)S(1)} %get-tuple-element.29), channel_id=1, source_target_pairs={{0,24},{8,16},{16,8},{24,0},{1,25},{9,17},{17,9},{25,1},{2,26},{10... | collective-permute-start | bytes 98312 | tf_op jit(solution)/shard_map/ppermute | solution.py:593
  12.3 6.4 %collective-permute-start.5 = (f32[4,8,8,128]{3,2,1,0:T(8,128)S(1)}, f32[4,8,8,128]{3,2,1,0:T(8,128)S(1)}, u32[]{:S(2)}, u32[]{:S(2)}) collective-permute-start(f32[4,8,8,128]{3,2,1,0:T(8,128)S(1)} %join_slots.1.fresh_ref), channel_id=1, source_target_pairs={{0,6},{2,0},{4,2},{6,4},{1,7},{3,1},{5,3},{7,5},{8,14},{10,8},{12,... | collective-permute-start | bytes 393224 | tf_op jit(solution)/shard_map/ppermute | solution.py:596
  16.0 6.8 %collective-permute-start.4 = (f32[4,8,8,128]{3,2,1,0:T(8,128)S(1)}, f32[4,8,8,128]{3,2,1,0:T(8,128)S(1)}, u32[]{:S(2)}, u32[]{:S(2)}) collective-permute-start(f32[4,8,8,128]{3,2,1,0:T(8,128)S(1)} %join_slots.1.fresh_ref), channel_id=1, source_target_pairs={{0,2},{2,4},{4,6},{6,0},{1,3},{3,5},{5,7},{7,1},{8,10},{10,12},{12... | collective-permute-start | bytes 393224 | tf_op jit(solution)/shard_map/ppermute | solution.py:595
  24.7 3.8 %collective-permute-start.6 = (f32[4,8,128]{2,1,0:T(8,128)S(1)}, f32[4,8,128]{2,1,0:T(8,128)S(1)}, u32[]{:S(2)}, u32[]{:S(2)}) collective-permute-start(f32[4,8,128]{2,1,0:T(8,128)S(1)} %get-tuple-element.47), channel_id=1, source_target_pairs={{0,8},{8,0},{16,24},{24,16},{1,9},{9,1},{17,25},{25,17},{2,10},{10... | collective-permute-start | bytes 49160 | tf_op jit(solution)/shard_map/ppermute | solution.py:602
  25.3 3.7 %collective-permute-start.7 = (f32[4,8,128]{2,1,0:T(8,128)S(1)}, f32[4,8,128]{2,1,0:T(8,128)S(1)}, u32[]{:S(2)}, u32[]{:S(2)}) collective-permute-start(f32[4,8,128]{2,1,0:T(8,128)S(1)} %get-tuple-element.48), channel_id=1, source_target_pairs={{0,16},{8,24},{16,0},{24,8},{1,17},{9,25},{17,1},{25,9},{2,18},{10... | collective-permute-start | bytes 49160 | tf_op jit(solution)/shard_map/ppermute | solution.py:602
  25.8 4.6 %collective-permute-start.8 = (f32[4,8,128]{2,1,0:T(8,128)S(1)}, f32[4,8,128]{2,1,0:T(8,128)S(1)}, u32[]{:S(2)}, u32[]{:S(2)}) collective-permute-start(f32[4,8,128]{2,1,0:T(8,128)S(1)} %get-tuple-element.49), channel_id=1, source_target_pairs={{0,24},{8,16},{16,8},{24,0},{1,25},{9,17},{17,9},{25,1},{2,26},{10... | collective-permute-start | bytes 49160 | tf_op jit(solution)/shard_map/ppermute | solution.py:602

commit v9 on v7

--- a/solution.py
+++ b/solution.py
@@ -85,6 +85,13 @@
     return value if c == 1.0 else -value if c == -1.0 else c * value
 
 
+def pair_sums(f):
+    s = [f[i] + f[i + 1] for i in range(1, 19, 2)]
+    xy, xz, yz = s[3] + s[4], s[5] + s[6], s[7] + s[8]
+    axes, diagonals = s[0] + s[1] + s[2], xy + xz + yz
+    return s + [xy, xz, yz, axes, diagonals, f[0] + axes + diagonals]
+
+
 def moments(f):
     d = [None] + [f[i] - f[i + 1] for i in range(1, 19, 2)]
     jx = d[1] + ((d[4] + d[5]) + (d[6] + d[7]))
@@ -93,13 +100,10 @@
     return jx, jy, jz
 
 
-def collide(f, force, solid):
-    s = [None] + [f[i] + f[i + 1] for i in range(1, 19, 2)]
+def collide(f, sums, force, solid):
+    s = [None] + sums[:9]
     d = [None] + [f[i] - f[i + 1] for i in range(1, 19, 2)]
-    xy, xz, yz = s[4] + s[5], s[6] + s[7], s[8] + s[9]
-    axes = s[1] + s[2] + s[3]
-    diagonals = xy + xz + yz
-    rho = f[0] + axes + diagonals
+    xy, xz, yz, axes, diagonals, rho = sums[9:]
     p_xy, q_xy = d[4] + d[5], d[4] - d[5]
     p_xz, q_xz = d[6] + d[7], d[6] - d[7]
     p_yz, q_yz = d[8] + d[9], d[8] - d[9]
@@ -377,9 +381,10 @@
         scale = here * (1.0 / 36.0)
         return [scale * value for value in (fx, fy, fz)]
 
-    def run(self, stage, held, raw, force_ref, fresh, k, finish):
+    def run(self, stage, held, raw, force_ref, sums_ref, fresh, k, finish):
         sh = self.sh
         table = {other: self.buffers(other) for other in STAGES}
+        keep = stage == STAGES[-1]
 
         def at(owner, name, y):
             return held[owner, name], y - table[owner][name][1]
@@ -419,8 +424,11 @@
                 held[stage, ("f", 0)][i, n] = row
 
         def weigh(s, y):
-            rows = [f(s, i, y) for i in range(19)]
-            psi = potential(sum(rows[1:], rows[0]))
+            sums = pair_sums([f(s, i, y) for i in range(19)])
+            psi = potential(sums[-1])
+            if keep:
+                for n, value in enumerate(sums):
+                    sums_ref[s, n, y - self.weighed(stage, s)[0]] = value
             to = held[stage, ("psi", s)]
             to[y - self.weighed(stage, s)[0]] = jnp.where(solid(y), WALL_POTENTIAL, psi)
 
@@ -430,7 +438,13 @@
 
         def advance(s, y):
             force = [force_ref[s, axis, y] for axis in range(3)]
-            post = collide([f(s, i, y) for i in range(19)], force, solid(y))
+            row = [f(s, i, y) for i in range(19)]
+            first, last = self.weighed(stage, s)
+            if keep and first <= y <= last:
+                sums = [sums_ref[s, n, y - first] for n in range(15)]
+            else:
+                sums = pair_sums(row)
+            post = collide(row, sums, force, solid(y))
             base = self.collided(stage, s)[0] - 1
             for i in range(19):
                 cx, cy, cz = (int(c) for c in C[i])
@@ -489,7 +503,7 @@
         if last_stage:
             outs, refs = refs[: sh.nx], refs[sh.nx :]
         held.update(zip(own, refs))
-        raw, force_ref, done = refs[len(own) :]
+        raw, force_ref, sums_ref, done = refs[len(own) :]
         k = lax.axis_index("gx")
         low = Rows(sh)
 
@@ -502,7 +516,7 @@
                 at = pl.ds(y - low.own, sh.subs, stride=sh.y)
                 done[v, at, :] = jnp.where(wall, 0.0, value)
 
-        low.run(stage, held, raw, force_ref, fresh_ref, k, finish)
+        low.run(stage, held, raw, force_ref, sums_ref, fresh_ref, k, finish)
         if not last_stage:
             return
         lane = lax.broadcasted_iota(jnp.int32, (sh.y, LANES), 1)
@@ -523,6 +537,7 @@
     extra = [
         pltpu.VMEM((5, sh.subs * sh.y, LANES), jnp.float32),
         pltpu.VMEM((STEPS, 3, sh.rows, sh.subs, LANES), jnp.float32),
+        pltpu.VMEM((STEPS, 15, sh.y, sh.subs, LANES), jnp.float32),
         pltpu.VMEM((4, sh.subs * sh.y, LANES), jnp.float32),
     ]
     outs = [jax.ShapeDtypeStruct(shape, jnp.float32) for shape in shapes]

time: 31.4 us -> 31.5 us (level)
  no operation moved by 1% of the time
where the time goes in v9:
time: 31.5 us; the launch traced here: 31.3 us
  starting transfers between devices  12.2 us (39%)
  waiting for transfers between devices  12 us (38%)
  Pallas kernels  5.65 us (18%)
  other arithmetic  0.78 us (2%)
  between operations  0.68 us (2%)
    ppermute x3, waiting for transfers between devices, on_device(): got.append(lax.ppermute(slabs[slot], 'gx', sh.perm(slot)))  4.79 us
    pallas_call x3, Pallas kernels, run_stage(): pl.pallas_call(body, name='stage_' + stage, out_shape=outs, in_specs=vmem...  4.7 us
    ppermute x3, starting transfers between devices, on_device(): got.append(lax.ppermute(slabs[slot], 'gx', sh.perm(slot)))  4.43 us
    ppermute x1, starting transfers between devices, on_device(): above = lax.ppermute(middle, 'gy', ring(sh.ny, -1))  3.65 us
    ppermute x3, starting transfers between devices, on_device(): back.append(lax.ppermute(pieces[slot], 'gx', sh.perm(slot)))  3.55 us
    ppermute x1, waiting for transfers between devices, on_device(): below = lax.ppermute(middle, 'gy', ring(sh.ny, 1))  2.2 us
    ppermute x3, waiting for transfers between devices, on_device(): back.append(lax.ppermute(pieces[slot], 'gx', sh.perm(slot)))  2.19 us
    ppermute x1, waiting for transfers between devices, on_device(): above = lax.ppermute(middle, 'gy', ring(sh.ny, -1))  1.91 us
  transfers between devices with their start and end apart: 9, of which 9 were waited for; matrix products, arithmetic and copies ran while one was open for 0% of the time, Pallas kernels for 8%

profile of v9, /device:TPU:0, one launch (start us, length us, event | category | flops | bytes accessed | tf_op | source)
XLA Modules:
  0.0 31.3 jit_solution(9489755509922991117)
XLA Ops:
  0.6 0.8 %select_bitcast_fusion = (f32[1,4,8,128]{3,2,1,0:T(8,128)S(1)}, f32[1,4,8,128]{3,2,1,0:T(8,128)S(1)}) fusion(s32[4,8,128]{2,1,0:T(8,128)} %param.7, f32[4,8,128]{2,1,0:T(8,128)} %param.4, s32[4,8,128]{2,1,0:T(8,128)} %param.6), kind=kLoop, calls=%fused_computation.1 | loop fusion | flops 20480 | bytes 81920 | tf_op jit(solution)/shard_map/broadcast_in_dim | solution.py:255
  1.4 0.0 copy-done
  1.4 0.5 %collective-permute-start = (f32[5,4,8,128]{3,2,1,0:T(8,128)S(1)}, f32[5,4,8,128]{3,2,1,0:T(8,128)S(1)}, u32[]{:S(2)}, u32[]{:S(2)}) collective-permute-start(f32[5,4,8,128]{3,2,1,0:T(8,128)S(1)} %pad_maximum_fusion.v_ref), channel_id=1, source_target_pairs={{0,1},{1,0},{2,3},{3,2},{4,5},{5,4},{6,7},{7,6},{8,9},{9,8},{10,11... | collective-permute-start | bytes 245768 | tf_op jit(solution)/shard_map/ppermute | solution.py:601
  2.0 0.9 %collective-permute-done.b_ref.a_ref = f32[5,4,8,128]{3,2,1,0:T(8,128)S(1)} collective-permute-done((f32[5,4,8,128]{3,2,1,0:T(8,128)S(1)}, f32[5,4,8,128]{3,2,1,0:T(8,128)S(1)}, u32[]{:S(2)}, u32[]{:S(2)}) %collective-permute-start) | collective-permute-done | bytes 81952 | tf_op jit(solution)/shard_map/ppermute | solution.py:601
  2.9 0.2 cut_slabs.1
  3.1 2.9 %collective-permute-start.1 = (f32[8,8,128]{2,1,0:T(8,128)S(1)}, f32[8,8,128]{2,1,0:T(8,128)S(1)}, u32[]{:S(2)}, u32[]{:S(2)}) collective-permute-start(f32[8,8,128]{2,1,0:T(8,128)S(1)} %get-tuple-element.27), channel_id=1, source_target_pairs={{0,8},{8,0},{16,24},{24,16},{1,9},{9,1},{17,25},{25,17},{2,10},{10... | collective-permute-start | bytes 98312 | tf_op jit(solution)/shard_map/ppermute | solution.py:606
  6.0 1.5 %collective-permute-start.2 = (f32[8,8,128]{2,1,0:T(8,128)S(1)}, f32[8,8,128]{2,1,0:T(8,128)S(1)}, u32[]{:S(2)}, u32[]{:S(2)}) collective-permute-start(f32[8,8,128]{2,1,0:T(8,128)S(1)} %get-tuple-element.28), channel_id=1, source_target_pairs={{0,16},{8,24},{16,0},{24,8},{1,17},{9,25},{17,1},{25,9},{2,18},{10... | collective-permute-start | bytes 98312 | tf_op jit(solution)/shard_map/ppermute | solution.py:606
  7.5 0.0 collective-permute-start.3
  7.5 0.4 %collective-permute-done.1.refs_1_ = f32[8,8,128]{2,1,0:T(8,128)S(1)} collective-permute-done((f32[8,8,128]{2,1,0:T(8,128)S(1)}, f32[8,8,128]{2,1,0:T(8,128)S(1)}, u32[]{:S(2)}, u32[]{:S(2)}) %collective-permute-start.1) | collective-permute-done | bytes 32800 | tf_op jit(solution)/shard_map/ppermute | solution.py:606
  7.9 2.0 %collective-permute-done.2.refs_2_ = f32[8,8,128]{2,1,0:T(8,128)S(1)} collective-permute-done((f32[8,8,128]{2,1,0:T(8,128)S(1)}, f32[8,8,128]{2,1,0:T(8,128)S(1)}, u32[]{:S(2)}, u32[]{:S(2)}) %collective-permute-start.2) | collective-permute-done | bytes 32800 | tf_op jit(solution)/shard_map/ppermute | solution.py:606
  9.9 2.4 %collective-permute-done.3.refs_3_ = f32[8,8,128]{2,1,0:T(8,128)S(1)} collective-permute-done((f32[8,8,128]{2,1,0:T(8,128)S(1)}, f32[8,8,128]{2,1,0:T(8,128)S(1)}, u32[]{:S(2)}, u32[]{:S(2)}) %collective-permute-start.3) | collective-permute-done | bytes 32800 | tf_op jit(solution)/shard_map/ppermute | solution.py:606
  12.3 3.7 %collective-permute-start.5 = (f32[4,8,8,128]{3,2,1,0:T(8,128)S(1)}, f32[4,8,8,128]{3,2,1,0:T(8,128)S(1)}, u32[]{:S(2)}, u32[]{:S(2)}) collective-permute-start(f32[4,8,8,128]{3,2,1,0:T(8,128)S(1)} %join_slots.1.fresh_ref), channel_id=1, source_target_pairs={{0,6},{2,0},{4,2},{6,4},{1,7},{3,1},{5,3},{7,5},{8,14},{10,8},{12,... | collective-permute-start | bytes 393224 | tf_op jit(solution)/shard_map/ppermute | solution.py:609
  16.0 0.9 %stage_own.1 = (f32[8,8,128]{2,1,0:T(8,128)S(1)}, f32[19,8,8,128]{3,2,1,0:T(8,128)S(1)}, f32[8,8,128]{2,1,0:T(8,128)S(1)}, f32[19,8,8,128]{3,2,1,0:T(8,128)S(1)}...) custom-call(f32[4,8,8,128]{3,2,1,0:T(8,128)S(1)} %join_slots.1.fresh_ref), custom_call_target="tpu_custom_call" | custom-call | flops 5000000 | bytes 5210112 | tf_op jit(solution)/shard_map/stage_own/pallas_call | solution.py:548
  16.8 1.9 %collective-permute-done.5.fresh_ref = f32[4,8,8,128]{3,2,1,0:T(8,128)S(1)} collective-permute-done((f32[4,8,8,128]{3,2,1,0:T(8,128)S(1)}, f32[4,8,8,128]{3,2,1,0:T(8,128)S(1)}, u32[]{:S(2)}, u32[]{:S(2)}) %collective-permute-start.5) | collective-permute-done | bytes 131104 | tf_op jit(solution)/shard_map/ppermute | solution.py:609
  18.7 1.8 %stage_above.1 = (f32[8,8,128]{2,1,0:T(8,128)S(1)}, f32[19,8,8,128]{3,2,1,0:T(8,128)S(1)}, f32[8,8,128]{2,1,0:T(8,128)S(1)}, f32[19,10,8,128]{3,2,1,0:T(8,128)S(...) custom-call(f32[4,8,8,128]{3,2,1,0:T(8,128)S(1)} %collective-permute, ...), custom_call_target="tpu_custom_call" | custom-call | flops 20000000 | bytes 8470528 | tf_op jit(solution)/shard_map/stage_above/pallas_call | solution.py:548
  20.5 2.2 %collective-permute-done.4.fresh_ref = f32[4,8,8,128]{3,2,1,0:T(8,128)S(1)} collective-permute-done((f32[4,8,8,128]{3,2,1,0:T(8,128)S(1)}, f32[4,8,8,128]{3,2,1,0:T(8,128)S(1)}, u32[]{:S(2)}, u32[]{:S(2)}) %collective-permute-start.4) | collective-permute-done | bytes 131104 | tf_op jit(solution)/shard_map/ppermute | solution.py:608
  22.7 2.1 %stage_below.1 = (f32[4,8,128]{2,1,0:T(8,128)S(1)}, f32[4,8,128]{2,1,0:T(8,128)S(1)}, f32[4,8,128]{2,1,0:T(8,128)S(1)}, f32[4,8,128]{2,1,0:T(8,128)S(1)}) custom-call(f32[4,8,8,128]{3,2,1,0:T(8,128)S(1)} %collective-permute-done.4.fresh_ref, f32[8,8,128]{2,1,0:T(8,128)S(1)} %get-tuple-element.30.refs_0_, f32[19,8,8,128]{3,2,1,0:T(8,128)S(1)} %get-tuple-element.31.refs_1_, ...), custom_call_target="tpu_custom_call" | custom-call | flops 30000000 | bytes 12435456 | tf_op jit(solution)/shard_map/stage_below/pallas_call | solution.py:548
  24.8 0.6 %collective-permute-start.6 = (f32[4,8,128]{2,1,0:T(8,128)S(1)}, f32[4,8,128]{2,1,0:T(8,128)S(1)}, u32[]{:S(2)}, u32[]{:S(2)}) collective-permute-start(f32[4,8,128]{2,1,0:T(8,128)S(1)} %get-tuple-element.47), channel_id=1, source_target_pairs={{0,8},{8,0},{16,24},{24,16},{1,9},{9,1},{17,25},{25,17},{2,10},{10... | collective-permute-start | bytes 49160 | tf_op jit(solution)/shard_map/ppermute | solution.py:615
  25.4 0.5 %collective-permute-start.7 = (f32[4,8,128]{2,1,0:T(8,128)S(1)}, f32[4,8,128]{2,1,0:T(8,128)S(1)}, u32[]{:S(2)}, u32[]{:S(2)}) collective-permute-start(f32[4,8,128]{2,1,0:T(8,128)S(1)} %get-tuple-element.48), channel_id=1, source_target_pairs={{0,16},{8,24},{16,0},{24,8},{1,17},{9,25},{17,1},{25,9},{2,18},{10... | collective-permute-start | bytes 49160 | tf_op jit(solution)/shard_map/ppermute | solution.py:615
  25.9 2.4 %collective-permute-start.8 = (f32[4,8,128]{2,1,0:T(8,128)S(1)}, f32[4,8,128]{2,1,0:T(8,128)S(1)}, u32[]{:S(2)}, u32[]{:S(2)}) collective-permute-start(f32[4,8,128]{2,1,0:T(8,128)S(1)} %get-tuple-element.49), channel_id=1, source_target_pairs={{0,24},{8,16},{16,8},{24,0},{1,25},{9,17},{17,9},{25,1},{2,26},{10... | collective-permute-start | bytes 49160 | tf_op jit(solution)/shard_map/ppermute | solution.py:615
  28.4 0.2 collective-permute-done.6.refs_1_
  28.6 0.5 %collective-permute-done.7.refs_2_ = f32[4,8,128]{2,1,0:T(8,128)S(1)} collective-permute-done((f32[4,8,128]{2,1,0:T(8,128)S(1)}, f32[4,8,128]{2,1,0:T(8,128)S(1)}, u32[]{:S(2)}, u32[]{:S(2)}) %collective-permute-start.7) | collective-permute-done | bytes 16416 | tf_op jit(solution)/shard_map/ppermute | solution.py:615
  29.1 1.4 %collective-permute-done.8.refs_3_ = f32[4,8,128]{2,1,0:T(8,128)S(1)} collective-permute-done((f32[4,8,128]{2,1,0:T(8,128)S(1)}, f32[4,8,128]{2,1,0:T(8,128)S(1)}, u32[]{:S(2)}, u32[]{:S(2)}) %collective-permute-start.8) | collective-permute-done | bytes 16416 | tf_op jit(solution)/shard_map/ppermute | solution.py:615
  30.6 0.8 %place_outputs.1 = (f32[4,8,128]{2,1,0:T(8,128)}, f32[3,4,8,128]{3,2,1,0:T(8,128)}) custom-call(f32[4,8,128]{2,1,0:T(8,128)S(1)} %get-tuple-element.46.refs_0_, f32[4,8,128]{2,1,0:T(8,128)S(1)} %collective-permute-done.6.refs_1_, f32[4,8,128]{2,1,0:T(8,128)S(1)} %collective-permute-done.7.refs_2_, f32[4,8,128]{2,1,0:T(8,128)S(1)} %collective-permute-done.8.refs_3_), custom_call_target="tpu_custom_call" | custom-call | tf_op jit(solution)/shard_map/place_outputs/pallas_call | solution.py:580
  (4 shorter events, 0.0 us)
Async XLA Ops:
  0.6 0.8 %copy-start = (f32[3,4,8,128]{3,2,1,0:T(8,128)S(1)}, f32[3,4,8,128]{3,2,1,0:T(8,128)}, u32[]{:S(2)}) copy-start(f32[3,4,8,128]{3,2,1,0:T(8,128)} %param.5) | copy-start | bytes 147460
  1.4 1.5 %collective-permute-start = (f32[5,4,8,128]{3,2,1,0:T(8,128)S(1)}, f32[5,4,8,128]{3,2,1,0:T(8,128)S(1)}, u32[]{:S(2)}, u32[]{:S(2)}) collective-permute-start(f32[5,4,8,128]{3,2,1,0:T(8,128)S(1)} %pad_maximum_fusion.v_ref), channel_id=1, source_target_pairs={{0,1},{1,0},{2,3},{3,2},{4,5},{5,4},{6,7},{7,6},{8,9},{9,8},{10,11... | collective-permute-start | bytes 245768 | tf_op jit(solution)/shard_map/ppermute | solution.py:601
  3.1 4.8 %collective-permute-start.1 = (f32[8,8,128]{2,1,0:T(8,128)S(1)}, f32[8,8,128]{2,1,0:T(8,128)S(1)}, u32[]{:S(2)}, u32[]{:S(2)}) collective-permute-start(f32[8,8,128]{2,1,0:T(8,128)S(1)} %get-tuple-element.27), channel_id=1, source_target_pairs={{0,8},{8,0},{16,24},{24,16},{1,9},{9,1},{17,25},{25,17},{2,10},{10... | collective-permute-start | bytes 98312 | tf_op jit(solution)/shard_map/ppermute | solution.py:606
  6.0 3.9 %collective-permute-start.2 = (f32[8,8,128]{2,1,0:T(8,128)S(1)}, f32[8,8,128]{2,1,0:T(8,128)S(1)}, u32[]{:S(2)}, u32[]{:S(2)}) collective-permute-start(f32[8,8,128]{2,1,0:T(8,128)S(1)} %get-tuple-element.28), channel_id=1, source_target_pairs={{0,16},{8,24},{16,0},{24,8},{1,17},{9,25},{17,1},{25,9},{2,18},{10... | collective-permute-start | bytes 98312 | tf_op jit(solution)/shard_map/ppermute | solution.py:606
  7.5 4.8 %collective-permute-start.3 = (f32[8,8,128]{2,1,0:T(8,128)S(1)}, f32[8,8,128]{2,1,0:T(8,128)S(1)}, u32[]{:S(2)}, u32[]{:S(2)}) collective-permute-start(f32[8,8,128]{2,1,0:T(8,128)S(1)} %get-tuple-element.29), channel_id=1, source_target_pairs={{0,24},{8,16},{16,8},{24,0},{1,25},{9,17},{17,9},{25,1},{2,26},{10... | collective-permute-start | bytes 98312 | tf_op jit(solution)/shard_map/ppermute | solution.py:606
  12.3 6.4 %collective-permute-start.5 = (f32[4,8,8,128]{3,2,1,0:T(8,128)S(1)}, f32[4,8,8,128]{3,2,1,0:T(8,128)S(1)}, u32[]{:S(2)}, u32[]{:S(2)}) collective-permute-start(f32[4,8,8,128]{3,2,1,0:T(8,128)S(1)} %join_slots.1.fresh_ref), channel_id=1, source_target_pairs={{0,6},{2,0},{4,2},{6,4},{1,7},{3,1},{5,3},{7,5},{8,14},{10,8},{12,... | collective-permute-start | bytes 393224 | tf_op jit(solution)/shard_map/ppermute | solution.py:609
  16.0 6.8 %collective-permute-start.4 = (f32[4,8,8,128]{3,2,1,0:T(8,128)S(1)}, f32[4,8,8,128]{3,2,1,0:T(8,128)S(1)}, u32[]{:S(2)}, u32[]{:S(2)}) collective-permute-start(f32[4,8,8,128]{3,2,1,0:T(8,128)S(1)} %join_slots.1.fresh_ref), channel_id=1, source_target_pairs={{0,2},{2,4},{4,6},{6,0},{1,3},{3,5},{5,7},{7,1},{8,10},{10,12},{12... | collective-permute-start | bytes 393224 | tf_op jit(solution)/shard_map/ppermute | solution.py:608
  24.8 3.8 %collective-permute-start.6 = (f32[4,8,128]{2,1,0:T(8,128)S(1)}, f32[4,8,128]{2,1,0:T(8,128)S(1)}, u32[]{:S(2)}, u32[]{:S(2)}) collective-permute-start(f32[4,8,128]{2,1,0:T(8,128)S(1)} %get-tuple-element.47), channel_id=1, source_target_pairs={{0,8},{8,0},{16,24},{24,16},{1,9},{9,1},{17,25},{25,17},{2,10},{10... | collective-permute-start | bytes 49160 | tf_op jit(solution)/shard_map/ppermute | solution.py:615
  25.4 3.7 %collective-permute-start.7 = (f32[4,8,128]{2,1,0:T(8,128)S(1)}, f32[4,8,128]{2,1,0:T(8,128)S(1)}, u32[]{:S(2)}, u32[]{:S(2)}) collective-permute-start(f32[4,8,128]{2,1,0:T(8,128)S(1)} %get-tuple-element.48), channel_id=1, source_target_pairs={{0,16},{8,24},{16,0},{24,8},{1,17},{9,25},{17,1},{25,9},{2,18},{10... | collective-permute-start | bytes 49160 | tf_op jit(solution)/shard_map/ppermute | solution.py:615
  25.9 4.6 %collective-permute-start.8 = (f32[4,8,128]{2,1,0:T(8,128)S(1)}, f32[4,8,128]{2,1,0:T(8,128)S(1)}, u32[]{:S(2)}, u32[]{:S(2)}) collective-permute-start(f32[4,8,128]{2,1,0:T(8,128)S(1)} %get-tuple-element.49), channel_id=1, source_target_pairs={{0,24},{8,16},{16,8},{24,0},{1,25},{9,17},{17,9},{25,1},{2,26},{10... | collective-permute-start | bytes 49160 | tf_op jit(solution)/shard_map/ppermute | solution.py:615
